TPU v7x, 256 devices: a whole 4x4x8 slice. The times are simulated.
256 devices in a mesh: kv: 8 (over y, core), blk: 32 (over x, z).
Axes of the slice: x: 4, y: 4, z: 8, core: 2. Of those that a mesh axis runs over, the one named last changes fastest.
Arguments:
- hidden_in: bfloat16 [4096, 5120], P('blk', 'kv'), may hold values from -6 to 6
- norm_gain: bfloat16 [5120], replicated, may hold values from 0.099609375 to 1.8984375
- w_query: bfloat16 [5120, 5120], P(None, 'kv'), may hold values from -0.078125 to 0.078125
- key_weight: bfloat16 [5120, 1024], P(None, 'kv'), may hold values from -0.078125 to 0.078125
- value_weight: bfloat16 [5120, 1024], P(None, 'kv'), may hold values from -0.3125 to 0.3125
- b_query: bfloat16 [5120], P('kv'), may hold values from -3 to 3
- key_bias: bfloat16 [1024], P('kv'), may hold values from -3 to 3
- value_bias: bfloat16 [1024], P('kv'), may hold values from -4 to 4
- key_cache: bfloat16 [384, 128, 1024], P('blk', None, 'kv'), as said below
- value_cache: bfloat16 [384, 128, 1024], P('blk', None, 'kv'), may hold values from -24 to 24
- cached_len: int32 [4], replicated, may hold values from 1 to 8192, as said below
- block_table: int32 [4, 72], replicated, may hold values from -1 to 383, as said below
Outputs:
- attn_out: bfloat16 [4096, 5120], P('blk', 'kv')
- cache_k_out: bfloat16 [384, 128, 1024], P('blk', None, 'kv')
- cache_v_out: bfloat16 [384, 128, 1024], P('blk', None, 'kv')
Inputs may be any that keep to these rules, and one draw needn't show every extreme that they name: `cached_len`: the lengths sum to 24576; the largest is exactly 8192. `block_table`: row r names, in its first ceil((cached_len[r] + 1024) / 128) entries, the blocks holding positions j * 128 to (j + 1) * 128 - 1 of request r in order; its other entries are -1. No block is named twice. `key_cache`: keys as the layer wrote them, already rotated.
All inputs are finite; a program needn't handle non-finite values.
Results may differ from a plain program's by a relative error of at most 0.02.
The roundings to bfloat16 on the way count: a program that leaves them out, or rounds other values in their place, can miss the bound.
Values may be sent and summed in bfloat16 or wider, within the bound.
A program may use at most 128 MiB of HBM per device.

v0:
```python
import math

import jax
import jax.numpy as jnp
from jax import lax
from jax.sharding import PartitionSpec as P

HEAD_SIZE = 128


EPS = 1e-06
THETA = 1000000.0
NEG_FILL = -1e30


def apply_rotary(values, token_positions, head_dim):
    half = head_dim // 2
    rates = THETA ** (-(jnp.arange(half, dtype=jnp.float32) * 2.0) / head_dim)
    angle = token_positions.astype(jnp.float32)[:, None] * rates[None, :]
    cosine = jnp.cos(angle)[:, None, :]
    sine = jnp.sin(angle)[:, None, :]
    first = values[..., :half]
    second_half = values[..., half:]
    return jnp.concatenate(
        [first * cosine - second_half * sine, second_half * cosine + first * sine], axis=-1
    )


def lookup(table_values, slot_index):
    matches = slot_index[:, None] == jnp.arange(table_values.shape[0], dtype=jnp.int32)[None, :]
    return jnp.sum(jnp.where(matches, table_values[None, :], 0), axis=1)


def append_rows(cache, rows, slot_ids, first_block):
    nb_dev, block_size, kv_width = cache.shape
    flattened = cache.reshape(nb_dev * block_size, kv_width)
    local_slot = slot_ids - first_block * block_size
    inside = (local_slot >= 0) & (local_slot < nb_dev * block_size)
    target = jnp.where(inside, local_slot, nb_dev * block_size)
    return flattened.at[target].set(rows, mode="drop").reshape(cache.shape)


def block_owner(block_table, block_id):
    matched = block_table == block_id
    row_ids = jnp.arange(block_table.shape[0], dtype=jnp.int32)[:, None]
    col_ids = jnp.arange(block_table.shape[1], dtype=jnp.int32)[None, :]
    used = jnp.any(matched)
    owner = jnp.sum(jnp.where(matched, row_ids, 0))
    column = jnp.sum(jnp.where(matched, col_ids, 0))
    return (used, owner, column)


def attend_block(state, queries, query_pos, keys, values, key_pos, used, head_dim):
    top, total, weighted = state
    score = jnp.einsum(
        "rgfd,kgd->rgfk", queries, keys, preferred_element_type=jnp.float32
    ) / math.sqrt(head_dim)
    allowed = ((key_pos[None, :] <= query_pos[:, None]) & used)[:, None, None, :]
    block_top = jnp.max(jnp.where(allowed, score, NEG_FILL), axis=3)
    new_top = jnp.maximum(top, block_top)
    weights = jnp.where(allowed, jnp.exp(score - new_top[..., None]), 0.0)
    factor = jnp.exp(top - new_top)
    new_total = total * factor + jnp.sum(weights, axis=3)
    mixed = jnp.einsum(
        "rgfk,kgd->rgfd", weights.astype(jnp.bfloat16), values, preferred_element_type=jnp.float32
    )
    return (new_top, new_total, weighted * factor[..., None] + mixed)


def on_device(
    hidden_in,
    norm_gain,
    w_query,
    key_weight,
    value_weight,
    b_query,
    key_bias,
    value_bias,
    key_cache,
    value_cache,
    cached_len,
    block_table,
):
    tok_dev = hidden_in.shape[0]
    n_blk = lax.axis_size("blk")
    device = lax.axis_index("blk")
    requests = cached_len.shape[0]
    tokens = tok_dev * n_blk
    span = tokens // requests
    nb_dev, block_size, kv_width = key_cache.shape
    head_dim = HEAD_SIZE
    kv_heads = kv_width // head_dim
    q_heads = w_query.shape[1] // head_dim
    group_size = q_heads // kv_heads
    gain = norm_gain.astype(jnp.float32)
    whole = lax.all_gather(hidden_in, "kv", axis=1, tiled=True)
    wide_in = whole.astype(jnp.float32)
    scale = lax.rsqrt(jnp.mean(wide_in * wide_in, axis=1, keepdims=True) + EPS)
    normed = (wide_in * scale * gain[None, :]).astype(jnp.bfloat16)
    q_lin = jnp.dot(normed, w_query, preferred_element_type=jnp.float32)
    key_linear = jnp.dot(normed, key_weight, preferred_element_type=jnp.float32)
    value_linear = jnp.dot(normed, value_weight, preferred_element_type=jnp.float32)
    my_tokens = device * tok_dev + jnp.arange(tok_dev, dtype=jnp.int32)
    my_pos = lookup(cached_len, my_tokens // span) + my_tokens % span
    fresh_queries = apply_rotary(
        (q_lin + b_query.astype(jnp.float32)[None, :]).reshape(tok_dev, q_heads, head_dim),
        my_pos,
        head_dim,
    )
    fresh_queries = fresh_queries.astype(jnp.bfloat16).reshape(tok_dev, q_heads * head_dim)
    fresh_keys = apply_rotary(
        (key_linear + key_bias.astype(jnp.float32)[None, :]).reshape(tok_dev, kv_heads, head_dim),
        my_pos,
        head_dim,
    )
    fresh_keys = fresh_keys.astype(jnp.bfloat16).reshape(tok_dev, kv_width)
    fresh_values = (value_linear + value_bias.astype(jnp.float32)[None, :]).astype(jnp.bfloat16)
    all_tokens = jnp.arange(tokens, dtype=jnp.int32)
    all_req = all_tokens // span
    all_pos = lookup(cached_len, all_req) + all_tokens % span
    slot_ids = block_table[all_req, all_pos // block_size] * block_size + all_pos % block_size
    first_block = device * nb_dev
    offsets = jnp.arange(block_size, dtype=jnp.int32)
    q_all, k_all, v_all = (
        lax.all_gather(fresh_queries, "blk", axis=0, tiled=True),
        lax.all_gather(fresh_keys, "blk", axis=0, tiled=True),
        lax.all_gather(fresh_values, "blk", axis=0, tiled=True),
    )
    new_k = append_rows(key_cache, k_all, slot_ids, first_block)
    new_v = append_rows(value_cache, v_all, slot_ids, first_block)
    grouped_queries = q_all.reshape(tokens, kv_heads, group_size, head_dim)

    def visit(slot_index, state):
        used, owner, column = block_owner(block_table, first_block + slot_index)
        start = owner * span
        queries = lax.dynamic_slice_in_dim(grouped_queries, start, span, 0)
        query_pos = lax.dynamic_slice_in_dim(all_pos, start, span, 0)
        keys = lax.dynamic_index_in_dim(new_k, slot_index, 0, keepdims=False).reshape(
            block_size, kv_heads, head_dim
        )
        values = lax.dynamic_index_in_dim(new_v, slot_index, 0, keepdims=False).reshape(
            block_size, kv_heads, head_dim
        )
        key_pos = column * block_size + offsets
        partial_value = (
            lax.dynamic_slice_in_dim(state[0], start, span, 0),
            lax.dynamic_slice_in_dim(state[1], start, span, 0),
            lax.dynamic_slice_in_dim(state[2], start, span, 0),
        )
        partial_value = attend_block(
            partial_value, queries, query_pos, keys, values, key_pos, used, head_dim
        )
        return (
            lax.dynamic_update_slice_in_dim(state[0], partial_value[0], start, 0),
            lax.dynamic_update_slice_in_dim(state[1], partial_value[1], start, 0),
            lax.dynamic_update_slice_in_dim(state[2], partial_value[2], start, 0),
        )

    initial = (
        jnp.full((tokens, kv_heads, group_size), NEG_FILL, jnp.float32),
        jnp.zeros((tokens, kv_heads, group_size), jnp.float32),
        jnp.zeros((tokens, kv_heads, group_size, head_dim), jnp.float32),
    )
    top, total, weighted = lax.fori_loop(0, nb_dev, visit, initial)
    best = lax.pmax(top.astype(jnp.bfloat16), "blk").astype(top.dtype)
    factor = jnp.exp(top - best)
    mine_weighted, mine_total = (
        lax.psum_scatter(
            (weighted * factor[..., None]).astype(jnp.bfloat16),
            "blk",
            scatter_dimension=0,
            tiled=True,
        ).astype(jnp.float32),
        lax.psum_scatter(
            (total * factor).astype(jnp.bfloat16), "blk", scatter_dimension=0, tiled=True
        ).astype(jnp.float32),
    )
    attn_out = (
        (mine_weighted / mine_total[..., None])
        .astype(jnp.bfloat16)
        .reshape(tok_dev, q_heads * head_dim)
    )
    return (attn_out, new_k, new_v)


def solution(mesh):
    in_specs = (
        P("blk", "kv"),
        P(),
        P(None, "kv"),
        P(None, "kv"),
        P(None, "kv"),
        P("kv"),
        P("kv"),
        P("kv"),
        P("blk", None, "kv"),
        P("blk", None, "kv"),
        P(),
        P(),
    )
    out_specs = (P("blk", "kv"), P("blk", None, "kv"), P("blk", None, "kv"))
    return jax.shard_map(
        on_device, mesh=mesh, in_specs=in_specs, out_specs=out_specs, check_vma=False
    )
```

profile of v0, /device:TPU:1, one launch (start us, length us, event | category | flops | bytes accessed | tf_op | source)
XLA Modules:
  0.0 996.7 jit_solution(12240637072034662351)
XLA Ops:
  10.1 30.3 %all-gather.5.cloned.1.call-done = bf16[128,5120]{1,0:T(8,128)(2,1)} async-done(((bf16[128,640]{1,0:T(8,128)(2,1)}), bf16[128,5120]{1,0:T(8,128)(2,1)}) %all-gather.5.cloned.1.call-update) | async-done | bytes 1310736 | tf_op jit(solution)/shard_map/all_gather | solution.py:96
  53.5 33.5 %gather_fusion = s32[4096]{0:T(1024)S(1)} fusion(s32[4,72]{1,0:T(4,128)S(1)} %copy-done.1, s32[4096]{0:T(1024)S(1)} %bitcast.109), kind=kCustom, calls=%fused_computation | custom fusion | bytes 65536 | tf_op jit(solution)/shard_map/gather | solution.py:121
  87.1 24.8 %all-gather.7.cloned.1.call-done = bf16[4096,128]{0,1:T(8,128)(2,1)} async-done(((bf16[128,128]{0,1:T(8,128)(2,1)}), bf16[4096,128]{0,1:T(8,128)(2,1)}) %all-gather.7.cloned.1.call-update) | async-done | bytes 1048592 | tf_op jit(solution)/shard_map/all_gather | solution.py:126
  113.6 11.0 %scatter_fusion = bf16[1536,128]{1,0:T(8,128)(2,1)S(1)} fusion(bf16[1536,128]{1,0:T(8,128)(2,1)S(1)} %bitcast.113, s32[4096]{0:T(1024)S(1)} %bitcast.122, bf16[4096,128]{1,0:T(8,128)(2,1)S(1)} %copy.31), kind=kCustom, calls=%fused_computation.1 | custom fusion | bytes 3162112 | tf_op jit(solution)/shard_map/scatter | solution.py:40
  124.6 65.2 %all-gather.11.cloned.1.call-done = bf16[4096,128]{1,0:T(8,128)(2,1)} async-done(((bf16[128,128]{1,0:T(8,128)(2,1)}), bf16[4096,128]{1,0:T(8,128)(2,1)}) %all-gather.11.cloned.1.call-update) | async-done | bytes 1048592 | tf_op jit(solution)/shard_map/all_gather | solution.py:127
  189.9 11.3 %scatter_fusion.1 = bf16[1536,128]{1,0:T(8,128)(2,1)S(1)} fusion(bf16[1536,128]{1,0:T(8,128)(2,1)S(1)} %bitcast.111, s32[4096]{0:T(1024)S(1)} %bitcast.123, bf16[4096,128]{1,0:T(8,128)(2,1)} %all-gather.11.cloned.1.call-done), kind=kCustom, calls=%fused_computation.2 | custom fusion | bytes 3162112 | tf_op jit(solution)/shard_map/scatter | solution.py:40
  201.2 78.4 %all-gather.9.cloned.1.call-done = bf16[4096,640]{0,1:T(8,128)(2,1)} async-done(((bf16[128,640]{0,1:T(8,128)(2,1)}), bf16[4096,640]{0,1:T(8,128)(2,1)}) %all-gather.9.cloned.1.call-update) | async-done | bytes 5242896 | tf_op jit(solution)/shard_map/all_gather | solution.py:125
  279.6 5.3 broadcast_in_dim.156
  284.9 124.3 %while.18 = (s32[]{:T(128)}, f32[4096,1,5]{0,2,1:T(8,128)S(1)}, f32[4096,1,5]{0,2,1:T(8,128)S(1)}, f32[4096,1,5,128]{0,3,2,1:T(8,128)}, s32[]{:T(128)}, /*index=...) while((s32[]{:T(128)}, f32[4096,1,5]{0,2,1:T(8,128)S(1)}, ...), condition=%wide.region_11.12_spmd.clone, body=%wide.region_5.11_spmd.clone.sunk | while | flops 344343360 | bytes 15429561 | solution.py:164
  290.4 4.2 fusion.84
  300.7 4.3 fusion.84
  311.1 4.2 fusion.84
  321.5 4.2 fusion.84
  342.1 4.3 fusion.84
  362.9 4.2 fusion.84
  373.2 4.3 fusion.84
  383.6 4.2 fusion.84
  394.0 4.2 fusion.84
  404.3 4.2 fusion.84
  409.2 113.6 %pmax.7 = bf16[4096,1,5]{0,2,1:T(8,128)(2,1)S(1)} all-reduce(bf16[4096,1,5]{0,2,1:T(8,128)(2,1)S(1)} %convert_element_type.73), channel_id=1, replica_groups=mesh['kv'=8,'blk'=32] {'blk'}, use_global_device_ids=true, to_apply=%region_12.13 | all-reduce | flops 20480 | bytes 81920 | tf_op jit(solution)/shard_map/pmax | solution.py:165
  524.3 7.7 multiply_convert_fusion
  532.0 7.9 copy.41
  539.9 219.6 %reduce-scatter.9.cloned.1.call-done = bf16[128,5]{1,0:T(8,128)(2,1)} async-done(((bf16[4096,5]{1,0:T(8,128)(2,1)}), bf16[128,5]{1,0:T(8,128)(2,1)}) %reduce-scatter.9.cloned.1.call-update) | async-done | bytes 1296
  760.3 227.6 %reduce-scatter.7.cloned.1.call-done = bf16[128,640]{1,0:T(8,128)(2,1)} async-done(((bf16[4096,640]{1,0:T(8,128)(2,1)}), bf16[128,640]{1,0:T(8,128)(2,1)}) %reduce-scatter.7.cloned.1.call-update) | async-done | bytes 163856
  (178 shorter events, 87.1 us)
Async XLA Ops:
  7.2 35.1 %copy-start = (bf16[5120,128]{1,0:T(8,128)(2,1)S(1)}, bf16[5120,128]{1,0:T(8,128)(2,1)}, u32[]{:S(2)}) copy-start(bf16[5120,128]{1,0:T(8,128)(2,1)} %param.17) | copy-start | bytes 3932164
  7.2 33.3 %all-gather.5.cloned.1.call-start = ((), (), s32[]{:S(2)}) async-start(), calls=%async_computation.2 | async-start | bytes 1474560 | tf_op jit(solution)/shard_map/all_gather | solution.py:96
  7.2 38.0 %copy-start.9 = (bf16[128]{0:T(256)(128)(2,1)S(1)}, bf16[128]{0:T(256)(128)(2,1)}, u32[]{:S(2)}) copy-start(bf16[128]{0:T(256)(128)(2,1)} %param.21) | copy-start | bytes 772
  7.9 104.0 %all-gather.7.cloned.1.call-start = ((), (), s32[]{:S(2)}) async-start(), calls=%async_computation.3 | async-start | bytes 1081344 | tf_op jit(solution)/shard_map/all_gather | solution.py:126
  40.5 4.8 copy-start.6
  44.3 3.5 copy-start.7
  45.2 144.7 %all-gather.11.cloned.1.call-start = ((), (), s32[]{:S(2)}) async-start(), calls=%async_computation.5 | async-start | bytes 1081344 | tf_op jit(solution)/shard_map/all_gather | solution.py:127
  47.8 231.8 %all-gather.9.cloned.1.call-start = ((), (), s32[]{:S(2)}) async-start(), calls=%async_computation.4 | async-start | bytes 5406720 | tf_op jit(solution)/shard_map/all_gather | solution.py:125
  48.1 5.1 copy-start.8
  52.2 1.3 copy-start.1
  53.1 706.4 %reduce-scatter.9.cloned.1.call-start = ((), (), s32[]{:S(2)}) async-start(), calls=%async_computation.7 | async-start | bytes 1081344
  87.0 26.6 %copy-start.5 = (bf16[12,128,128]{2,1,0:T(8,128)(2,1)S(1)}, bf16[12,128,128]{2,1,0:T(8,128)(2,1)}, u32[]{:S(2)}) copy-start(bf16[12,128,128]{2,1,0:T(8,128)(2,1)} %param.22) | copy-start | bytes 1179652
  113.6 76.3 %copy-start.3 = (bf16[12,128,128]{2,1,0:T(8,128)(2,1)S(1)}, bf16[12,128,128]{2,1,0:T(8,128)(2,1)}, u32[]{:S(2)}) copy-start(bf16[12,128,128]{2,1,0:T(8,128)(2,1)} %param.23) | copy-start | bytes 1179652
  409.2 122.9 %copy-start.2 = (bf16[12,128,128]{2,1,0:T(8,128)(2,1)}, bf16[12,128,128]{2,1,0:T(8,128)(2,1)S(1)}, u32[]{:S(2)}) copy-start(bf16[12,128,128]{2,1,0:T(8,128)(2,1)S(1)} %get-tuple-element.435) | copy-start | bytes 1179652
  409.2 122.9 %copy-start.4 = (bf16[12,128,128]{2,1,0:T(8,128)(2,1)}, bf16[12,128,128]{2,1,0:T(8,128)(2,1)S(1)}, u32[]{:S(2)}) copy-start(bf16[12,128,128]{2,1,0:T(8,128)(2,1)S(1)} %get-tuple-element.436) | copy-start | bytes 1179652
  524.3 463.6 %reduce-scatter.7.cloned.1.call-start = ((), (), s32[]{:S(2)}) async-start(), calls=%async_computation.6 | async-start | bytes 5406720
Sparse Core Ops, SparseCore 0:
  9.9 30.5 all-gather.4
  45.3 66.5 all-gather.6
  115.1 74.7 all-gather.10
  192.8 86.7 all-gather.8
  524.4 235.0 reduce-scatter.8
  763.3 224.5 reduce-scatter.6
where the time goes:
time: 1000 us; the launch traced here: 997 us
  waiting for transfers between devices  647 us (65%)
  blocking collectives  114 us (11%)
  matrix products  84 us (8%)
  local copies, waits for them, and re-layouts  75.1 us (8%)
  other arithmetic  46.2 us (5%)
  loops' own time  16.5 us (2%)
  between operations  14.4 us (1%)
    unnamed x8, waiting for transfers between devices  448 us
    pmax x1, blocking collectives, on_device(): best = lax.pmax(top.astype(jnp.bfloat16), 'blk').astype(top.dtype)  114 us
    all_gather x1, waiting for transfers between devices, on_device(): lax.all_gather(fresh_queries, 'blk', axis=0, tiled=True)  78.4 us
    all_gather x1, waiting for transfers between devices, on_device(): lax.all_gather(fresh_values, 'blk', axis=0, tiled=True)  65.2 us
    dot_general x12, matrix products, attend_block(): jnp.einsum('rgfk,kgd->rgfd', weights.astype(jnp.bfloat16), values, prefer...  50.9 us
    gather x1, local copies, waits for them, and re-layouts, on_device(): block_table[all_req, all_pos // block_size] * block_size  33.5 us
    all_gather x1, waiting for transfers between devices, on_device(): whole = lax.all_gather(hidden_in, 'kv', axis=1, tiled=True)  30.3 us
    all_gather x1, waiting for transfers between devices, on_device(): lax.all_gather(fresh_keys, 'blk', axis=0, tiled=True)  24.8 us
  transfers between devices with their start and end apart: 6, of which 6 were waited for; matrix products, arithmetic and copies ran while one was open for 8% of the time, Pallas kernels for 0%

commit v1 on v0

v1 whole, which is shorter than its diff:
```python
import functools
import math

import jax
import jax.numpy as jnp
from jax import lax
from jax.experimental import pallas as pl
from jax.experimental.pallas import tpu as pltpu
from jax.sharding import PartitionSpec as P

HEAD_SIZE = 128


EPS = 1e-06
THETA = 1000000.0
NEG_FILL = -1e30


def apply_rotary(values, token_positions, head_dim):
    half = head_dim // 2
    rates = THETA ** (-(jnp.arange(half, dtype=jnp.float32) * 2.0) / head_dim)
    angle = token_positions.astype(jnp.float32)[:, None] * rates[None, :]
    cosine = jnp.cos(angle)[:, None, :]
    sine = jnp.sin(angle)[:, None, :]
    first = values[..., :half]
    second_half = values[..., half:]
    return jnp.concatenate(
        [first * cosine - second_half * sine, second_half * cosine + first * sine], axis=-1
    )


def lookup(table_values, slot_index):
    matches = slot_index[:, None] == jnp.arange(table_values.shape[0], dtype=jnp.int32)[None, :]
    return jnp.sum(jnp.where(matches, table_values[None, :], 0), axis=1)


def block_owner(block_table, block_id):
    matched = block_table == block_id
    row_ids = jnp.arange(block_table.shape[0], dtype=jnp.int32)[:, None]
    col_ids = jnp.arange(block_table.shape[1], dtype=jnp.int32)[None, :]
    used = jnp.any(matched)
    owner = jnp.sum(jnp.where(matched, row_ids, 0))
    column = jnp.sum(jnp.where(matched, col_ids, 0))
    return (used, owner, column)


def merge_new_rows(key_cache, value_cache, kv_all, used, owner, column, cached_len, span):
    nb_dev, block_size, kv_width = key_cache.shape
    padded = jnp.pad(kv_all, ((block_size, block_size), (0, 0)))
    start = block_size + owner * span + column * block_size - cached_len[owner]
    rows = jax.vmap(lambda s: lax.dynamic_slice_in_dim(padded, s, block_size, 0))(start)
    key_pos = column[:, None] * block_size + jnp.arange(block_size, dtype=jnp.int32)[None, :]
    first_new = cached_len[owner][:, None]
    fresh = (used[:, None] == 1) & (key_pos >= first_new) & (key_pos < first_new + span)
    new_k = jnp.where(fresh[..., None], rows[..., :kv_width], key_cache)
    new_v = jnp.where(fresh[..., None], rows[..., kv_width:], value_cache)
    return new_k, new_v


def attention_kernel(
    used_ref, owner_ref, column_ref, clen_ref, q_ref, k_ref, v_ref, o_ref, m_sc, l_sc, acc_sc,
    *, q_heads, head_dim
):
    r = pl.program_id(0)
    i = pl.program_id(1)
    rows = q_ref.shape[0]
    block_size = k_ref.shape[1]

    @pl.when(i == 0)
    def _init():
        m_sc[...] = jnp.full(m_sc.shape, NEG_FILL, jnp.float32)
        l_sc[...] = jnp.zeros(l_sc.shape, jnp.float32)
        acc_sc[...] = jnp.zeros(acc_sc.shape, jnp.float32)

    @pl.when((used_ref[i] == 1) & (owner_ref[i] == r))
    def _work():
        keys = k_ref[0]
        values = v_ref[0]
        query_pos = clen_ref[r] + lax.broadcasted_iota(jnp.int32, (rows, block_size), 0)
        key_pos = column_ref[i] * block_size + lax.broadcasted_iota(
            jnp.int32, (rows, block_size), 1
        )
        allowed = key_pos <= query_pos
        for g in range(q_heads):
            queries = q_ref[:, g * head_dim : (g + 1) * head_dim]
            score = lax.dot_general(
                queries, keys, (((1,), (1,)), ((), ())), preferred_element_type=jnp.float32
            ) / math.sqrt(head_dim)
            score = jnp.where(allowed, score, NEG_FILL)
            top = m_sc[g]
            new_top = jnp.maximum(top, jnp.max(score, axis=1, keepdims=True))
            weights = jnp.where(allowed, jnp.exp(score - new_top), 0.0)
            factor = jnp.exp(top - new_top)
            l_sc[g] = l_sc[g] * factor + jnp.sum(weights, axis=1, keepdims=True)
            acc_sc[g] = acc_sc[g] * factor + jnp.dot(
                weights.astype(jnp.bfloat16), values, preferred_element_type=jnp.float32
            )
            m_sc[g] = new_top

    @pl.when(i == pl.num_programs(1) - 1)
    def _finish():
        lane = lax.broadcasted_iota(jnp.int32, (rows, head_dim), 1)
        stats = jnp.zeros((rows, head_dim), jnp.float32)
        for g in range(q_heads):
            top = m_sc[g]
            valid = top > NEG_FILL / 2
            ref = jnp.where(valid, top.astype(jnp.bfloat16).astype(jnp.float32), NEG_FILL)
            factor = jnp.where(valid, jnp.exp(top - ref), 0.0)
            o_ref[:, g * head_dim : (g + 1) * head_dim] = (acc_sc[g] * factor).astype(o_ref.dtype)
            stats = jnp.where(lane == g, l_sc[g] * factor, stats)
            stats = jnp.where(lane == q_heads + g, ref, stats)
        o_ref[:, q_heads * head_dim :] = stats.astype(o_ref.dtype)


def local_attention(packed_all, new_k, new_v, used, owner, column, cached_len, span, q_heads, head_dim):
    tokens = packed_all.shape[0]
    nb_dev, block_size, kv_width = new_k.shape
    requests = tokens // span
    out_width = (q_heads + 1) * head_dim
    grid_spec = pltpu.PrefetchScalarGridSpec(
        num_scalar_prefetch=4,
        grid=(requests, nb_dev),
        in_specs=[
            pl.BlockSpec((span, q_heads * head_dim), lambda r, i, *_: (r, 0)),
            pl.BlockSpec((1, block_size, kv_width), lambda r, i, *_: (i, 0, 0)),
            pl.BlockSpec((1, block_size, kv_width), lambda r, i, *_: (i, 0, 0)),
        ],
        out_specs=pl.BlockSpec((span, out_width), lambda r, i, *_: (r, 0)),
        scratch_shapes=[
            pltpu.VMEM((q_heads, span, head_dim), jnp.float32),
            pltpu.VMEM((q_heads, span, head_dim), jnp.float32),
            pltpu.VMEM((q_heads, span, head_dim), jnp.float32),
        ],
    )
    flops = 4 * nb_dev * span * q_heads * block_size * head_dim
    return pl.pallas_call(
        functools.partial(attention_kernel, q_heads=q_heads, head_dim=head_dim),
        grid_spec=grid_spec,
        out_shape=jax.ShapeDtypeStruct((tokens, out_width), jnp.bfloat16),
        compiler_params=pltpu.CompilerParams(
            dimension_semantics=("arbitrary", "arbitrary"), vmem_limit_bytes=48 * 1024 * 1024
        ),
        cost_estimate=pl.CostEstimate(
            flops=flops,
            transcendentals=nb_dev * span * q_heads * block_size,
            bytes_accessed=tokens * (q_heads * head_dim + out_width) * 2,
        ),
    )(used, owner, column, cached_len, packed_all, new_k, new_v)


def on_device(
    hidden_in,
    norm_gain,
    w_query,
    key_weight,
    value_weight,
    b_query,
    key_bias,
    value_bias,
    key_cache,
    value_cache,
    cached_len,
    block_table,
):
    tok_dev = hidden_in.shape[0]
    n_blk = lax.axis_size("blk")
    device = lax.axis_index("blk")
    requests = cached_len.shape[0]
    tokens = tok_dev * n_blk
    span = tokens // requests
    nb_dev, block_size, kv_width = key_cache.shape
    head_dim = HEAD_SIZE
    kv_heads = kv_width // head_dim
    q_heads = w_query.shape[1] // head_dim
    group_size = q_heads // kv_heads
    gain = norm_gain.astype(jnp.float32)
    whole = lax.all_gather(hidden_in, "kv", axis=1, tiled=True)
    wide_in = whole.astype(jnp.float32)
    scale = lax.rsqrt(jnp.mean(wide_in * wide_in, axis=1, keepdims=True) + EPS)
    normed = (wide_in * scale * gain[None, :]).astype(jnp.bfloat16)
    q_lin = jnp.dot(normed, w_query, preferred_element_type=jnp.float32)
    key_linear = jnp.dot(normed, key_weight, preferred_element_type=jnp.float32)
    value_linear = jnp.dot(normed, value_weight, preferred_element_type=jnp.float32)
    my_tokens = device * tok_dev + jnp.arange(tok_dev, dtype=jnp.int32)
    my_pos = lookup(cached_len, my_tokens // span) + my_tokens % span
    fresh_queries = apply_rotary(
        (q_lin + b_query.astype(jnp.float32)[None, :]).reshape(tok_dev, q_heads, head_dim),
        my_pos,
        head_dim,
    )
    fresh_queries = fresh_queries.astype(jnp.bfloat16).reshape(tok_dev, q_heads * head_dim)
    fresh_keys = apply_rotary(
        (key_linear + key_bias.astype(jnp.float32)[None, :]).reshape(tok_dev, kv_heads, head_dim),
        my_pos,
        head_dim,
    )
    fresh_keys = fresh_keys.astype(jnp.bfloat16).reshape(tok_dev, kv_width)
    fresh_values = (value_linear + value_bias.astype(jnp.float32)[None, :]).astype(jnp.bfloat16)
    q_width = q_heads * head_dim
    packed = jnp.concatenate([fresh_queries, fresh_keys, fresh_values], axis=1)
    packed_all = lax.all_gather(packed, "blk", axis=0, tiled=True)
    first_block = device * nb_dev
    owner_info = [block_owner(block_table, first_block + b) for b in range(nb_dev)]
    used = jnp.stack([o[0] for o in owner_info]).astype(jnp.int32)
    owner = jnp.stack([o[1] for o in owner_info]).astype(jnp.int32)
    column = jnp.stack([o[2] for o in owner_info]).astype(jnp.int32)
    new_k, new_v = merge_new_rows(
        key_cache, value_cache, packed_all[:, q_width:], used, owner, column, cached_len, span
    )
    parts = local_attention(
        packed_all, new_k, new_v, used, owner, column, cached_len, span, q_heads, head_dim
    )
    got = lax.all_to_all(parts, "blk", 0, 0, tiled=True).reshape(n_blk, tok_dev, q_width + 128)
    got = got.astype(jnp.float32)
    got_w = got[..., :q_width].reshape(n_blk, tok_dev, q_heads, head_dim)
    got_l = got[..., q_width : q_width + group_size]
    got_m = got[..., q_width + group_size : q_width + 2 * group_size]
    best = jnp.max(got_m, axis=0)
    scale_d = jnp.exp(got_m - best[None])
    mine_total = jnp.sum(got_l * scale_d, axis=0)
    mine_weighted = jnp.sum(got_w * scale_d[..., None], axis=0)
    attn_out = (
        (mine_weighted / mine_total[..., None])
        .astype(jnp.bfloat16)
        .reshape(tok_dev, q_heads * head_dim)
    )
    return (attn_out, new_k, new_v)


def solution(mesh):
    in_specs = (
        P("blk", "kv"),
        P(),
        P(None, "kv"),
        P(None, "kv"),
        P(None, "kv"),
        P("kv"),
        P("kv"),
        P("kv"),
        P("blk", None, "kv"),
        P("blk", None, "kv"),
        P(),
        P(),
    )
    out_specs = (P("blk", "kv"), P("blk", None, "kv"), P("blk", None, "kv"))
    return jax.shard_map(
        on_device, mesh=mesh, in_specs=in_specs, out_specs=out_specs, check_vma=False
    )
```

time: 1000 us -> 387 us (0.39)
  waiting for transfers between devices: 647 us -> 73.8 us
  matrix products: 84 us -> 7.13 us
  blocking collectives: 114 us -> 155 us
  other arithmetic: 46.2 us -> 23.2 us
  Pallas kernels: 0 us -> 22.8 us
  loops' own time: 16.5 us -> 0.02 us
    unnamed x8 -> x2, waiting for transfers between devices: 448 us -> 0.7 us
    all_to_all x0 -> x1, blocking collectives: none -> 155 us  [on_device(): lax.all_to_all(parts, 'blk', 0, 0, tiled=True)]
    all_gather x3 -> x1, waiting for transfers between devices: 168 us -> 44.3 us  [on_device(): packed_all = lax.all_gather(packed, 'blk', axis=0, tiled=True)]
    pmax x1 -> x0, blocking collectives: 114 us -> none  [on_device(): best = lax.pmax(top.astype(jnp.bfloat16), 'blk').astype(top.dtype)]
    dot_general x24 -> x0, matrix products: 75.3 us -> none  [the longest x12 50.9 us: attend_block(): jnp.einsum('rgfk,kgd->rgfd', weights.astype(jnp.bfloat16), values, prefer...]
    another operation x0 -> x5, local copies, waits for them, and re-layouts: none -> 38.3 us  [the longest x2 15.6 us: on_device(): owner = jnp.stack([o[1] for o in owner_info]).astype(jnp.int32)]
    pallas_call x0 -> x1, Pallas kernels: none -> 22.8 us  [local_attention(): pl.pallas_call(functools.partial(attention_kernel, q_heads=q_heads, head_...]
    scatter x2 -> x0, local copies, waits for them, and re-layouts: 22.3 us -> none  [append_rows(): return flattened.at[target].set(rows, mode='drop').reshape(cache.shape)]
  transfers between devices with their start and end apart: 6 -> 2, of which waited for: 6 -> 2; matrix products, arithmetic and copies ran while one was open for 8% -> 14% of each run, Pallas kernels for 0% -> 0%
where the time goes in v1:
time: 387 us; the launch traced here: 381 us
  blocking collectives  155 us (40%)
  local copies, waits for them, and re-layouts  85 us (22%)
  waiting for transfers between devices  73.8 us (19%)
  other arithmetic  23.2 us (6%)
  Pallas kernels  22.8 us (6%)
  between operations  14.3 us (4%)
  matrix products  7.13 us (2%)
    all_to_all x1, blocking collectives, on_device(): lax.all_to_all(parts, 'blk', 0, 0, tiled=True)  155 us
    all_gather x1, waiting for transfers between devices, on_device(): packed_all = lax.all_gather(packed, 'blk', axis=0, tiled=True)  44.3 us
    gather x36, local copies, waits for them, and re-layouts  33.1 us
    all_gather x1, waiting for transfers between devices, on_device(): whole = lax.all_gather(hidden_in, 'kv', axis=1, tiled=True)  28.8 us
    pallas_call x1, Pallas kernels, local_attention(): pl.pallas_call(functools.partial(attention_kernel, q_heads=q_heads, head_...  22.8 us
    another operation x2, local copies, waits for them, and re-layouts, on_device(): owner = jnp.stack([o[1] for o in owner_info]).astype(jnp.int32)  15.6 us
    another operation x2, local copies, waits for them, and re-layouts, on_device(): column = jnp.stack([o[2] for o in owner_info]).astype(jnp.int32)  15 us
    all_to_all x1, local copies, waits for them, and re-layouts, on_device(): lax.all_to_all(parts, 'blk', 0, 0, tiled=True)  8.66 us
  transfers between devices with their start and end apart: 2, of which 2 were waited for; matrix products, arithmetic and copies ran while one was open for 14% of the time, Pallas kernels for 0%

profile of v1, /device:TPU:1, one launch (start us, length us, event | category | flops | bytes accessed | tf_op | source)
XLA Modules:
  0.0 381.4 jit_solution(5074706851053167185)
XLA Ops:
  11.7 28.8 %all-gather.3.cloned.1.call-done = bf16[128,5120]{1,0:T(8,128)(2,1)} async-done(((bf16[128,640]{1,0:T(8,128)(2,1)}), bf16[128,5120]{1,0:T(8,128)(2,1)}) %all-gather.3.cloned.1.call-update) | async-done | bytes 1310736 | tf_op jit(solution)/shard_map/all_gather | solution.py:177
  42.1 4.6 %convolution_add_fusion = f32[128,640]{1,0:T(8,128)S(1)} fusion(bf16[5120,640]{1,0:T(8,128)(2,1)} %param.14, f32[640]{0:T(1024)S(1)} %convert_element_type.54, bf16[128,5120]{1,0:T(8,128)(2,1)} %all-gather.3.cloned.1.call-done, f32[5120]{0:T(1024)S(1)} %convert_element_type.52, f32[128]{0:T(128)S(1)} %add_rsqrt_fusion), kind=kOutput, calls=%fused_computation.10 | convolution fusion | flops 841564160 | bytes 8215552 | tf_op jit(solution)/shard_map/dot_general | solution.py:181
  60.1 7.8 %stack.220 = s32[12,1]{0,1:T(1,128)S(1)} concatenate(s32[1,1]{0,1:T(1,128)} %bitcast.41, s32[1,1]{0,1:T(1,128)} %bitcast.42, s32[1,1]{0,1:T(1,128)} %bitcast.43, s32[1,1]{0,1:T(1,128)} %bitcast.44, s32[1,1]{0,1:T(1,128)} %bitcast.45, s32[1,1]{0,1:T(1,128)} %bitcast.46, s32[1,1]{0,1:T(1,128)} %bitcast.47, s32[1,1]{0,1:T(1,128)} %bitcast.48, s32[1,1]{0,1:T(1,128)} %bitcast.49, ...), dimensions={0} | concatenate | bytes 96 | tf_op jit(solution)/shard_map/stack | solution.py:205
  68.6 7.5 %stack.233 = s32[12,1]{0,1:T(1,128)S(1)} concatenate(s32[1,1]{0,1:T(1,128)} %bitcast.54, s32[1,1]{0,1:T(1,128)} %bitcast.55, s32[1,1]{0,1:T(1,128)} %bitcast.56, s32[1,1]{0,1:T(1,128)} %bitcast.57, s32[1,1]{0,1:T(1,128)} %bitcast.58, s32[1,1]{0,1:T(1,128)} %bitcast.59, s32[1,1]{0,1:T(1,128)} %bitcast.60, s32[1,1]{0,1:T(1,128)} %bitcast.61, s32[1,1]{0,1:T(1,128)} %bitcast.62, ...), dimensions={0} | concatenate | bytes 96 | tf_op jit(solution)/shard_map/stack | solution.py:206
  76.1 7.6 %stack.181 = pred[12]{0:T(512)(128)(4,1)S(1)} concatenate(pred[1]{0:T(512)(128)(4,1)} %bitcast, pred[1]{0:T(512)(128)(4,1)} %bitcast.1, pred[1]{0:T(512)(128)(4,1)} %bitcast.2, pred[1]{0:T(512)(128)(4,1)} %bitcast.3, pred[1]{0:T(512)(128)(4,1)} %bitcast.4, pred[1]{0:T(512)(128)(4,1)} %bitcast.5, pred[1]{0:T(512)(128)(4,1)} %bitcast.6, pred[1]{0:T(512)(128)(4,1)} %bitcast.7, ...), dimensions={0} | concatenate | bytes 24 | tf_op jit(solution)/shard_map/stack | solution.py:204
  83.8 7.5 %stack.207.column_ref = s32[12]{0:T(128)S(1)} concatenate(s32[1]{0:T(128)} %bitcast.24, s32[1]{0:T(128)} %bitcast.25, s32[1]{0:T(128)} %bitcast.26, s32[1]{0:T(128)} %bitcast.27, s32[1]{0:T(128)} %bitcast.28, s32[1]{0:T(128)} %bitcast.29, s32[1]{0:T(128)} %bitcast.30, s32[1]{0:T(128)} %bitcast.31, s32[1]{0:T(128)} %bitcast.32, s32[1]{0:T(128)} %bitcast.33, s32[1]{0:T(128)} %bitcast.34, ...), dimensions={0} | concatenate | bytes 96 | tf_op jit(solution)/shard_map/stack | solution.py:206
  91.3 7.8 %stack.194.owner_ref = s32[12]{0:T(128)S(1)} concatenate(s32[1]{0:T(128)} %bitcast.12, s32[1]{0:T(128)} %bitcast.13, s32[1]{0:T(128)} %bitcast.14, s32[1]{0:T(128)} %bitcast.15, s32[1]{0:T(128)} %bitcast.16, s32[1]{0:T(128)} %bitcast.17, s32[1]{0:T(128)} %bitcast.18, s32[1]{0:T(128)} %bitcast.19, s32[1]{0:T(128)} %bitcast.20, s32[1]{0:T(128)} %bitcast.21, s32[1]{0:T(128)} %bitcast.22, ...), dimensions={0} | concatenate | bytes 96 | tf_op jit(solution)/shard_map/stack | solution.py:205
  99.2 44.3 %all-gather.5.cloned.1.call-done.q_ref = bf16[4096,896]{1,0:T(8,128)(2,1)} async-done(((bf16[128,896]{1,0:T(8,128)(2,1)}), bf16[4096,896]{1,0:T(8,128)(2,1)}) %all-gather.5.cloned.1.call-update) | async-done | bytes 7340048 | tf_op jit(solution)/shard_map/all_gather | solution.py:201
  146.7 33.1 %while.1 = (s32[]{:T(128)}, bf16[4352,256]{1,0:T(8,128)(2,1)}, s32[12,2]{0,1:T(2,128)S(1)}, bf16[12,128,256]{2,1,0:T(8,128)(2,1)}, s32[]{:T(128)}) while((s32[]{:T(128)}, bf16[4352,256]{1,0:T(8,128)(2,1)}, s32[12,2]{0,1:T(2,128)S(1)}, bf16[12,128,256]{2,1,0:T(8,128)(2,1)}, s32[]{:T(128)}) %tuple.86), condition=%wide.while_cond, body=%wide.while_body.sunk | while | flops 2 | bytes 131685 | solution.py:51
  147.2 2.2 bitcast_dynamic-update-slice_fusion.2
  150.0 2.2 bitcast_dynamic-update-slice_fusion.2
  152.8 2.2 bitcast_dynamic-update-slice_fusion.2
  158.3 2.2 bitcast_dynamic-update-slice_fusion.2
  161.0 2.2 bitcast_dynamic-update-slice_fusion.2
  163.8 2.2 bitcast_dynamic-update-slice_fusion.2
  166.5 2.2 bitcast_dynamic-update-slice_fusion.2
  169.3 2.2 bitcast_dynamic-update-slice_fusion.2
  172.1 2.2 bitcast_dynamic-update-slice_fusion.2
  174.8 2.2 bitcast_dynamic-update-slice_fusion.2
  177.6 2.2 bitcast_dynamic-update-slice_fusion.2
  181.4 22.8 %shard_map.139 = bf16[4096,768]{1,0:T(8,128)(2,1)} custom-call(s32[12]{0:T(128)S(1)} %get-tuple-element.105.used_ref, s32[12]{0:T(128)S(1)} %stack.194.owner_ref, s32[12]{0:T(128)S(1)} %stack.207.column_ref, s32[4]{0:T(128)S(1)} %copy-done.1, bf16[4096,896]{1,0:T(8,128)(2,1)} %all-gather.5.cloned.1.call-done.q_ref, ...), custom_call_target="tpu_custom_call" | custom-call | flops 4026531840 | bytes 11534336 | tf_op jit(solution)/shard_map/pallas_call | solution.py:136
  204.2 8.7 %copy.27 = bf16[32,128,768]{1,2,0:T(8,128)(2,1)} copy(bf16[32,128,768]{2,1,0:T(8,128)(2,1)} %bitcast.91) | data formatting | bytes 12582912 | tf_op jit(solution)/shard_map/all_to_all | solution.py:213
  212.9 155.1 %all_to_all.9 = bf16[32,128,768]{1,2,0:T(8,128)(2,1)} all-to-all(bf16[32,128,768]{1,2,0:T(8,128)(2,1)} %copy.27), channel_id=1, replica_groups=mesh['kv'=8,'blk'=32] {'blk'}, dimensions={0} | all-to-all | bytes 12582912 | tf_op jit(solution)/shard_map/all_to_all | solution.py:213
  368.0 4.3 %convert_element_type.60 = f32[32,128,768]{1,2,0:T(8,128)S(1)} convert(bf16[32,128,768]{1,2,0:T(8,128)(2,1)} %all_to_all.9) | non-fusion elementwise | flops 3145728 | bytes 18874368 | tf_op jit(solution)/shard_map/convert_element_type | solution.py:214
  (91 shorter events, 36.4 us)
Async XLA Ops:
  7.2 39.7 %copy-start = (bf16[5120,128]{1,0:T(8,128)(2,1)S(1)}, bf16[5120,128]{1,0:T(8,128)(2,1)}, u32[]{:S(2)}) copy-start(bf16[5120,128]{1,0:T(8,128)(2,1)} %param.15) | copy-start | bytes 3932164
  7.2 33.3 %all-gather.3.cloned.1.call-start = ((), (), s32[]{:S(2)}) async-start(), calls=%async_computation.1 | async-start | bytes 1474560 | tf_op jit(solution)/shard_map/all_gather | solution.py:177
  7.9 135.6 %all-gather.5.cloned.1.call-start = ((), (), s32[]{:S(2)}) async-start(), calls=%async_computation.2 | async-start | bytes 7569408 | tf_op jit(solution)/shard_map/all_gather | solution.py:201
  42.1 4.8 %copy-start.4 = (bf16[128,5120]{1,0:T(8,128)(2,1)S(1)}, bf16[128,5120]{1,0:T(8,128)(2,1)}, u32[]{:S(2)}) copy-start(bf16[128,5120]{1,0:T(8,128)(2,1)} %all-gather.3.cloned.1.call-done) | copy-start | bytes 3932164
  47.9 3.0 copy-start.5
  47.9 20.0 %copy-start.1 = (s32[4]{0:T(128)S(1)}, s32[4]{0:T(128)}, u32[]{:S(2)}) copy-start(s32[4]{0:T(128)} %clen_ref.1) | copy-start | bytes 52
  143.5 1.6 slice-start
  181.4 22.9 %copy-start.2 = (bf16[12,128,128]{2,1,0:T(8,128)(2,1)}, bf16[12,128,128]{2,1,0:T(8,128)(2,1)S(1)}, u32[]{:S(2)}) copy-start(bf16[12,128,128]{2,1,0:T(8,128)(2,1)S(1)} %get-tuple-element.63.v_ref) | copy-start | bytes 1179652
  181.4 22.9 %copy-start.3 = (bf16[12,128,128]{2,1,0:T(8,128)(2,1)}, bf16[12,128,128]{2,1,0:T(8,128)(2,1)S(1)}, u32[]{:S(2)}) copy-start(bf16[12,128,128]{2,1,0:T(8,128)(2,1)S(1)} %get-tuple-element.64.k_ref) | copy-start | bytes 1179652
Sparse Core Ops, SparseCore 0:
  9.9 30.5 all-gather.2
  51.0 92.4 all-gather.4

commit v2 on v1

--- a/solution.py
+++ b/solution.py
@@ -34,37 +34,43 @@
     return jnp.sum(jnp.where(matches, table_values[None, :], 0), axis=1)
 
 
-def block_owner(block_table, block_id):
-    matched = block_table == block_id
-    row_ids = jnp.arange(block_table.shape[0], dtype=jnp.int32)[:, None]
-    col_ids = jnp.arange(block_table.shape[1], dtype=jnp.int32)[None, :]
-    used = jnp.any(matched)
-    owner = jnp.sum(jnp.where(matched, row_ids, 0))
-    column = jnp.sum(jnp.where(matched, col_ids, 0))
-    return (used, owner, column)
-
-
-def merge_new_rows(key_cache, value_cache, kv_all, used, owner, column, cached_len, span):
-    nb_dev, block_size, kv_width = key_cache.shape
-    padded = jnp.pad(kv_all, ((block_size, block_size), (0, 0)))
-    start = block_size + owner * span + column * block_size - cached_len[owner]
-    rows = jax.vmap(lambda s: lax.dynamic_slice_in_dim(padded, s, block_size, 0))(start)
-    key_pos = column[:, None] * block_size + jnp.arange(block_size, dtype=jnp.int32)[None, :]
-    first_new = cached_len[owner][:, None]
-    fresh = (used[:, None] == 1) & (key_pos >= first_new) & (key_pos < first_new + span)
-    new_k = jnp.where(fresh[..., None], rows[..., :kv_width], key_cache)
-    new_v = jnp.where(fresh[..., None], rows[..., kv_width:], value_cache)
-    return new_k, new_v
+def block_owners(block_table, block_ids):
+    matched = block_table[None, :, :] == block_ids[:, None, None]
+    row_ids = jnp.arange(block_table.shape[0], dtype=jnp.int32)[None, :, None]
+    col_ids = jnp.arange(block_table.shape[1], dtype=jnp.int32)[None, None, :]
+    used = jnp.any(matched, axis=(1, 2)).astype(jnp.int32)
+    owner = jnp.sum(jnp.where(matched, row_ids, 0), axis=(1, 2)).astype(jnp.int32)
+    column = jnp.sum(jnp.where(matched, col_ids, 0), axis=(1, 2)).astype(jnp.int32)
+    return used, owner, column
 
 
 def attention_kernel(
-    used_ref, owner_ref, column_ref, clen_ref, q_ref, k_ref, v_ref, o_ref, m_sc, l_sc, acc_sc,
-    *, q_heads, head_dim
+    used_ref, owner_ref, column_ref, clen_ref, start_ref, q_ref, fresh_ref, kc_ref, vc_ref,
+    o_ref, nk_ref, nv_ref, m_sc, l_sc, acc_sc, *, q_heads, head_dim
 ):
     r = pl.program_id(0)
     i = pl.program_id(1)
     rows = q_ref.shape[0]
-    block_size = k_ref.shape[1]
+    block_size, kv_width = kc_ref.shape[1], kc_ref.shape[2]
+
+    start = start_ref[i]
+    base = pl.multiple_of((start // 8) * 8, 8)
+    window = fresh_ref[pl.ds(base, block_size + 8), :].astype(jnp.bfloat16)
+    pick = lax.broadcasted_iota(jnp.int32, (block_size, block_size + 8), 1) == (
+        lax.broadcasted_iota(jnp.int32, (block_size, block_size + 8), 0) + (start - base)
+    )
+    window = jnp.dot(pick.astype(jnp.bfloat16), window, preferred_element_type=jnp.float32)
+    slot_pos = column_ref[i] * block_size + lax.broadcasted_iota(
+        jnp.int32, (block_size, kv_width), 0
+    )
+    first_new = clen_ref[owner_ref[i]]
+    fresh = (used_ref[i] == 1) & (slot_pos >= first_new) & (slot_pos < first_new + rows)
+    keys = jnp.where(fresh, window[:, :kv_width], kc_ref[0].astype(jnp.float32))
+    values = jnp.where(fresh, window[:, kv_width:], vc_ref[0].astype(jnp.float32))
+    keys = keys.astype(nk_ref.dtype)
+    values = values.astype(nv_ref.dtype)
+    nk_ref[0] = keys
+    nv_ref[0] = values
 
     @pl.when(i == 0)
     def _init():
@@ -74,8 +80,6 @@
 
     @pl.when((used_ref[i] == 1) & (owner_ref[i] == r))
     def _work():
-        keys = k_ref[0]
-        values = v_ref[0]
         query_pos = clen_ref[r] + lax.broadcasted_iota(jnp.int32, (rows, block_size), 0)
         key_pos = column_ref[i] * block_size + lax.broadcasted_iota(
             jnp.int32, (rows, block_size), 1
@@ -112,20 +116,35 @@
         o_ref[:, q_heads * head_dim :] = stats.astype(o_ref.dtype)
 
 
-def local_attention(packed_all, new_k, new_v, used, owner, column, cached_len, span, q_heads, head_dim):
+def local_attention(packed_all, key_cache, value_cache, block_table, cached_len, device, q_heads, head_dim):
     tokens = packed_all.shape[0]
-    nb_dev, block_size, kv_width = new_k.shape
-    requests = tokens // span
-    out_width = (q_heads + 1) * head_dim
+    nb_dev, block_size, kv_width = key_cache.shape
+    requests = cached_len.shape[0]
+    span = tokens // requests
+    q_width = q_heads * head_dim
+    out_width = q_width + head_dim
+    used, owner, column = block_owners(
+        block_table, device * nb_dev + jnp.arange(nb_dev, dtype=jnp.int32)
+    )
+    fresh_rows = jnp.pad(
+        packed_all[:, q_width:].astype(jnp.float32), ((block_size, block_size + 8), (0, 0))
+    )
+    start = block_size + owner * span + column * block_size - cached_len[owner]
+    start = jnp.clip(start, 0, fresh_rows.shape[0] - block_size - 8).astype(jnp.int32)
     grid_spec = pltpu.PrefetchScalarGridSpec(
-        num_scalar_prefetch=4,
+        num_scalar_prefetch=5,
         grid=(requests, nb_dev),
         in_specs=[
-            pl.BlockSpec((span, q_heads * head_dim), lambda r, i, *_: (r, 0)),
+            pl.BlockSpec((span, q_width), lambda r, i, *_: (r, 0)),
+            pl.BlockSpec(fresh_rows.shape, lambda r, i, *_: (0, 0)),
             pl.BlockSpec((1, block_size, kv_width), lambda r, i, *_: (i, 0, 0)),
             pl.BlockSpec((1, block_size, kv_width), lambda r, i, *_: (i, 0, 0)),
         ],
-        out_specs=pl.BlockSpec((span, out_width), lambda r, i, *_: (r, 0)),
+        out_specs=[
+            pl.BlockSpec((span, out_width), lambda r, i, *_: (r, 0)),
+            pl.BlockSpec((1, block_size, kv_width), lambda r, i, *_: (i, 0, 0)),
+            pl.BlockSpec((1, block_size, kv_width), lambda r, i, *_: (i, 0, 0)),
+        ],
         scratch_shapes=[
             pltpu.VMEM((q_heads, span, head_dim), jnp.float32),
             pltpu.VMEM((q_heads, span, head_dim), jnp.float32),
@@ -136,16 +155,20 @@
     return pl.pallas_call(
         functools.partial(attention_kernel, q_heads=q_heads, head_dim=head_dim),
         grid_spec=grid_spec,
-        out_shape=jax.ShapeDtypeStruct((tokens, out_width), jnp.bfloat16),
+        out_shape=(
+            jax.ShapeDtypeStruct((tokens, out_width), jnp.bfloat16),
+            jax.ShapeDtypeStruct(key_cache.shape, key_cache.dtype),
+            jax.ShapeDtypeStruct(value_cache.shape, value_cache.dtype),
+        ),
         compiler_params=pltpu.CompilerParams(
             dimension_semantics=("arbitrary", "arbitrary"), vmem_limit_bytes=48 * 1024 * 1024
         ),
         cost_estimate=pl.CostEstimate(
             flops=flops,
             transcendentals=nb_dev * span * q_heads * block_size,
-            bytes_accessed=tokens * (q_heads * head_dim + out_width) * 2,
+            bytes_accessed=tokens * (q_width + out_width) * 2,
         ),
-    )(used, owner, column, cached_len, packed_all, new_k, new_v)
+    )(used, owner, column, cached_len, start, packed_all, fresh_rows, key_cache, value_cache)
 
 
 def on_device(
@@ -199,16 +222,8 @@
     q_width = q_heads * head_dim
     packed = jnp.concatenate([fresh_queries, fresh_keys, fresh_values], axis=1)
     packed_all = lax.all_gather(packed, "blk", axis=0, tiled=True)
-    first_block = device * nb_dev
-    owner_info = [block_owner(block_table, first_block + b) for b in range(nb_dev)]
-    used = jnp.stack([o[0] for o in owner_info]).astype(jnp.int32)
-    owner = jnp.stack([o[1] for o in owner_info]).astype(jnp.int32)
-    column = jnp.stack([o[2] for o in owner_info]).astype(jnp.int32)
-    new_k, new_v = merge_new_rows(
-        key_cache, value_cache, packed_all[:, q_width:], used, owner, column, cached_len, span
-    )
-    parts = local_attention(
-        packed_all, new_k, new_v, used, owner, column, cached_len, span, q_heads, head_dim
+    parts, new_k, new_v = local_attention(
+        packed_all, key_cache, value_cache, block_table, cached_len, device, q_heads, head_dim
     )
     got = lax.all_to_all(parts, "blk", 0, 0, tiled=True).reshape(n_blk, tok_dev, q_width + 128)
     got = got.astype(jnp.float32)

time: 387 us -> 366 us (0.946)
  local copies, waits for them, and re-layouts: 85 us -> 12.8 us
  waiting for transfers between devices: 73.8 us -> 120 us
  Pallas kernels: 22.8 us -> 42.1 us
  other arithmetic: 23.2 us -> 13.6 us
  blocking collectives: 155 us -> 151 us
    all_gather x1, waiting for transfers between devices: 44.3 us -> 90.9 us  [on_device(): packed_all = lax.all_gather(packed, 'blk', axis=0, tiled=True)]
    another operation x5 -> x0, local copies, waits for them, and re-layouts: 38.3 us -> none  [the longest x2 15.6 us: on_device(): owner = jnp.stack([o[1] for o in owner_info]).astype(jnp.int32)]
    gather x37 -> x1, local copies, waits for them, and re-layouts: 33.7 us -> 0.66 us  [local_attention(): start = block_size + owner * span + column * block_size - cached_len[owner]]
    pallas_call x1, Pallas kernels: 22.8 us -> 42.1 us  [local_attention(): pl.pallas_call(functools.partial(attention_kernel, q_heads=q_heads, head_...]
    reduce_or x12 -> x1, other arithmetic: 8.08 us -> 0.37 us  [block_owners(): used = jnp.any(matched, axis=(1, 2)).astype(jnp.int32)]
  transfers between devices with their start and end apart: 2 -> 2, of which waited for: 2 -> 2; matrix products, arithmetic and copies ran while one was open for 14% -> 1% of each run, Pallas kernels for 0% -> 0%
where the time goes in v2:
time: 366 us; the launch traced here: 362 us
  blocking collectives  151 us (41%)
  waiting for transfers between devices  120 us (33%)
  Pallas kernels  42.1 us (12%)
  between operations  14.2 us (4%)
  other arithmetic  13.6 us (4%)
  local copies, waits for them, and re-layouts  12.8 us (3%)
  matrix products  7.13 us (2%)
    all_to_all x1, blocking collectives, on_device(): lax.all_to_all(parts, 'blk', 0, 0, tiled=True)  151 us
    all_gather x1, waiting for transfers between devices, on_device(): packed_all = lax.all_gather(packed, 'blk', axis=0, tiled=True)  90.9 us
    pallas_call x1, Pallas kernels, local_attention(): pl.pallas_call(functools.partial(attention_kernel, q_heads=q_heads, head_...  42.1 us
    all_gather x1, waiting for transfers between devices, on_device(): whole = lax.all_gather(hidden_in, 'kv', axis=1, tiled=True)  28.8 us
    all_to_all x1, local copies, waits for them, and re-layouts, on_device(): lax.all_to_all(parts, 'blk', 0, 0, tiled=True)  8.66 us
  transfers between devices with their start and end apart: 2, of which 2 were waited for; matrix products, arithmetic and copies ran while one was open for 1% of the time, Pallas kernels for 0%

profile of v2, /device:TPU:1, one launch (start us, length us, event | category | flops | bytes accessed | tf_op | source)
XLA Modules:
  0.0 361.6 jit_solution(7164318818958791801)
XLA Ops:
  7.2 0.7 all-gather.3.cloned.1.call-update
  8.0 0.7 convert_element_type.58
  8.6 0.7 convert_element_type.59
  9.3 0.7 convert_element_type.55
  10.0 0.7 convert_element_type.53
  10.7 0.7 select_reduce_fusion
  11.7 28.8 %all-gather.3.cloned.1.call-done = bf16[128,5120]{1,0:T(8,128)(2,1)} async-done(((bf16[128,640]{1,0:T(8,128)(2,1)}), bf16[128,5120]{1,0:T(8,128)(2,1)}) %all-gather.3.cloned.1.call-update) | async-done | bytes 1310736 | tf_op jit(solution)/shard_map/all_gather | solution.py:200
  40.5 1.6 fusion.1
  42.1 4.6 %convolution_add_fusion = f32[128,640]{1,0:T(8,128)S(1)} fusion(bf16[5120,640]{1,0:T(8,128)(2,1)} %param.14, f32[640]{0:T(1024)S(1)} %convert_element_type.55, bf16[128,5120]{1,0:T(8,128)(2,1)} %all-gather.3.cloned.1.call-done, f32[5120]{0:T(1024)S(1)} %convert_element_type.53, f32[128]{0:T(128)S(1)} %add_rsqrt_fusion), kind=kOutput, calls=%fused_computation.9 | convolution fusion | flops 841564160 | bytes 8215552 | tf_op jit(solution)/shard_map/dot_general | solution.py:204
  46.9 0.6 fusion.4
  48.1 1.9 fusion.5
  50.1 0.8 pad_maximum_fusion
  50.9 0.4 compare_reduce_fusion
  51.3 0.6 fusion.19
  51.9 0.7 gather_fusion
  52.6 90.9 %all-gather.5.cloned.1.call-done.q_ref = bf16[4096,896]{1,0:T(8,128)(2,1)} async-done(((bf16[128,896]{1,0:T(8,128)(2,1)}), bf16[4096,896]{1,0:T(8,128)(2,1)}) %all-gather.5.cloned.1.call-update) | async-done | bytes 7340048 | tf_op jit(solution)/shard_map/all_gather | solution.py:224
  143.5 1.6 slice-done
  145.4 0.6 copy-done.2
  146.2 42.1 %shard_map.139 = (bf16[4096,768]{1,0:T(8,128)(2,1)}, bf16[12,128,128]{2,1,0:T(8,128)(2,1)}, bf16[12,128,128]{2,1,0:T(8,128)(2,1)}) custom-call(s32[12]{0:T(128)S(1)} %convert_element_type.51.used_ref, s32[12]{0:T(128)S(1)} %get-tuple-element.16.owner_ref, s32[12]{0:T(128)S(1)} %get-tuple-element.15.column_ref, s32[4]{0:T(128)S(1)} %copy-done.1, ...), custom_call_target="tpu_custom_call" | custom-call | flops 4026531840 | bytes 11534336 | tf_op jit(solution)/shard_map/pallas_call | solution.py:155
  188.3 8.7 %copy.27 = bf16[32,128,768]{1,2,0:T(8,128)(2,1)} copy(bf16[32,128,768]{2,1,0:T(8,128)(2,1)} %bitcast.22) | data formatting | bytes 12582912 | tf_op jit(solution)/shard_map/all_to_all | solution.py:228
  196.9 151.3 %all_to_all.9 = bf16[32,128,768]{1,2,0:T(8,128)(2,1)} all-to-all(bf16[32,128,768]{1,2,0:T(8,128)(2,1)} %copy.27), channel_id=1, replica_groups=mesh['kv'=8,'blk'=32] {'blk'}, dimensions={0} | all-to-all | bytes 12582912 | tf_op jit(solution)/shard_map/all_to_all | solution.py:228
  348.2 4.3 %convert_element_type.61 = f32[32,128,768]{1,2,0:T(8,128)S(1)} convert(bf16[32,128,768]{1,2,0:T(8,128)(2,1)} %all_to_all.9) | non-fusion elementwise | flops 3145728 | bytes 18874368 | tf_op jit(solution)/shard_map/convert_element_type | solution.py:229
  352.6 1.4 fusion
  354.0 0.8 copy.28
  (34 shorter events, 1.7 us)
Async XLA Ops:
  7.2 39.7 %copy-start = (bf16[5120,128]{1,0:T(8,128)(2,1)S(1)}, bf16[5120,128]{1,0:T(8,128)(2,1)}, u32[]{:S(2)}) copy-start(bf16[5120,128]{1,0:T(8,128)(2,1)} %param.15) | copy-start | bytes 3932164
  7.2 33.3 %all-gather.3.cloned.1.call-start = ((), (), s32[]{:S(2)}) async-start(), calls=%async_computation.1 | async-start | bytes 1474560 | tf_op jit(solution)/shard_map/all_gather | solution.py:200
  7.9 135.6 %all-gather.5.cloned.1.call-start = ((), (), s32[]{:S(2)}) async-start(), calls=%async_computation.2 | async-start | bytes 7569408 | tf_op jit(solution)/shard_map/all_gather | solution.py:224
  42.1 4.8 %copy-start.4 = (bf16[128,5120]{1,0:T(8,128)(2,1)S(1)}, bf16[128,5120]{1,0:T(8,128)(2,1)}, u32[]{:S(2)}) copy-start(bf16[128,5120]{1,0:T(8,128)(2,1)} %all-gather.3.cloned.1.call-done) | copy-start | bytes 3932164
  47.9 3.0 copy-start.5
  47.9 4.0 %copy-start.1 = (s32[4]{0:T(128)S(1)}, s32[4]{0:T(128)}, u32[]{:S(2)}) copy-start(s32[4]{0:T(128)} %clen_ref.1) | copy-start | bytes 52
  143.5 1.6 slice-start
  145.1 1.0 copy-start.2
  145.1 1.1 copy-start.3
Sparse Core Ops, SparseCore 0:
  9.9 30.5 all-gather.2
  51.0 92.4 all-gather.4

commit v3 on v2

--- a/solution.py
+++ b/solution.py
@@ -169,6 +169,69 @@
             bytes_accessed=tokens * (q_width + out_width) * 2,
         ),
     )(used, owner, column, cached_len, start, packed_all, fresh_rows, key_cache, value_cache)
+
+
+MESH = pl.DeviceIdType.MESH
+
+
+def exchange_kernel(src_ref, dst_ref, send_sem, recv_sem, own_sem, *, n, rows, gather):
+    me = lax.axis_index("blk")
+    kv = lax.axis_index("kv")
+    barrier = pltpu.get_barrier_semaphore()
+    for k in range(1, n):
+        peer = lax.rem(me + k, n)
+        pl.semaphore_signal(barrier, inc=1, device_id=(kv, peer), device_id_type=MESH)
+    pl.semaphore_wait(barrier, n - 1)
+
+    def chunk(j):
+        if gather:
+            return src_ref
+        return src_ref.at[pl.ds(pl.multiple_of(j * rows, rows), rows)]
+
+    own = pltpu.make_async_copy(chunk(me), dst_ref.at[me], own_sem)
+    own.start()
+    copies = []
+    for k in range(1, n):
+        peer = lax.rem(me + k, n)
+        copy = pltpu.make_async_remote_copy(
+            src_ref=chunk(peer),
+            dst_ref=dst_ref.at[me],
+            send_sem=send_sem.at[k],
+            recv_sem=recv_sem.at[k],
+            device_id=(kv, peer),
+            device_id_type=MESH,
+        )
+        copy.start()
+        copies.append(copy)
+    own.wait()
+    for k in range(1, n):
+        sender = lax.rem(me + n - k, n)
+        incoming = pltpu.make_async_remote_copy(
+            src_ref=chunk(me),
+            dst_ref=dst_ref.at[sender],
+            send_sem=send_sem.at[k],
+            recv_sem=recv_sem.at[k],
+            device_id=(kv, sender),
+            device_id_type=MESH,
+        )
+        copies[k - 1].wait_send()
+        incoming.wait_recv()
+
+
+def exchange(x, n, gather, collective_id):
+    rows = x.shape[0] if gather else x.shape[0] // n
+    return pl.pallas_call(
+        functools.partial(exchange_kernel, n=n, rows=rows, gather=gather),
+        out_shape=jax.ShapeDtypeStruct((n, rows, x.shape[1]), x.dtype),
+        in_specs=[pl.BlockSpec(memory_space=pl.ANY)],
+        out_specs=pl.BlockSpec(memory_space=pl.ANY),
+        scratch_shapes=[
+            pltpu.SemaphoreType.DMA((n,)),
+            pltpu.SemaphoreType.DMA((n,)),
+            pltpu.SemaphoreType.DMA,
+        ],
+        compiler_params=pltpu.CompilerParams(collective_id=collective_id, has_side_effects=True),
+    )(x)
 
 
 def on_device(
@@ -225,7 +288,7 @@
     parts, new_k, new_v = local_attention(
         packed_all, key_cache, value_cache, block_table, cached_len, device, q_heads, head_dim
     )
-    got = lax.all_to_all(parts, "blk", 0, 0, tiled=True).reshape(n_blk, tok_dev, q_width + 128)
+    got = exchange(parts, n_blk, False, 0)
     got = got.astype(jnp.float32)
     got_w = got[..., :q_width].reshape(n_blk, tok_dev, q_heads, head_dim)
     got_l = got[..., q_width : q_width + group_size]

time: 366 us -> 388 us (1.060)
  Pallas kernels: 42.1 us -> 197 us
  blocking collectives: 151 us -> 0 us
  local copies, waits for them, and re-layouts: 12.8 us -> 24.4 us
  other arithmetic: 13.6 us -> 22.2 us
    pallas_call x0 -> x1, Pallas kernels: none -> 157 us  [exchange(): pl.pallas_call(functools.partial(exchange_kernel, n=n, rows=rows, gather=...]
    all_to_all x1 -> x0, blocking collectives: 151 us -> none  [on_device(): lax.all_to_all(parts, 'blk', 0, 0, tiled=True)]
    mul x0 -> x2, local copies, waits for them, and re-layouts: none -> 15.8 us  [on_device(): mine_weighted = jnp.sum(got_w * scale_d[..., None], axis=0)]
    all_to_all x1 -> x0, local copies, waits for them, and re-layouts: 8.66 us -> none  [on_device(): lax.all_to_all(parts, 'blk', 0, 0, tiled=True)]
    reduce_sum x1, other arithmetic: 1.36 us -> 8.04 us  [on_device(): mine_weighted = jnp.sum(got_w * scale_d[..., None], axis=0)]
where the time goes in v3:
time: 388 us; the launch traced here: 384 us
  Pallas kernels  197 us (51%)
  waiting for transfers between devices  120 us (31%)
  local copies, waits for them, and re-layouts  24.4 us (6%)
  other arithmetic  22.2 us (6%)
  between operations  14.3 us (4%)
  matrix products  5.75 us (1%)
    pallas_call x1, Pallas kernels, exchange(): pl.pallas_call(functools.partial(exchange_kernel, n=n, rows=rows, gather=...  157 us
    all_gather x1, waiting for transfers between devices, on_device(): packed_all = lax.all_gather(packed, 'blk', axis=0, tiled=True)  90.9 us
    pallas_call x1, Pallas kernels, local_attention(): pl.pallas_call(functools.partial(attention_kernel, q_heads=q_heads, head_...  40.1 us
    all_gather x1, waiting for transfers between devices, on_device(): whole = lax.all_gather(hidden_in, 'kv', axis=1, tiled=True)  28.8 us
    mul x2, local copies, waits for them, and re-layouts, on_device(): mine_weighted = jnp.sum(got_w * scale_d[..., None], axis=0)  15.8 us
    reduce_sum x1, other arithmetic, on_device(): mine_weighted = jnp.sum(got_w * scale_d[..., None], axis=0)  8.04 us
  transfers between devices with their start and end apart: 2, of which 2 were waited for; matrix products, arithmetic and copies ran while one was open for 1% of the time, Pallas kernels for 0%

profile of v3, /device:TPU:1, one launch (start us, length us, event | category | flops | bytes accessed | tf_op | source)
XLA Modules:
  0.0 384.0 jit_solution(16329909402483153357)
XLA Ops:
  7.2 0.7 all-gather.3.cloned.1.call-update
  8.0 0.7 convert_element_type.53
  8.7 0.7 convert_element_type.55
  9.4 0.7 convert_element_type.58
  10.0 0.7 convert_element_type.59
  10.7 0.7 select_reduce_fusion
  11.7 28.8 %all-gather.3.cloned.1.call-done = bf16[128,5120]{1,0:T(8,128)(2,1)} async-done(((bf16[128,640]{1,0:T(8,128)(2,1)}), bf16[128,5120]{1,0:T(8,128)(2,1)}) %all-gather.3.cloned.1.call-update) | async-done | bytes 1310736 | tf_op jit(solution)/shard_map/all_gather | solution.py:263
  40.5 1.6 fusion.1
  42.1 4.6 %convolution_add_fusion = f32[128,640]{1,0:T(8,128)S(1)} fusion(bf16[5120,640]{1,0:T(8,128)(2,1)} %param.14, f32[640]{0:T(1024)S(1)} %convert_element_type.55, bf16[128,5120]{1,0:T(8,128)(2,1)} %all-gather.3.cloned.1.call-done, f32[5120]{0:T(1024)S(1)} %convert_element_type.53, f32[128]{0:T(128)S(1)} %add_rsqrt_fusion), kind=kOutput, calls=%fused_computation.13 | convolution fusion | flops 841564160 | bytes 8215552 | tf_op jit(solution)/shard_map/dot_general | solution.py:267
  49.1 0.8 pad_maximum_fusion
  50.5 0.7 gather_fusion
  51.6 90.9 %all-gather.5.cloned.1.call-done.q_ref = bf16[4096,896]{1,0:T(8,128)(2,1)} async-done(((bf16[128,896]{1,0:T(8,128)(2,1)}), bf16[4096,896]{1,0:T(8,128)(2,1)}) %all-gather.5.cloned.1.call-update) | async-done | bytes 7340048 | tf_op jit(solution)/shard_map/all_gather | solution.py:287
  142.5 1.6 slice-done
  144.4 0.6 copy-done.3
  145.2 40.1 %shard_map.139 = (bf16[4096,768]{1,0:T(8,128)(2,1)}, bf16[12,128,128]{2,1,0:T(8,128)(2,1)}, bf16[12,128,128]{2,1,0:T(8,128)(2,1)}) custom-call(s32[12]{0:T(128)S(1)} %convert_element_type.51.used_ref, s32[12]{0:T(128)S(1)} %get-tuple-element.13.owner_ref, s32[12]{0:T(128)S(1)} %get-tuple-element.12.column_ref, s32[4]{0:T(128)S(1)} %copy-done.2, ...), custom_call_target="tpu_custom_call" | custom-call | flops 4026531840 | bytes 11534336 | tf_op jit(solution)/shard_map/pallas_call | solution.py:155
  185.3 156.8 %shard_map.140 = bf16[32,128,768]{2,1,0:T(8,128)(2,1)} custom-call(bf16[4096,768]{1,0:T(8,128)(2,1)} %get-tuple-element.6.src_ref), custom_call_target="tpu_custom_call" | custom-call | tf_op jit(solution)/shard_map/pallas_call | solution.py:223
  342.1 4.4 %convert_element_type.61 = f32[32,128,768]{2,1,0:T(8,128)S(1)} convert(bf16[32,128,768]{2,1,0:T(8,128)(2,1)} %shard_map.140) | non-fusion elementwise | flops 3145728 | bytes 18874368 | tf_op jit(solution)/shard_map/convert_element_type | solution.py:292
  347.1 4.0 %copy-done.5 = f32[32,128,768]{2,1,0:T(8,128)} copy-done((f32[32,128,768]{2,1,0:T(8,128)}, f32[32,128,768]{2,1,0:T(8,128)S(1)}, u32[]{:S(2)}) %copy-start.5) | copy-done | bytes 12582936
  351.1 0.6 fusion.4
  351.7 0.6 copy.36
  352.3 4.5 %mul.160 = f32[32,128,5,128]{1,3,2,0:T(8,128)} broadcast(f32[32,128,5]{1,2,0:T(8,128)S(1)} %copy.36), dimensions={0,1,2} | broadcast | bytes 10567680 | tf_op jit(solution)/shard_map/mul | solution.py:299
  356.8 11.3 %copy.37 = f32[32,128,640]{2,1,0:T(8,128)} copy(f32[32,128,640]{1,2,0:T(8,128)} %bitcast.17) | data formatting | bytes 20971520 | tf_op jit(solution)/shard_map/mul | solution.py:299
  368.1 8.0 %fusion = f32[128,640]{1,0:T(8,128)S(1)} fusion(f32[32,128,640]{2,1,0:T(8,128)} %copy.37, f32[32,128,768]{2,1,0:T(8,128)} %copy-done.5), kind=kLoop, calls=%fused_computation.2 | loop fusion | flops 5160960 | bytes 21299200 | tf_op jit(solution)/shard_map/reduce_sum | solution.py:299
  376.4 0.7 divide_convert_fusion
  (44 shorter events, 5.0 us)
Async XLA Ops:
  7.2 40.0 %copy-start = (bf16[5120,128]{1,0:T(8,128)(2,1)S(1)}, bf16[5120,128]{1,0:T(8,128)(2,1)}, u32[]{:S(2)}) copy-start(bf16[5120,128]{1,0:T(8,128)(2,1)} %param.15) | copy-start | bytes 3932164
  7.2 33.3 %all-gather.3.cloned.1.call-start = ((), (), s32[]{:S(2)}) async-start(), calls=%async_computation | async-start | bytes 1474560 | tf_op jit(solution)/shard_map/all_gather | solution.py:263
  7.9 134.6 %all-gather.5.cloned.1.call-start = ((), (), s32[]{:S(2)}) async-start(), calls=%async_computation.1 | async-start | bytes 7569408 | tf_op jit(solution)/shard_map/all_gather | solution.py:287
  42.1 5.0 %copy-start.6 = (bf16[128,5120]{1,0:T(8,128)(2,1)S(1)}, bf16[128,5120]{1,0:T(8,128)(2,1)}, u32[]{:S(2)}) copy-start(bf16[128,5120]{1,0:T(8,128)(2,1)} %all-gather.3.cloned.1.call-done) | copy-start | bytes 3932164
  47.2 1.3 copy-start.8
  47.8 2.1 copy-start.7
  47.8 2.7 copy-start.2
  142.5 1.6 slice-start
  144.1 1.0 copy-start.3
  144.1 1.1 copy-start.4
  346.5 4.6 %copy-start.5 = (f32[32,128,768]{2,1,0:T(8,128)}, f32[32,128,768]{2,1,0:T(8,128)S(1)}, u32[]{:S(2)}) copy-start(f32[32,128,768]{2,1,0:T(8,128)S(1)} %convert_element_type.61) | copy-start | bytes 37748740
  368.1 9.0 %copy-start.1 = (bf16[5120,128]{1,0:T(8,128)(2,1)S(1)}, bf16[5120,128]{1,0:T(8,128)(2,1)}, u32[]{:S(2)}) copy-start(bf16[5120,128]{1,0:T(8,128)(2,1)} %param.15) | copy-start | bytes 3932164
Sparse Core Ops, SparseCore 0:
  9.9 30.5 all-gather.2
  50.0 92.4 all-gather.4

commit v4 on v2

--- a/solution.py
+++ b/solution.py
@@ -44,15 +44,8 @@
     return used, owner, column
 
 
-def attention_kernel(
-    used_ref, owner_ref, column_ref, clen_ref, start_ref, q_ref, fresh_ref, kc_ref, vc_ref,
-    o_ref, nk_ref, nv_ref, m_sc, l_sc, acc_sc, *, q_heads, head_dim
-):
-    r = pl.program_id(0)
-    i = pl.program_id(1)
-    rows = q_ref.shape[0]
+def merged_block(i, used_ref, owner_ref, column_ref, clen_ref, start_ref, fresh_ref, kc_ref, vc_ref, span):
     block_size, kv_width = kc_ref.shape[1], kc_ref.shape[2]
-
     start = start_ref[i]
     base = pl.multiple_of((start // 8) * 8, 8)
     window = fresh_ref[pl.ds(base, block_size + 8), :].astype(jnp.bfloat16)
@@ -64,13 +57,29 @@
         jnp.int32, (block_size, kv_width), 0
     )
     first_new = clen_ref[owner_ref[i]]
-    fresh = (used_ref[i] == 1) & (slot_pos >= first_new) & (slot_pos < first_new + rows)
+    fresh = (used_ref[i] == 1) & (slot_pos >= first_new) & (slot_pos < first_new + span)
     keys = jnp.where(fresh, window[:, :kv_width], kc_ref[0].astype(jnp.float32))
     values = jnp.where(fresh, window[:, kv_width:], vc_ref[0].astype(jnp.float32))
-    keys = keys.astype(nk_ref.dtype)
-    values = values.astype(nv_ref.dtype)
+    return keys.astype(kc_ref.dtype), values.astype(vc_ref.dtype)
+
+
+def merge_kernel(used_ref, owner_ref, column_ref, clen_ref, start_ref, fresh_ref, kc_ref, vc_ref, nk_ref, nv_ref, *, span):
+    keys, values = merged_block(
+        pl.program_id(0), used_ref, owner_ref, column_ref, clen_ref, start_ref, fresh_ref,
+        kc_ref, vc_ref, span,
+    )
     nk_ref[0] = keys
     nv_ref[0] = values
+
+
+def attention_kernel(
+    used_ref, owner_ref, column_ref, clen_ref, start_ref, req_ref, q_ref, fresh_ref, kc_ref, vc_ref,
+    o_ref, m_sc, l_sc, acc_sc, *, q_heads, head_dim
+):
+    i = pl.program_id(0)
+    r = req_ref[0]
+    rows = q_ref.shape[0]
+    block_size = kc_ref.shape[1]
 
     @pl.when(i == 0)
     def _init():
@@ -80,6 +89,9 @@
 
     @pl.when((used_ref[i] == 1) & (owner_ref[i] == r))
     def _work():
+        keys, values = merged_block(
+            i, used_ref, owner_ref, column_ref, clen_ref, start_ref, fresh_ref, kc_ref, vc_ref, rows
+        )
         query_pos = clen_ref[r] + lax.broadcasted_iota(jnp.int32, (rows, block_size), 0)
         key_pos = column_ref[i] * block_size + lax.broadcasted_iota(
             jnp.int32, (rows, block_size), 1
@@ -101,7 +113,7 @@
             )
             m_sc[g] = new_top
 
-    @pl.when(i == pl.num_programs(1) - 1)
+    @pl.when(i == pl.num_programs(0) - 1)
     def _finish():
         lane = lax.broadcasted_iota(jnp.int32, (rows, head_dim), 1)
         stats = jnp.zeros((rows, head_dim), jnp.float32)
@@ -116,59 +128,148 @@
         o_ref[:, q_heads * head_dim :] = stats.astype(o_ref.dtype)
 
 
-def local_attention(packed_all, key_cache, value_cache, block_table, cached_len, device, q_heads, head_dim):
-    tokens = packed_all.shape[0]
+def block_meta(block_table, block_ids, cached_len, span, block_size, fresh_len):
+    used, owner, column = block_owners(block_table, block_ids)
+    start = block_size + owner * span + column * block_size - cached_len[owner]
+    start = jnp.clip(start, 0, fresh_len - block_size - 8).astype(jnp.int32)
+    return used, owner, column, cached_len, start
+
+
+def merge_local(meta, fresh_rows, key_cache, value_cache, span):
     nb_dev, block_size, kv_width = key_cache.shape
-    requests = cached_len.shape[0]
-    span = tokens // requests
+    block = pl.BlockSpec((1, block_size, kv_width), lambda i, *_: (i, 0, 0))
+    grid_spec = pltpu.PrefetchScalarGridSpec(
+        num_scalar_prefetch=5,
+        grid=(nb_dev,),
+        in_specs=[pl.BlockSpec(fresh_rows.shape, lambda i, *_: (0, 0)), block, block],
+        out_specs=[block, block],
+    )
+    return pl.pallas_call(
+        functools.partial(merge_kernel, span=span),
+        grid_spec=grid_spec,
+        out_shape=(
+            jax.ShapeDtypeStruct(key_cache.shape, key_cache.dtype),
+            jax.ShapeDtypeStruct(value_cache.shape, value_cache.dtype),
+        ),
+        compiler_params=pltpu.CompilerParams(vmem_limit_bytes=32 * 1024 * 1024),
+    )(*meta, fresh_rows, key_cache, value_cache)
+
+
+def attend(packed_all, fresh_rows, keys, values, meta, request, span, q_heads, head_dim):
+    n_blocks, block_size, kv_width = keys.shape
     q_width = q_heads * head_dim
     out_width = q_width + head_dim
-    used, owner, column = block_owners(
-        block_table, device * nb_dev + jnp.arange(nb_dev, dtype=jnp.int32)
-    )
-    fresh_rows = jnp.pad(
-        packed_all[:, q_width:].astype(jnp.float32), ((block_size, block_size + 8), (0, 0))
-    )
-    start = block_size + owner * span + column * block_size - cached_len[owner]
-    start = jnp.clip(start, 0, fresh_rows.shape[0] - block_size - 8).astype(jnp.int32)
+    block = pl.BlockSpec((1, block_size, kv_width), lambda i, *_: (i, 0, 0))
     grid_spec = pltpu.PrefetchScalarGridSpec(
-        num_scalar_prefetch=5,
-        grid=(requests, nb_dev),
+        num_scalar_prefetch=6,
+        grid=(n_blocks,),
         in_specs=[
-            pl.BlockSpec((span, q_width), lambda r, i, *_: (r, 0)),
-            pl.BlockSpec(fresh_rows.shape, lambda r, i, *_: (0, 0)),
-            pl.BlockSpec((1, block_size, kv_width), lambda r, i, *_: (i, 0, 0)),
-            pl.BlockSpec((1, block_size, kv_width), lambda r, i, *_: (i, 0, 0)),
+            pl.BlockSpec((span, q_width), lambda i, *s: (s[5][0], 0)),
+            pl.BlockSpec(fresh_rows.shape, lambda i, *_: (0, 0)),
+            block,
+            block,
         ],
-        out_specs=[
-            pl.BlockSpec((span, out_width), lambda r, i, *_: (r, 0)),
-            pl.BlockSpec((1, block_size, kv_width), lambda r, i, *_: (i, 0, 0)),
-            pl.BlockSpec((1, block_size, kv_width), lambda r, i, *_: (i, 0, 0)),
-        ],
+        out_specs=pl.BlockSpec((span, out_width), lambda i, *_: (0, 0)),
         scratch_shapes=[
             pltpu.VMEM((q_heads, span, head_dim), jnp.float32),
             pltpu.VMEM((q_heads, span, head_dim), jnp.float32),
             pltpu.VMEM((q_heads, span, head_dim), jnp.float32),
         ],
     )
-    flops = 4 * nb_dev * span * q_heads * block_size * head_dim
+    flops = n_blocks * span * q_heads * block_size * head_dim
     return pl.pallas_call(
         functools.partial(attention_kernel, q_heads=q_heads, head_dim=head_dim),
         grid_spec=grid_spec,
-        out_shape=(
-            jax.ShapeDtypeStruct((tokens, out_width), jnp.bfloat16),
-            jax.ShapeDtypeStruct(key_cache.shape, key_cache.dtype),
-            jax.ShapeDtypeStruct(value_cache.shape, value_cache.dtype),
-        ),
-        compiler_params=pltpu.CompilerParams(
-            dimension_semantics=("arbitrary", "arbitrary"), vmem_limit_bytes=48 * 1024 * 1024
-        ),
+        out_shape=jax.ShapeDtypeStruct((span, out_width), jnp.bfloat16),
+        compiler_params=pltpu.CompilerParams(vmem_limit_bytes=48 * 1024 * 1024),
         cost_estimate=pl.CostEstimate(
             flops=flops,
-            transcendentals=nb_dev * span * q_heads * block_size,
-            bytes_accessed=tokens * (q_width + out_width) * 2,
+            transcendentals=n_blocks * span * q_heads * block_size // 4,
+            bytes_accessed=span * (q_width + out_width) * 2 + n_blocks * block_size * kv_width * 4,
         ),
-    )(used, owner, column, cached_len, start, packed_all, fresh_rows, key_cache, value_cache)
+    )(*meta, request, packed_all, fresh_rows, keys, values)
+
+
+MESH = pl.DeviceIdType.MESH
+
+
+def group_exchange_kernel(*refs, m, stride, gather, n_arr):
+    srcs, dsts = refs[:n_arr], refs[n_arr : 2 * n_arr]
+    send_sem, recv_sem, own_sem = refs[2 * n_arr :]
+    me = lax.axis_index("blk")
+    kv = lax.axis_index("kv")
+    pos = lax.rem(me // stride, m)
+    base = me - pos * stride
+
+    def member(j):
+        return base + j * stride
+
+    barrier = pltpu.get_barrier_semaphore()
+    for k in range(1, m):
+        peer = member(lax.rem(pos + k, m))
+        pl.semaphore_signal(barrier, inc=1, device_id=(kv, peer), device_id_type=MESH)
+    pl.semaphore_wait(barrier, m - 1)
+
+    def chunk(src, j):
+        if gather:
+            return src
+        rows = src.shape[0] // m
+        return src.at[pl.ds(pl.multiple_of(j * rows, rows), rows)]
+
+    owns = []
+    for a in range(n_arr):
+        own = pltpu.make_async_copy(chunk(srcs[a], pos), dsts[a].at[pos], own_sem.at[a])
+        own.start()
+        owns.append(own)
+    copies = []
+    for k in range(1, m):
+        peer_pos = lax.rem(pos + k, m)
+        for a in range(n_arr):
+            copy = pltpu.make_async_remote_copy(
+                src_ref=chunk(srcs[a], peer_pos),
+                dst_ref=dsts[a].at[pos],
+                send_sem=send_sem.at[k * n_arr + a],
+                recv_sem=recv_sem.at[k * n_arr + a],
+                device_id=(kv, member(peer_pos)),
+                device_id_type=MESH,
+            )
+            copy.start()
+            copies.append(copy)
+    for own in owns:
+        own.wait()
+    for k in range(1, m):
+        sender_pos = lax.rem(pos + m - k, m)
+        for a in range(n_arr):
+            incoming = pltpu.make_async_remote_copy(
+                src_ref=chunk(srcs[a], pos),
+                dst_ref=dsts[a].at[sender_pos],
+                send_sem=send_sem.at[k * n_arr + a],
+                recv_sem=recv_sem.at[k * n_arr + a],
+                device_id=(kv, member(sender_pos)),
+                device_id_type=MESH,
+            )
+            copies[(k - 1) * n_arr + a].wait_send()
+            incoming.wait_recv()
+
+
+def group_exchange(arrays, m, stride, gather, collective_id):
+    n_arr = len(arrays)
+    shapes = []
+    for x in arrays:
+        rows = x.shape[0] if gather else x.shape[0] // m
+        shapes.append(jax.ShapeDtypeStruct((m, rows) + x.shape[1:], x.dtype))
+    return pl.pallas_call(
+        functools.partial(group_exchange_kernel, m=m, stride=stride, gather=gather, n_arr=n_arr),
+        out_shape=tuple(shapes),
+        in_specs=[pl.BlockSpec(memory_space=pl.ANY)] * n_arr,
+        out_specs=tuple([pl.BlockSpec(memory_space=pl.ANY)] * n_arr),
+        scratch_shapes=[
+            pltpu.SemaphoreType.DMA((m * n_arr,)),
+            pltpu.SemaphoreType.DMA((m * n_arr,)),
+            pltpu.SemaphoreType.DMA((n_arr,)),
+        ],
+        compiler_params=pltpu.CompilerParams(collective_id=collective_id, has_side_effects=True),
+    )(*arrays)
 
 
 def on_device(
@@ -222,12 +323,34 @@
     q_width = q_heads * head_dim
     packed = jnp.concatenate([fresh_queries, fresh_keys, fresh_values], axis=1)
     packed_all = lax.all_gather(packed, "blk", axis=0, tiled=True)
-    parts, new_k, new_v = local_attention(
-        packed_all, key_cache, value_cache, block_table, cached_len, device, q_heads, head_dim
-    )
-    got = lax.all_to_all(parts, "blk", 0, 0, tiled=True).reshape(n_blk, tok_dev, q_width + 128)
+    ring = span // tok_dev
+    cols = n_blk // ring
+    position = device % ring
+    col_keys, col_values = group_exchange([key_cache, value_cache], cols, ring, True, 0)
+    fresh_rows = jnp.pad(
+        packed_all[:, q_width:].astype(jnp.float32), ((block_size, block_size + 8), (0, 0))
+    )
+    local_ids = device * nb_dev + jnp.arange(nb_dev, dtype=jnp.int32)
+    meta = block_meta(block_table, local_ids, cached_len, span, block_size, fresh_rows.shape[0])
+    new_k, new_v = merge_local(meta, fresh_rows, key_cache, value_cache, span)
+    holders = jnp.arange(cols, dtype=jnp.int32) * ring + position
+    col_ids = (holders[:, None] * nb_dev + jnp.arange(nb_dev, dtype=jnp.int32)[None, :]).reshape(-1)
+    meta = block_meta(block_table, col_ids, cached_len, span, block_size, fresh_rows.shape[0])
+    request = (device // ring).reshape(1).astype(jnp.int32)
+    parts = attend(
+        packed_all,
+        fresh_rows,
+        col_keys.reshape(cols * nb_dev, block_size, kv_width),
+        col_values.reshape(cols * nb_dev, block_size, kv_width),
+        meta,
+        request,
+        span,
+        q_heads,
+        head_dim,
+    )
+    (got,) = group_exchange([parts], ring, 1, False, 1)
     got = got.astype(jnp.float32)
-    got_w = got[..., :q_width].reshape(n_blk, tok_dev, q_heads, head_dim)
+    got_w = got[..., :q_width].reshape(ring, tok_dev, q_heads, head_dim)
     got_l = got[..., q_width : q_width + group_size]
     got_m = got[..., q_width + group_size : q_width + 2 * group_size]
     best = jnp.max(got_m, axis=0)

time: 366 us -> 256 us (0.70)
  the two profiles are of different devices: /device:TPU:1 before, /device:TPU:70 now
where the time goes in v4:
time: 256 us; the launch traced here: 255 us
  Pallas kernels  119 us (46%)
  waiting for transfers between devices  82.9 us (32%)
  other arithmetic  18.8 us (7%)
  local copies, waits for them, and re-layouts  14.8 us (6%)
  between operations  14.3 us (6%)
  matrix products  5.85 us (2%)
    pallas_call x2, Pallas kernels, group_exchange(): pl.pallas_call(functools.partial(group_exchange_kernel, m=m, stride=strid...  93.9 us
    all_gather x1, waiting for transfers between devices, on_device(): packed_all = lax.all_gather(packed, 'blk', axis=0, tiled=True)  55.5 us
    all_gather x1, waiting for transfers between devices, on_device(): whole = lax.all_gather(hidden_in, 'kv', axis=1, tiled=True)  26.8 us
    pallas_call x1, Pallas kernels, attend(): pl.pallas_call(functools.partial(attention_kernel, q_heads=q_heads, head_...  19.2 us
    unnamed x24, local copies, waits for them, and re-layouts  6 us
    pallas_call x1, Pallas kernels, merge_local(): pl.pallas_call(functools.partial(merge_kernel, span=span), grid_spec=grid...  5.5 us
  transfers between devices with their start and end apart: 2, of which 2 were waited for; matrix products, arithmetic and copies ran while one was open for 4% of the time, Pallas kernels for 17%

profile of v4, /device:TPU:70, one launch (start us, length us, event | category | flops | bytes accessed | tf_op | source)
XLA Modules:
  0.0 255.3 jit_solution(3683724313122759512)
XLA Ops:
  8.0 0.7 convert_element_type.56
  8.7 0.7 convert_element_type.58
  10.7 0.7 select_reduce_fusion
  11.7 26.8 %all-gather.3.cloned.1.call-done = bf16[128,5120]{1,0:T(8,128)(2,1)} async-done(((bf16[128,640]{1,0:T(8,128)(2,1)}), bf16[128,5120]{1,0:T(8,128)(2,1)}) %all-gather.3.cloned.1.call-update) | async-done | bytes 1310736 | tf_op jit(solution)/shard_map/all_gather | solution.py:301
  38.4 1.6 fusion
  40.1 4.6 %convolution_add_fusion = f32[128,640]{1,0:T(8,128)S(1)} fusion(bf16[5120,640]{1,0:T(8,128)(2,1)} %param.14, f32[640]{0:T(1024)S(1)} %convert_element_type.58, bf16[128,5120]{1,0:T(8,128)(2,1)} %all-gather.3.cloned.1.call-done, f32[5120]{0:T(1024)S(1)} %convert_element_type.56, f32[128]{0:T(128)S(1)} %add_rsqrt_fusion), kind=kOutput, calls=%fused_computation.9 | convolution fusion | flops 841564160 | bytes 8215552 | tf_op jit(solution)/shard_map/dot_general | solution.py:305
  47.1 0.8 pad_maximum_fusion
  49.9 42.4 %shard_map.139 = (bf16[4,12,128,128]{3,2,1,0:T(8,128)(2,1)}, bf16[4,12,128,128]{3,2,1,0:T(8,128)(2,1)}) custom-call(bf16[12,128,128]{2,1,0:T(8,128)(2,1)} %kc_ref.1, bf16[12,128,128]{2,1,0:T(8,128)(2,1)} %vc_ref.1), custom_call_target="tpu_custom_call" | custom-call | tf_op jit(solution)/shard_map/pallas_call | solution.py:261
  93.3 2.6 %fusion.25.start_ref = s32[48]{0:T(128)S(1)} fusion(s32[48]{0:T(128)S(1)} %get-tuple-element.17.owner_ref, s32[48]{0:T(128)S(1)} %get-tuple-element.16.column_ref, s32[]{:T(128)} %bitcast.1, s32[]{:T(128)} %bitcast.2, s32[]{:T(128)} %bitcast.4, s32[]{:T(128)} %bitcast.3), kind=kLoop, calls=%fused_computation.71 | loop fusion | flops 720 | bytes 592 | tf_op jit(solution)/shard_map/jit(clip)/min | solution.py:134
  95.8 55.5 %all-gather.5.cloned.1.call-done.q_ref = bf16[4096,896]{1,0:T(8,128)(2,1)} async-done(((bf16[128,896]{1,0:T(8,128)(2,1)}), bf16[4096,896]{1,0:T(8,128)(2,1)}) %all-gather.5.cloned.1.call-update) | async-done | bytes 7340048 | tf_op jit(solution)/shard_map/all_gather | solution.py:325
  151.3 1.6 slice-done
  152.9 2.5 pad_convert_fusion.fresh_ref
  155.4 0.8 copy-done.5
  156.2 19.2 %shard_map.140.refs_0_ = bf16[1024,768]{1,0:T(8,128)(2,1)S(1)} custom-call(s32[48]{0:T(128)S(1)} %convert_element_type.54.used_ref, s32[48]{0:T(128)S(1)} %get-tuple-element.17.owner_ref, s32[48]{0:T(128)S(1)} %get-tuple-element.16.column_ref, s32[4]{0:T(128)S(1)} %copy-done.1, s32[48]{0:T(128)S(1)} %fusion.25.start_ref, s32[1]{0:T(128)} %bitcast.6.req_ref, ...), custom_call_target="tpu_custom_call" | custom-call | flops 4026531840 | bytes 6029312 | tf_op jit(solution)/shard_map/pallas_call | solution.py:180
  175.4 1.1 copy-done.3
  176.6 51.4 %shard_map.141 = bf16[8,128,768]{2,1,0:T(8,128)(2,1)} custom-call(bf16[1024,768]{1,0:T(8,128)(2,1)} %copy-done.3), custom_call_target="tpu_custom_call" | custom-call | tf_op jit(solution)/shard_map/pallas_call | solution.py:261
  228.0 1.7 convert_element_type.64
  229.9 1.4 copy-done.8
  231.8 1.8 mul.186
  233.6 3.3 %copy.37 = f32[8,128,640]{2,1,0:T(8,128)} copy(f32[8,128,640]{1,2,0:T(8,128)} %bitcast.36) | data formatting | bytes 5242880 | tf_op jit(solution)/shard_map/mul | solution.py:359
  236.8 2.9 %fusion.3 = f32[128,640]{1,0:T(8,128)S(1)} fusion(f32[8,128,640]{2,1,0:T(8,128)} %copy.37, f32[8,128,768]{2,1,0:T(8,128)} %copy-done.8), kind=kLoop, calls=%fused_computation.7 | loop fusion | flops 1228800 | bytes 5570560 | tf_op jit(solution)/shard_map/reduce_sum | solution.py:359
  240.0 0.7 divide_convert_fusion
  240.7 2.3 copy-done.2
  243.0 5.5 %shard_map.142 = (bf16[12,128,128]{2,1,0:T(8,128)(2,1)}, bf16[12,128,128]{2,1,0:T(8,128)(2,1)}) custom-call(s32[12]{0:T(128)S(1)} %convert_element_type.66.used_ref, s32[12]{0:T(128)S(1)} %get-tuple-element.15.owner_ref, s32[12]{0:T(128)S(1)} %get-tuple-element.14.column_ref, s32[4]{0:T(128)S(1)} %copy-done.1, s32[12]{0:T(128)S(1)} %subtract_clamp_fusion.start_ref, ...), custom_call_target="tpu_custom_call" | custom-call | tf_op jit(solution)/shard_map/pallas_call | solution.py:147
  (60 shorter events, 8.4 us)
Async XLA Ops:
  7.2 37.9 %copy-start = (bf16[5120,128]{1,0:T(8,128)(2,1)S(1)}, bf16[5120,128]{1,0:T(8,128)(2,1)}, u32[]{:S(2)}) copy-start(bf16[5120,128]{1,0:T(8,128)(2,1)} %param.15) | copy-start | bytes 3932164
  7.2 31.2 %all-gather.3.cloned.1.call-start = ((), (), s32[]{:S(2)}) async-start(), calls=%async_computation | async-start | bytes 1474560 | tf_op jit(solution)/shard_map/all_gather | solution.py:301
  7.9 143.4 %all-gather.5.cloned.1.call-start = ((), (), s32[]{:S(2)}) async-start(), calls=%async_computation.1 | async-start | bytes 7569408 | tf_op jit(solution)/shard_map/all_gather | solution.py:325
  40.1 5.0 %copy-start.9 = (bf16[128,5120]{1,0:T(8,128)(2,1)S(1)}, bf16[128,5120]{1,0:T(8,128)(2,1)}, u32[]{:S(2)}) copy-start(bf16[128,5120]{1,0:T(8,128)(2,1)} %all-gather.3.cloned.1.call-done) | copy-start | bytes 3932164
  45.1 1.3 copy-start.11
  45.8 2.3 copy-start.10
  45.8 3.1 %copy-start.1 = (s32[4]{0:T(128)S(1)}, s32[4]{0:T(128)}, u32[]{:S(2)}) copy-start(s32[4]{0:T(128)} %clen_ref.3) | copy-start | bytes 52
  151.3 1.6 slice-start
  152.9 2.5 copy-start.4
  152.9 3.3 %copy-start.5 = (bf16[4,12,128,128]{3,2,1,0:T(8,128)(2,1)S(1)}, bf16[4,12,128,128]{3,2,1,0:T(8,128)(2,1)}, u32[]{:S(2)}) copy-start(bf16[4,12,128,128]{3,2,1,0:T(8,128)(2,1)} %get-tuple-element.8) | copy-start | bytes 4718596
  175.4 1.2 copy-start.3
  229.7 1.7 copy-start.8
  236.8 3.9 %copy-start.6 = (bf16[12,128,128]{2,1,0:T(8,128)(2,1)S(1)}, bf16[12,128,128]{2,1,0:T(8,128)(2,1)}, u32[]{:S(2)}) copy-start(bf16[12,128,128]{2,1,0:T(8,128)(2,1)} %kc_ref.1) | copy-start | bytes 1179652
  236.8 3.9 %copy-start.7 = (bf16[12,128,128]{2,1,0:T(8,128)(2,1)S(1)}, bf16[12,128,128]{2,1,0:T(8,128)(2,1)}, u32[]{:S(2)}) copy-start(bf16[12,128,128]{2,1,0:T(8,128)(2,1)} %vc_ref.1) | copy-start | bytes 1179652
  240.7 2.3 copy-start.2
Sparse Core Ops, SparseCore 0:
  9.9 28.5 all-gather.2
  48.0 103.2 all-gather.4

commit v5 on v4

--- a/solution.py
+++ b/solution.py
@@ -155,7 +155,7 @@
     )(*meta, fresh_rows, key_cache, value_cache)
 
 
-def attend(packed_all, fresh_rows, keys, values, meta, request, span, q_heads, head_dim):
+def attend(queries, fresh_rows, keys, values, meta, request, span, q_heads, head_dim):
     n_blocks, block_size, kv_width = keys.shape
     q_width = q_heads * head_dim
     out_width = q_width + head_dim
@@ -164,7 +164,7 @@
         num_scalar_prefetch=6,
         grid=(n_blocks,),
         in_specs=[
-            pl.BlockSpec((span, q_width), lambda i, *s: (s[5][0], 0)),
+            pl.BlockSpec((span, q_width), lambda i, *_: (0, 0)),
             pl.BlockSpec(fresh_rows.shape, lambda i, *_: (0, 0)),
             block,
             block,
@@ -187,7 +187,7 @@
             transcendentals=n_blocks * span * q_heads * block_size // 4,
             bytes_accessed=span * (q_width + out_width) * 2 + n_blocks * block_size * kv_width * 4,
         ),
-    )(*meta, request, packed_all, fresh_rows, keys, values)
+    )(*meta, request, queries, fresh_rows, keys, values)
 
 
 MESH = pl.DeviceIdType.MESH
@@ -321,15 +321,14 @@
     fresh_keys = fresh_keys.astype(jnp.bfloat16).reshape(tok_dev, kv_width)
     fresh_values = (value_linear + value_bias.astype(jnp.float32)[None, :]).astype(jnp.bfloat16)
     q_width = q_heads * head_dim
-    packed = jnp.concatenate([fresh_queries, fresh_keys, fresh_values], axis=1)
-    packed_all = lax.all_gather(packed, "blk", axis=0, tiled=True)
+    packed = jnp.concatenate([fresh_keys, fresh_values], axis=1)
+    kv_all = lax.all_gather(packed, "blk", axis=0, tiled=True)
     ring = span // tok_dev
     cols = n_blk // ring
     position = device % ring
     col_keys, col_values = group_exchange([key_cache, value_cache], cols, ring, True, 0)
-    fresh_rows = jnp.pad(
-        packed_all[:, q_width:].astype(jnp.float32), ((block_size, block_size + 8), (0, 0))
-    )
+    (ring_queries,) = group_exchange([fresh_queries], ring, 1, True, 2)
+    fresh_rows = jnp.pad(kv_all.astype(jnp.float32), ((block_size, block_size + 8), (0, 0)))
     local_ids = device * nb_dev + jnp.arange(nb_dev, dtype=jnp.int32)
     meta = block_meta(block_table, local_ids, cached_len, span, block_size, fresh_rows.shape[0])
     new_k, new_v = merge_local(meta, fresh_rows, key_cache, value_cache, span)
@@ -338,7 +337,7 @@
     meta = block_meta(block_table, col_ids, cached_len, span, block_size, fresh_rows.shape[0])
     request = (device // ring).reshape(1).astype(jnp.int32)
     parts = attend(
-        packed_all,
+        ring_queries.reshape(span, q_width),
         fresh_rows,
         col_keys.reshape(cols * nb_dev, block_size, kv_width),
         col_values.reshape(cols * nb_dev, block_size, kv_width),

time: 256 us -> 250 us (0.977)
  the two profiles are of different devices: /device:TPU:70 before, /device:TPU:1 now
where the time goes in v5:
time: 250 us; the launch traced here: 245 us
  Pallas kernels  157 us (63%)
  waiting for transfers between devices  34.5 us (14%)
  other arithmetic  19.7 us (8%)
  between operations  14.4 us (6%)
  local copies, waits for them, and re-layouts  12.7 us (5%)
  matrix products  6.69 us (3%)
    pallas_call x3, Pallas kernels, group_exchange(): pl.pallas_call(functools.partial(group_exchange_kernel, m=m, stride=strid...  132 us
    all_gather x1, waiting for transfers between devices, on_device(): whole = lax.all_gather(hidden_in, 'kv', axis=1, tiled=True)  29.7 us
    pallas_call x1, Pallas kernels, attend(): pl.pallas_call(functools.partial(attention_kernel, q_heads=q_heads, head_...  19 us
    pallas_call x1, Pallas kernels, merge_local(): pl.pallas_call(functools.partial(merge_kernel, span=span), grid_spec=grid...  5.5 us
  transfers between devices with their start and end apart: 2, of which 2 were waited for; matrix products, arithmetic and copies ran while one was open for 6% of the time, Pallas kernels for 34%

profile of v5, /device:TPU:1, one launch (start us, length us, event | category | flops | bytes accessed | tf_op | source)
XLA Modules:
  0.0 244.8 jit_solution(7840794745203163924)
XLA Ops:
  9.3 0.7 convert_element_type.56
  10.0 0.7 select_reduce_fusion
  10.8 29.7 %all-gather.3.cloned.1.call-done = bf16[128,5120]{1,0:T(8,128)(2,1)} async-done(((bf16[128,640]{1,0:T(8,128)(2,1)}), bf16[128,5120]{1,0:T(8,128)(2,1)}) %all-gather.3.cloned.1.call-update) | async-done | bytes 1310736 | tf_op jit(solution)/shard_map/all_gather | solution.py:301
  40.5 1.8 fusion
  42.3 1.9 fusion.4
  45.2 0.7 pad_maximum_fusion.1
  48.1 39.6 %shard_map.140 = (bf16[4,12,128,128]{3,2,1,0:T(8,128)(2,1)}, bf16[4,12,128,128]{3,2,1,0:T(8,128)(2,1)}) custom-call(bf16[12,128,128]{2,1,0:T(8,128)(2,1)} %kc_ref.1, bf16[12,128,128]{2,1,0:T(8,128)(2,1)} %vc_ref.1), custom_call_target="tpu_custom_call" | custom-call | tf_op jit(solution)/shard_map/pallas_call | solution.py:261
  88.5 2.5 %fusion.25.start_ref = s32[48]{0:T(128)S(1)} fusion(s32[48]{0:T(128)S(1)} %get-tuple-element.17.owner_ref, s32[48]{0:T(128)S(1)} %get-tuple-element.16.column_ref, s32[]{:T(128)} %bitcast.1, s32[]{:T(128)} %bitcast.2, s32[]{:T(128)} %bitcast.4, s32[]{:T(128)} %bitcast.3), kind=kLoop, calls=%fused_computation.71 | loop fusion | flops 720 | bytes 592 | tf_op jit(solution)/shard_map/jit(clip)/min | solution.py:134
  91.2 4.1 %convolution_add_fusion = f32[128,640]{1,0:T(8,128)S(1)} fusion(bf16[5120,640]{1,0:T(8,128)(2,1)} %param.14, f32[640]{0:T(1024)S(1)} %convert_element_type.58, bf16[128,5120]{1,0:T(8,128)(2,1)S(1)} %copy-done.10, f32[5120]{0:T(1024)S(1)} %convert_element_type.56, f32[128]{0:T(128)S(1)} %add_rsqrt_fusion), kind=kOutput, calls=%fused_computation.9 | convolution fusion | flops 841564160 | bytes 8215552 | tf_op jit(solution)/shard_map/dot_general | solution.py:305
  95.6 0.8 copy.33.refs_0_
  96.4 43.0 %shard_map.139 = bf16[8,128,640]{2,1,0:T(8,128)(2,1)} custom-call(bf16[128,640]{1,0:T(8,128)(2,1)} %copy.33.refs_0_), custom_call_target="tpu_custom_call" | custom-call | tf_op jit(solution)/shard_map/pallas_call | solution.py:261
  139.4 4.1 %all-gather.5.cloned.1.call-done = bf16[4096,256]{1,0:T(8,128)(2,1)} async-done(((bf16[128,256]{1,0:T(8,128)(2,1)}), bf16[4096,256]{1,0:T(8,128)(2,1)}) %all-gather.5.cloned.1.call-update) | async-done | bytes 2097168 | tf_op jit(solution)/shard_map/all_gather | solution.py:325
  143.5 4.1 %pad_convert_fusion.fresh_ref = f32[4360,256]{1,0:T(8,128)} fusion(bf16[4096,256]{1,0:T(8,128)(2,1)} %all-gather.5.cloned.1.call-done), kind=kLoop, calls=%fused_computation.8 | loop fusion | flops 1116160 | bytes 6561792 | tf_op jit(solution)/shard_map/jit(_pad)/pad | solution.py:331
  147.7 19.0 %shard_map.141.refs_0_ = bf16[1024,768]{1,0:T(8,128)(2,1)S(1)} custom-call(s32[48]{0:T(128)S(1)} %convert_element_type.54.used_ref, s32[48]{0:T(128)S(1)} %get-tuple-element.17.owner_ref, s32[48]{0:T(128)S(1)} %get-tuple-element.16.column_ref, s32[4]{0:T(128)S(1)} %copy-done.1, s32[48]{0:T(128)S(1)} %fusion.25.start_ref, s32[1]{0:T(128)} %bitcast.6.req_ref, ...), custom_call_target="tpu_custom_call" | custom-call | flops 4026531840 | bytes 6029312 | tf_op jit(solution)/shard_map/pallas_call | solution.py:180
  166.7 1.2 copy-done.3
  167.9 49.6 %shard_map.142 = bf16[8,128,768]{2,1,0:T(8,128)(2,1)} custom-call(bf16[1024,768]{1,0:T(8,128)(2,1)} %copy-done.3), custom_call_target="tpu_custom_call" | custom-call | tf_op jit(solution)/shard_map/pallas_call | solution.py:261
  217.5 1.7 convert_element_type.64
  219.4 1.5 copy-done.9
  221.6 1.7 mul.186
  223.3 3.3 %copy.37 = f32[8,128,640]{2,1,0:T(8,128)} copy(f32[8,128,640]{1,2,0:T(8,128)} %bitcast.38) | data formatting | bytes 5242880 | tf_op jit(solution)/shard_map/mul | solution.py:358
  226.5 2.9 %fusion.3 = f32[128,640]{1,0:T(8,128)S(1)} fusion(f32[8,128,640]{2,1,0:T(8,128)} %copy.37, f32[8,128,768]{2,1,0:T(8,128)} %copy-done.9), kind=kLoop, calls=%fused_computation.7 | loop fusion | flops 1228800 | bytes 5570560 | tf_op jit(solution)/shard_map/reduce_sum | solution.py:358
  229.4 2.3 copy-done.2
  231.7 5.5 %shard_map.143 = (bf16[12,128,128]{2,1,0:T(8,128)(2,1)}, bf16[12,128,128]{2,1,0:T(8,128)(2,1)}) custom-call(s32[12]{0:T(128)S(1)} %convert_element_type.66.used_ref, s32[12]{0:T(128)S(1)} %get-tuple-element.15.owner_ref, s32[12]{0:T(128)S(1)} %get-tuple-element.14.column_ref, s32[4]{0:T(128)S(1)} %copy-done.1, s32[12]{0:T(128)S(1)} %subtract_clamp_fusion.start_ref, ...), custom_call_target="tpu_custom_call" | custom-call | tf_op jit(solution)/shard_map/pallas_call | solution.py:147
  237.2 0.7 divide_convert_fusion
  (63 shorter events, 7.3 us)
Async XLA Ops:
  7.2 35.1 %copy-start = (bf16[5120,128]{1,0:T(8,128)(2,1)S(1)}, bf16[5120,128]{1,0:T(8,128)(2,1)}, u32[]{:S(2)}) copy-start(bf16[5120,128]{1,0:T(8,128)(2,1)} %param.15) | copy-start | bytes 3932164
  7.2 33.3 %all-gather.3.cloned.1.call-start = ((), (), s32[]{:S(2)}) async-start(), calls=%async_computation | async-start | bytes 1474560 | tf_op jit(solution)/shard_map/all_gather | solution.py:301
  7.9 135.6 %all-gather.5.cloned.1.call-start = ((), (), s32[]{:S(2)}) async-start(), calls=%async_computation.1 | async-start | bytes 2162688 | tf_op jit(solution)/shard_map/all_gather | solution.py:325
  40.5 4.1 %copy-start.10 = (bf16[128,5120]{1,0:T(8,128)(2,1)S(1)}, bf16[128,5120]{1,0:T(8,128)(2,1)}, u32[]{:S(2)}) copy-start(bf16[128,5120]{1,0:T(8,128)(2,1)} %all-gather.3.cloned.1.call-done) | copy-start | bytes 3932164
  40.5 4.1 %copy-start.13 = (bf16[5120,128]{1,0:T(8,128)(2,1)S(1)}, bf16[5120,128]{1,0:T(8,128)(2,1)}, u32[]{:S(2)}) copy-start(bf16[5120,128]{1,0:T(8,128)(2,1)} %param.16) | copy-start | bytes 3932164
  44.2 1.8 copy-start.11
  44.2 3.2 %copy-start.1 = (s32[4]{0:T(128)S(1)}, s32[4]{0:T(128)}, u32[]{:S(2)}) copy-start(s32[4]{0:T(128)} %clen_ref.3) | copy-start | bytes 52
  44.2 3.8 %copy-start.12 = (bf16[640]{0:T(1024)(128)(2,1)S(1)}, bf16[640]{0:T(1024)(128)(2,1)}, u32[]{:S(2)}) copy-start(bf16[640]{0:T(1024)(128)(2,1)} %param.17) | copy-start | bytes 3844
  139.4 8.3 %copy-start.6 = (bf16[8,128,640]{2,1,0:T(8,128)(2,1)S(1)}, bf16[8,128,640]{2,1,0:T(8,128)(2,1)}, u32[]{:S(2)}) copy-start(bf16[8,128,640]{2,1,0:T(8,128)(2,1)} %shard_map.139) | copy-start | bytes 3932164
  143.5 4.1 %copy-start.7 = (bf16[4,12,128,128]{3,2,1,0:T(8,128)(2,1)S(1)}, bf16[4,12,128,128]{3,2,1,0:T(8,128)(2,1)}, u32[]{:S(2)}) copy-start(bf16[4,12,128,128]{3,2,1,0:T(8,128)(2,1)} %get-tuple-element.7) | copy-start | bytes 4718596
  143.5 4.1 %copy-start.8 = (bf16[4,12,128,128]{3,2,1,0:T(8,128)(2,1)S(1)}, bf16[4,12,128,128]{3,2,1,0:T(8,128)(2,1)}, u32[]{:S(2)}) copy-start(bf16[4,12,128,128]{3,2,1,0:T(8,128)(2,1)} %get-tuple-element.8) | copy-start | bytes 4718596
  166.7 1.2 copy-start.3
  219.2 1.7 copy-start.9
  226.5 2.9 %copy-start.4 = (bf16[12,128,128]{2,1,0:T(8,128)(2,1)S(1)}, bf16[12,128,128]{2,1,0:T(8,128)(2,1)}, u32[]{:S(2)}) copy-start(bf16[12,128,128]{2,1,0:T(8,128)(2,1)} %kc_ref.1) | copy-start | bytes 1179652
  226.5 2.9 %copy-start.5 = (bf16[12,128,128]{2,1,0:T(8,128)(2,1)S(1)}, bf16[12,128,128]{2,1,0:T(8,128)(2,1)}, u32[]{:S(2)}) copy-start(bf16[12,128,128]{2,1,0:T(8,128)(2,1)} %vc_ref.1) | copy-start | bytes 1179652
  229.4 2.3 copy-start.2
Sparse Core Ops, SparseCore 0:
  9.9 30.5 all-gather.2
  46.1 97.4 all-gather.4

commit v6 on v5

--- a/solution.py
+++ b/solution.py
@@ -63,18 +63,9 @@
     return keys.astype(kc_ref.dtype), values.astype(vc_ref.dtype)
 
 
-def merge_kernel(used_ref, owner_ref, column_ref, clen_ref, start_ref, fresh_ref, kc_ref, vc_ref, nk_ref, nv_ref, *, span):
-    keys, values = merged_block(
-        pl.program_id(0), used_ref, owner_ref, column_ref, clen_ref, start_ref, fresh_ref,
-        kc_ref, vc_ref, span,
-    )
-    nk_ref[0] = keys
-    nv_ref[0] = values
-
-
 def attention_kernel(
     used_ref, owner_ref, column_ref, clen_ref, start_ref, req_ref, q_ref, fresh_ref, kc_ref, vc_ref,
-    o_ref, m_sc, l_sc, acc_sc, *, q_heads, head_dim
+    o_ref, nk_ref, nv_ref, m_sc, l_sc, acc_sc, *, q_heads, head_dim
 ):
     i = pl.program_id(0)
     r = req_ref[0]
@@ -87,11 +78,20 @@
         l_sc[...] = jnp.zeros(l_sc.shape, jnp.float32)
         acc_sc[...] = jnp.zeros(acc_sc.shape, jnp.float32)
 
-    @pl.when((used_ref[i] == 1) & (owner_ref[i] == r))
+    active = (used_ref[i] == 1) & (owner_ref[i] == r)
+
+    @pl.when(jnp.logical_not(active))
+    def _keep():
+        nk_ref[...] = kc_ref[...]
+        nv_ref[...] = vc_ref[...]
+
+    @pl.when(active)
     def _work():
         keys, values = merged_block(
             i, used_ref, owner_ref, column_ref, clen_ref, start_ref, fresh_ref, kc_ref, vc_ref, rows
         )
+        nk_ref[0] = keys
+        nv_ref[0] = values
         query_pos = clen_ref[r] + lax.broadcasted_iota(jnp.int32, (rows, block_size), 0)
         key_pos = column_ref[i] * block_size + lax.broadcasted_iota(
             jnp.int32, (rows, block_size), 1
@@ -128,31 +128,11 @@
         o_ref[:, q_heads * head_dim :] = stats.astype(o_ref.dtype)
 
 
-def block_meta(block_table, block_ids, cached_len, span, block_size, fresh_len):
+def block_meta(block_table, block_ids, cached_len, block_size, fresh_len):
     used, owner, column = block_owners(block_table, block_ids)
-    start = block_size + owner * span + column * block_size - cached_len[owner]
+    start = block_size + column * block_size - cached_len[owner]
     start = jnp.clip(start, 0, fresh_len - block_size - 8).astype(jnp.int32)
     return used, owner, column, cached_len, start
-
-
-def merge_local(meta, fresh_rows, key_cache, value_cache, span):
-    nb_dev, block_size, kv_width = key_cache.shape
-    block = pl.BlockSpec((1, block_size, kv_width), lambda i, *_: (i, 0, 0))
-    grid_spec = pltpu.PrefetchScalarGridSpec(
-        num_scalar_prefetch=5,
-        grid=(nb_dev,),
-        in_specs=[pl.BlockSpec(fresh_rows.shape, lambda i, *_: (0, 0)), block, block],
-        out_specs=[block, block],
-    )
-    return pl.pallas_call(
-        functools.partial(merge_kernel, span=span),
-        grid_spec=grid_spec,
-        out_shape=(
-            jax.ShapeDtypeStruct(key_cache.shape, key_cache.dtype),
-            jax.ShapeDtypeStruct(value_cache.shape, value_cache.dtype),
-        ),
-        compiler_params=pltpu.CompilerParams(vmem_limit_bytes=32 * 1024 * 1024),
-    )(*meta, fresh_rows, key_cache, value_cache)
 
 
 def attend(queries, fresh_rows, keys, values, meta, request, span, q_heads, head_dim):
@@ -169,7 +149,7 @@
             block,
             block,
         ],
-        out_specs=pl.BlockSpec((span, out_width), lambda i, *_: (0, 0)),
+        out_specs=[pl.BlockSpec((span, out_width), lambda i, *_: (0, 0)), block, block],
         scratch_shapes=[
             pltpu.VMEM((q_heads, span, head_dim), jnp.float32),
             pltpu.VMEM((q_heads, span, head_dim), jnp.float32),
@@ -180,7 +160,11 @@
     return pl.pallas_call(
         functools.partial(attention_kernel, q_heads=q_heads, head_dim=head_dim),
         grid_spec=grid_spec,
-        out_shape=jax.ShapeDtypeStruct((span, out_width), jnp.bfloat16),
+        out_shape=(
+            jax.ShapeDtypeStruct((span, out_width), jnp.bfloat16),
+            jax.ShapeDtypeStruct(keys.shape, keys.dtype),
+            jax.ShapeDtypeStruct(values.shape, values.dtype),
+        ),
         compiler_params=pltpu.CompilerParams(vmem_limit_bytes=48 * 1024 * 1024),
         cost_estimate=pl.CostEstimate(
             flops=flops,
@@ -193,80 +177,95 @@
 MESH = pl.DeviceIdType.MESH
 
 
-def group_exchange_kernel(*refs, m, stride, gather, n_arr):
-    srcs, dsts = refs[:n_arr], refs[n_arr : 2 * n_arr]
-    send_sem, recv_sem, own_sem = refs[2 * n_arr :]
-    me = lax.axis_index("blk")
-    kv = lax.axis_index("kv")
-    pos = lax.rem(me // stride, m)
-    base = me - pos * stride
-
-    def member(j):
-        return base + j * stride
+def multi_exchange_kernel(*refs, specs):
+    n_total = sum(s[4] for s in specs)
+    srcs, dsts = refs[:n_total], refs[n_total : 2 * n_total]
+    send_sem, recv_sem, own_sem = refs[2 * n_total :]
+    here = {"kv": lax.axis_index("kv"), "blk": lax.axis_index("blk")}
+
+    def device(axis, index):
+        return (index, here["blk"]) if axis == "kv" else (here["kv"], index)
+
+    groups = []
+    arr0, sem0 = 0, 0
+    for axis, m, stride, gather, n_arr in specs:
+        pos = lax.rem(here[axis] // stride, m)
+        base = here[axis] - pos * stride
+        groups.append((axis, m, stride, gather, n_arr, pos, base, arr0, sem0))
+        arr0 += n_arr
+        sem0 += m * n_arr
 
     barrier = pltpu.get_barrier_semaphore()
-    for k in range(1, m):
-        peer = member(lax.rem(pos + k, m))
-        pl.semaphore_signal(barrier, inc=1, device_id=(kv, peer), device_id_type=MESH)
-    pl.semaphore_wait(barrier, m - 1)
-
-    def chunk(src, j):
+    for axis, m, stride, gather, n_arr, pos, base, _, _ in groups:
+        for k in range(1, m):
+            peer = base + lax.rem(pos + k, m) * stride
+            pl.semaphore_signal(barrier, inc=1, device_id=device(axis, peer), device_id_type=MESH)
+    pl.semaphore_wait(barrier, sum(s[1] - 1 for s in specs))
+
+    def chunk(src, j, m, gather):
         if gather:
             return src
         rows = src.shape[0] // m
         return src.at[pl.ds(pl.multiple_of(j * rows, rows), rows)]
 
-    owns = []
-    for a in range(n_arr):
-        own = pltpu.make_async_copy(chunk(srcs[a], pos), dsts[a].at[pos], own_sem.at[a])
-        own.start()
-        owns.append(own)
-    copies = []
-    for k in range(1, m):
-        peer_pos = lax.rem(pos + k, m)
-        for a in range(n_arr):
-            copy = pltpu.make_async_remote_copy(
-                src_ref=chunk(srcs[a], peer_pos),
-                dst_ref=dsts[a].at[pos],
-                send_sem=send_sem.at[k * n_arr + a],
-                recv_sem=recv_sem.at[k * n_arr + a],
-                device_id=(kv, member(peer_pos)),
-                device_id_type=MESH,
-            )
-            copy.start()
-            copies.append(copy)
+    owns, copies = [], []
+    for axis, m, stride, gather, n_arr, pos, base, a0, s0 in groups:
+        for a in range(a0, a0 + n_arr):
+            own = pltpu.make_async_copy(chunk(srcs[a], pos, m, gather), dsts[a].at[pos], own_sem.at[a])
+            own.start()
+            owns.append(own)
+    for axis, m, stride, gather, n_arr, pos, base, a0, s0 in groups:
+        for k in range(1, m):
+            peer_pos = lax.rem(pos + k, m)
+            for a in range(n_arr):
+                copy = pltpu.make_async_remote_copy(
+                    src_ref=chunk(srcs[a0 + a], peer_pos, m, gather),
+                    dst_ref=dsts[a0 + a].at[pos],
+                    send_sem=send_sem.at[s0 + k * n_arr + a],
+                    recv_sem=recv_sem.at[s0 + k * n_arr + a],
+                    device_id=device(axis, base + peer_pos * stride),
+                    device_id_type=MESH,
+                )
+                copy.start()
+                copies.append(copy)
     for own in owns:
         own.wait()
-    for k in range(1, m):
-        sender_pos = lax.rem(pos + m - k, m)
-        for a in range(n_arr):
-            incoming = pltpu.make_async_remote_copy(
-                src_ref=chunk(srcs[a], pos),
-                dst_ref=dsts[a].at[sender_pos],
-                send_sem=send_sem.at[k * n_arr + a],
-                recv_sem=recv_sem.at[k * n_arr + a],
-                device_id=(kv, member(sender_pos)),
-                device_id_type=MESH,
-            )
-            copies[(k - 1) * n_arr + a].wait_send()
-            incoming.wait_recv()
-
-
-def group_exchange(arrays, m, stride, gather, collective_id):
-    n_arr = len(arrays)
-    shapes = []
-    for x in arrays:
-        rows = x.shape[0] if gather else x.shape[0] // m
-        shapes.append(jax.ShapeDtypeStruct((m, rows) + x.shape[1:], x.dtype))
+    c = 0
+    for axis, m, stride, gather, n_arr, pos, base, a0, s0 in groups:
+        for k in range(1, m):
+            sender_pos = lax.rem(pos + m - k, m)
+            for a in range(n_arr):
+                incoming = pltpu.make_async_remote_copy(
+                    src_ref=chunk(srcs[a0 + a], pos, m, gather),
+                    dst_ref=dsts[a0 + a].at[sender_pos],
+                    send_sem=send_sem.at[s0 + k * n_arr + a],
+                    recv_sem=recv_sem.at[s0 + k * n_arr + a],
+                    device_id=device(axis, base + sender_pos * stride),
+                    device_id_type=MESH,
+                )
+                copies[c].wait_send()
+                incoming.wait_recv()
+                c += 1
+
+
+def multi_exchange(groups, collective_id):
+    specs, arrays, shapes = [], [], []
+    for axis, m, stride, gather, arrs in groups:
+        specs.append((axis, m, stride, gather, len(arrs)))
+        for x in arrs:
+            rows = x.shape[0] if gather else x.shape[0] // m
+            arrays.append(x)
+            shapes.append(jax.ShapeDtypeStruct((m, rows) + x.shape[1:], x.dtype))
+    n_sem = sum(s[1] * s[4] for s in specs)
     return pl.pallas_call(
-        functools.partial(group_exchange_kernel, m=m, stride=stride, gather=gather, n_arr=n_arr),
+        functools.partial(multi_exchange_kernel, specs=tuple(specs)),
         out_shape=tuple(shapes),
-        in_specs=[pl.BlockSpec(memory_space=pl.ANY)] * n_arr,
-        out_specs=tuple([pl.BlockSpec(memory_space=pl.ANY)] * n_arr),
+        in_specs=[pl.BlockSpec(memory_space=pl.ANY)] * len(arrays),
+        out_specs=tuple([pl.BlockSpec(memory_space=pl.ANY)] * len(arrays)),
         scratch_shapes=[
-            pltpu.SemaphoreType.DMA((m * n_arr,)),
-            pltpu.SemaphoreType.DMA((m * n_arr,)),
-            pltpu.SemaphoreType.DMA((n_arr,)),
+            pltpu.SemaphoreType.DMA((n_sem,)),
+            pltpu.SemaphoreType.DMA((n_sem,)),
+            pltpu.SemaphoreType.DMA((len(arrays),)),
         ],
         compiler_params=pltpu.CompilerParams(collective_id=collective_id, has_side_effects=True),
     )(*arrays)
@@ -298,7 +297,14 @@
     q_heads = w_query.shape[1] // head_dim
     group_size = q_heads // kv_heads
     gain = norm_gain.astype(jnp.float32)
-    whole = lax.all_gather(hidden_in, "kv", axis=1, tiled=True)
+    ring = span // tok_dev
+    cols = n_blk // ring
+    position = device % ring
+    kv_n = lax.axis_size("kv")
+    got_hidden, col_keys, col_values = multi_exchange(
+        [("kv", kv_n, 1, True, [hidden_in]), ("blk", cols, ring, True, [key_cache, value_cache])], 0
+    )
+    whole = got_hidden.transpose(1, 0, 2).reshape(tok_dev, kv_n * hidden_in.shape[1])
     wide_in = whole.astype(jnp.float32)
     scale = lax.rsqrt(jnp.mean(wide_in * wide_in, axis=1, keepdims=True) + EPS)
     normed = (wide_in * scale * gain[None, :]).astype(jnp.bfloat16)
@@ -321,23 +327,18 @@
     fresh_keys = fresh_keys.astype(jnp.bfloat16).reshape(tok_dev, kv_width)
     fresh_values = (value_linear + value_bias.astype(jnp.float32)[None, :]).astype(jnp.bfloat16)
     q_width = q_heads * head_dim
-    packed = jnp.concatenate([fresh_keys, fresh_values], axis=1)
-    kv_all = lax.all_gather(packed, "blk", axis=0, tiled=True)
-    ring = span // tok_dev
-    cols = n_blk // ring
-    position = device % ring
-    col_keys, col_values = group_exchange([key_cache, value_cache], cols, ring, True, 0)
-    (ring_queries,) = group_exchange([fresh_queries], ring, 1, True, 2)
-    fresh_rows = jnp.pad(kv_all.astype(jnp.float32), ((block_size, block_size + 8), (0, 0)))
-    local_ids = device * nb_dev + jnp.arange(nb_dev, dtype=jnp.int32)
-    meta = block_meta(block_table, local_ids, cached_len, span, block_size, fresh_rows.shape[0])
-    new_k, new_v = merge_local(meta, fresh_rows, key_cache, value_cache, span)
+    packed = jnp.concatenate([fresh_queries, fresh_keys, fresh_values], axis=1)
+    (ring_packed,) = multi_exchange([("blk", ring, 1, True, [packed])], 1)
+    ring_packed = ring_packed.reshape(span, packed.shape[1])
+    fresh_rows = jnp.pad(
+        ring_packed[:, q_width:].astype(jnp.float32), ((block_size, block_size + 8), (0, 0))
+    )
     holders = jnp.arange(cols, dtype=jnp.int32) * ring + position
     col_ids = (holders[:, None] * nb_dev + jnp.arange(nb_dev, dtype=jnp.int32)[None, :]).reshape(-1)
-    meta = block_meta(block_table, col_ids, cached_len, span, block_size, fresh_rows.shape[0])
+    meta = block_meta(block_table, col_ids, cached_len, block_size, fresh_rows.shape[0])
     request = (device // ring).reshape(1).astype(jnp.int32)
-    parts = attend(
-        ring_queries.reshape(span, q_width),
+    parts, merged_k, merged_v = attend(
+        ring_packed,
         fresh_rows,
         col_keys.reshape(cols * nb_dev, block_size, kv_width),
         col_values.reshape(cols * nb_dev, block_size, kv_width),
@@ -347,7 +348,13 @@
         q_heads,
         head_dim,
     )
-    (got,) = group_exchange([parts], ring, 1, False, 1)
+    got, back_k, back_v = multi_exchange(
+        [("blk", ring, 1, False, [parts]), ("blk", cols, ring, False, [merged_k, merged_v])], 2
+    )
+    local_ids = device * nb_dev + jnp.arange(nb_dev, dtype=jnp.int32)
+    _, owner, _ = block_owners(block_table, local_ids)
+    new_k = back_k.reshape(cols, nb_dev, block_size, kv_width)[owner, jnp.arange(nb_dev)]
+    new_v = back_v.reshape(cols, nb_dev, block_size, kv_width)[owner, jnp.arange(nb_dev)]
     got = got.astype(jnp.float32)
     got_w = got[..., :q_width].reshape(ring, tok_dev, q_heads, head_dim)
     got_l = got[..., q_width : q_width + group_size]

time: 250 us -> 226 us (0.904); the launches traced: 245 us -> 224 us
  waiting for transfers between devices: 34.5 us -> 0 us
  Pallas kernels: 157 us -> 173 us
  between operations: 14.4 us -> 0.91 us
  local copies, waits for them, and re-layouts: 12.7 us -> 23 us
    all_gather x2 -> x0, waiting for transfers between devices: 33.8 us -> none  [the longest x1 29.7 us: on_device(): whole = lax.all_gather(hidden_in, 'kv', axis=1, tiled=True)]
    pallas_call x1, Pallas kernels: 19 us -> 31.8 us  [attend(): pl.pallas_call(functools.partial(attention_kernel, q_heads=q_heads, head_...]
    gather x2 -> x3, local copies, waits for them, and re-layouts: 1.3 us -> 7.21 us  [the longest x1 2.93 us: on_device(): back_k.reshape(cols, nb_dev, block_size, kv_width)]
    convert_element_type x0 -> x2, other arithmetic: none -> 5.17 us  [the longest x1 3.48 us: on_device(): normed = (wide_in * scale * gain[None, :]).astype(jnp.bfloat16)]
    pad x1, other arithmetic: 4.13 us -> 0.09 us  [on_device(): jnp.pad(ring_packed[:, q_width:].astype(jnp.float32), ((block_size, block...]
    pallas_call x4 -> x3, Pallas kernels: 138 us -> 141 us  [multi_exchange(): pl.pallas_call(functools.partial(multi_exchange_kernel, specs=tuple(specs...]
    convert_element_type x0 -> x1, local copies, waits for them, and re-layouts: none -> 3.25 us  [on_device(): wide_in = whole.astype(jnp.float32)]
    unnamed x28 -> x18, local copies, waits for them, and re-layouts: 4.96 us -> 5.65 us
  transfers between devices with their start and end apart: 2 -> 0, of which waited for: 2 -> 0; matrix products, arithmetic and copies ran while one was open for 6% -> 0% of each run, Pallas kernels for 34% -> 0%
where the time goes in v6:
time: 226 us; the launch traced here: 224 us
  Pallas kernels  173 us (77%)
  local copies, waits for them, and re-layouts  23 us (10%)
  other arithmetic  21.7 us (10%)
  matrix products  5.24 us (2%)
    pallas_call x3, Pallas kernels, multi_exchange(): pl.pallas_call(functools.partial(multi_exchange_kernel, specs=tuple(specs...  141 us
    pallas_call x1, Pallas kernels, attend(): pl.pallas_call(functools.partial(attention_kernel, q_heads=q_heads, head_...  31.8 us
    unnamed x18, local copies, waits for them, and re-layouts  5.65 us
    mul x2, local copies, waits for them, and re-layouts, on_device(): mine_weighted = jnp.sum(got_w * scale_d[..., None], axis=0)  4.93 us

profile of v6, /device:TPU:1, one launch (start us, length us, event | category | flops | bytes accessed | tf_op | source)
XLA Modules:
  0.0 223.7 jit_solution(18113267133319366686)
XLA Ops:
  0.7 1.1 select_reduce_fusion
  4.1 0.9 compare_reduce_fusion
  5.0 0.9 fusion.8
  5.9 1.5 fusion.28
  7.4 2.6 %fusion.26.start_ref = s32[48]{0:T(128)S(1)} fusion(s32[48]{0:T(128)S(1)} %get-tuple-element.25.owner_ref, s32[48]{0:T(128)S(1)} %get-tuple-element.24.column_ref, s32[]{:T(128)} %bitcast.1, s32[]{:T(128)} %bitcast.2, s32[]{:T(128)} %bitcast.4, s32[]{:T(128)} %bitcast.3), kind=kLoop, calls=%fused_computation.70 | loop fusion | flops 624 | bytes 592 | tf_op jit(solution)/shard_map/jit(clip)/min | solution.py:134
  11.6 42.4 %shard_map.139 = (bf16[8,128,640]{2,1,0:T(8,128)(2,1)}, bf16[4,12,128,128]{3,2,1,0:T(8,128)(2,1)}, bf16[4,12,128,128]{3,2,1,0:T(8,128)(2,1)}) custom-call(bf16[128,640]{1,0:T(8,128)(2,1)} %refs_0_.1, bf16[12,128,128]{2,1,0:T(8,128)(2,1)} %refs_1_.1, bf16[12,128,128]{2,1,0:T(8,128)(2,1)} %refs_2_.1), custom_call_target="tpu_custom_call" | custom-call | tf_op jit(solution)/shard_map/pallas_call | solution.py:260
  54.0 1.8 fusion
  55.8 1.7 convert_bitcast_fusion
  57.5 3.3 %copy.34 = f32[128,8,640]{0,2,1:T(8,128)} copy(f32[128,8,640]{2,0,1:T(8,128)} %convert_bitcast_fusion) | data formatting | bytes 5242880 | tf_op jit(solution)/shard_map/convert_element_type | solution.py:308
  60.7 3.5 %fusion.3 = bf16[128,5120]{0,1:T(8,128)(2,1)S(1)} fusion(f32[128,8,640]{0,2,1:T(8,128)} %copy.34, f32[5120]{0:T(1024)S(1)} %convert_element_type.66, f32[128]{0:T(128)S(1)} %add_rsqrt_fusion), kind=kLoop, calls=%fused_computation.9 | loop fusion | flops 1966080 | bytes 3953152 | tf_op jit(solution)/shard_map/convert_element_type | solution.py:310
  66.1 4.1 %convolution_add_fusion = f32[128,640]{1,0:T(8,128)S(1)} fusion(bf16[128,5120]{0,1:T(8,128)(2,1)S(1)} %fusion.3, bf16[5120,640]{1,0:T(8,128)(2,1)} %param.14, f32[640]{0:T(1024)S(1)} %convert_element_type.68), kind=kOutput, calls=%fused_computation.10 | convolution fusion | flops 838942720 | bytes 8194560 | tf_op jit(solution)/shard_map/dot_general | solution.py:311
  71.7 48.1 %shard_map.140 = bf16[8,128,896]{2,1,0:T(8,128)(2,1)} custom-call(bf16[128,896]{1,0:T(8,128)(2,1)} %pad_maximum_fusion.refs_0_), custom_call_target="tpu_custom_call" | custom-call | tf_op jit(solution)/shard_map/pallas_call | solution.py:260
  119.9 1.1 slice.45
  121.1 31.8 %shard_map.141 = (bf16[1024,768]{1,0:T(8,128)(2,1)S(1)}, bf16[48,128,128]{2,1,0:T(8,128)(2,1)S(1)}, bf16[48,128,128]{2,1,0:T(8,128)(2,1)S(1)}) custom-call(s32[48]{0:T(128)S(1)} %convert_element_type.61.used_ref, s32[48]{0:T(128)S(1)} %get-tuple-element.25.owner_ref, s32[48]{0:T(128)S(1)} %get-tuple-element.24.column_ref, s32[4]{0:T(128)S(1)} %copy-done.4, ...), custom_call_target="tpu_custom_call" | custom-call | flops 4026531840 | bytes 6029312 | tf_op jit(solution)/shard_map/pallas_call | solution.py:160
  152.8 1.1 copy-done.1
  154.0 1.1 copy-done.2
  155.1 1.1 copy-done.3
  156.3 50.6 %shard_map.142 = (bf16[8,128,768]{2,1,0:T(8,128)(2,1)}, bf16[4,12,128,128]{3,2,1,0:T(8,128)(2,1)}, bf16[4,12,128,128]{3,2,1,0:T(8,128)(2,1)}) custom-call(bf16[1024,768]{1,0:T(8,128)(2,1)} %copy-done.1, bf16[48,128,128]{2,1,0:T(8,128)(2,1)} %copy-done.2, bf16[48,128,128]{2,1,0:T(8,128)(2,1)} %copy-done.3), custom_call_target="tpu_custom_call" | custom-call | tf_op jit(solution)/shard_map/pallas_call | solution.py:260
  206.9 2.9 %gather_fusion = bf16[12,128,128]{2,1,0:T(8,128)(2,1)} fusion(bf16[4,12,128,128]{3,2,1,0:T(8,128)(2,1)} %get-tuple-element.19, s32[12]{0:T(128)S(1)} %fusion.25), kind=kCustom, calls=%fused_computation | custom fusion | bytes 786528 | tf_op jit(solution)/shard_map/gather | solution.py:356
  209.8 2.8 %gather_fusion.1 = bf16[12,128,128]{2,1,0:T(8,128)(2,1)} fusion(bf16[4,12,128,128]{3,2,1,0:T(8,128)(2,1)} %get-tuple-element.20, s32[12]{0:T(128)S(1)} %fusion.25), kind=kCustom, calls=%fused_computation.1 | custom fusion | bytes 786528 | tf_op jit(solution)/shard_map/gather | solution.py:357
  213.1 1.4 copy-done.5
  215.2 1.7 mul.174
  216.9 3.3 %copy.40 = f32[8,128,640]{2,1,0:T(8,128)} copy(f32[8,128,640]{1,2,0:T(8,128)} %bitcast.48) | data formatting | bytes 5242880 | tf_op jit(solution)/shard_map/mul | solution.py:365
  220.2 2.8 %fusion.1 = f32[128,640]{1,0:T(8,128)S(1)} fusion(f32[8,128,640]{2,1,0:T(8,128)} %copy.40, f32[8,128,768]{2,1,0:T(8,128)} %copy-done.5), kind=kLoop, calls=%fused_computation.6 | loop fusion | flops 1228800 | bytes 5570560 | tf_op jit(solution)/shard_map/reduce_sum | solution.py:365
  (47 shorter events, 9.2 us)
Async XLA Ops:
  0.6 63.6 %copy-start = (bf16[5120,128]{1,0:T(8,128)(2,1)S(1)}, bf16[5120,128]{1,0:T(8,128)(2,1)}, u32[]{:S(2)}) copy-start(bf16[5120,128]{1,0:T(8,128)(2,1)} %param.16) | copy-start | bytes 3932164
  54.0 1.8 copy-start.6
  64.2 1.3 copy-start.8
  119.9 1.2 copy-start.4
  152.8 1.2 copy-start.1
  154.0 1.1 copy-start.2
  155.1 1.1 copy-start.3
  206.8 5.7 %copy-start.7 = (bf16[8,128,768]{2,1,0:T(8,128)(2,1)S(1)}, bf16[8,128,768]{2,1,0:T(8,128)(2,1)}, u32[]{:S(2)}) copy-start(bf16[8,128,768]{2,1,0:T(8,128)(2,1)} %get-tuple-element.18) | copy-start | bytes 4718596
  212.9 1.7 copy-start.5

commit v7 on v6

--- a/solution.py
+++ b/solution.py
@@ -58,8 +58,8 @@
     )
     first_new = clen_ref[owner_ref[i]]
     fresh = (used_ref[i] == 1) & (slot_pos >= first_new) & (slot_pos < first_new + span)
-    keys = jnp.where(fresh, window[:, :kv_width], kc_ref[0].astype(jnp.float32))
-    values = jnp.where(fresh, window[:, kv_width:], vc_ref[0].astype(jnp.float32))
+    keys = jnp.where(fresh, window[:, :kv_width], kc_ref[i].astype(jnp.float32))
+    values = jnp.where(fresh, window[:, kv_width:], vc_ref[i].astype(jnp.float32))
     return keys.astype(kc_ref.dtype), values.astype(vc_ref.dtype)
 
 
@@ -82,16 +82,16 @@
 
     @pl.when(jnp.logical_not(active))
     def _keep():
-        nk_ref[...] = kc_ref[...]
-        nv_ref[...] = vc_ref[...]
+        nk_ref[i] = kc_ref[i]
+        nv_ref[i] = vc_ref[i]
 
     @pl.when(active)
     def _work():
         keys, values = merged_block(
             i, used_ref, owner_ref, column_ref, clen_ref, start_ref, fresh_ref, kc_ref, vc_ref, rows
         )
-        nk_ref[0] = keys
-        nv_ref[0] = values
+        nk_ref[i] = keys
+        nv_ref[i] = values
         query_pos = clen_ref[r] + lax.broadcasted_iota(jnp.int32, (rows, block_size), 0)
         key_pos = column_ref[i] * block_size + lax.broadcasted_iota(
             jnp.int32, (rows, block_size), 1
@@ -139,7 +139,7 @@
     n_blocks, block_size, kv_width = keys.shape
     q_width = q_heads * head_dim
     out_width = q_width + head_dim
-    block = pl.BlockSpec((1, block_size, kv_width), lambda i, *_: (i, 0, 0))
+    block = pl.BlockSpec(keys.shape, lambda i, *_: (0, 0, 0))
     grid_spec = pltpu.PrefetchScalarGridSpec(
         num_scalar_prefetch=6,
         grid=(n_blocks,),

time: 226 us -> 212 us (0.938)
  Pallas kernels: 173 us -> 161 us
    pallas_call x1, Pallas kernels: 31.8 us -> 17 us  [attend(): pl.pallas_call(functools.partial(attention_kernel, q_heads=q_heads, head_...]
    pallas_call x3, Pallas kernels: 141 us -> 144 us  [multi_exchange(): pl.pallas_call(functools.partial(multi_exchange_kernel, specs=tuple(specs...]
where the time goes in v7:
time: 212 us
  Pallas kernels  161 us (76%)
  local copies, waits for them, and re-layouts  23 us (11%)
  other arithmetic  21.7 us (10%)
  matrix products  5.24 us (2%)
    pallas_call x3, Pallas kernels, multi_exchange(): pl.pallas_call(functools.partial(multi_exchange_kernel, specs=tuple(specs...  144 us
    pallas_call x1, Pallas kernels, attend(): pl.pallas_call(functools.partial(attention_kernel, q_heads=q_heads, head_...  17 us
    unnamed x18, local copies, waits for them, and re-layouts  5.65 us
    mul x2, local copies, waits for them, and re-layouts, on_device(): mine_weighted = jnp.sum(got_w * scale_d[..., None], axis=0)  4.93 us

profile of v7, /device:TPU:1, one launch (start us, length us, event | category | flops | bytes accessed | tf_op | source)
XLA Modules:
  0.0 211.7 jit_solution(4124011915433570013)
XLA Ops:
  0.7 1.1 select_reduce_fusion
  4.1 0.9 compare_reduce_fusion
  5.0 0.9 fusion.8
  5.9 1.5 fusion.28
  7.4 2.6 %fusion.26.start_ref = s32[48]{0:T(128)S(1)} fusion(s32[48]{0:T(128)S(1)} %get-tuple-element.25.owner_ref, s32[48]{0:T(128)S(1)} %get-tuple-element.24.column_ref, s32[]{:T(128)} %bitcast.1, s32[]{:T(128)} %bitcast.2, s32[]{:T(128)} %bitcast.4, s32[]{:T(128)} %bitcast.3), kind=kLoop, calls=%fused_computation.70 | loop fusion | flops 624 | bytes 592 | tf_op jit(solution)/shard_map/jit(clip)/min | solution.py:134
  11.6 42.4 %shard_map.139 = (bf16[8,128,640]{2,1,0:T(8,128)(2,1)}, bf16[4,12,128,128]{3,2,1,0:T(8,128)(2,1)}, bf16[4,12,128,128]{3,2,1,0:T(8,128)(2,1)}) custom-call(bf16[128,640]{1,0:T(8,128)(2,1)} %refs_0_.1, bf16[12,128,128]{2,1,0:T(8,128)(2,1)} %refs_1_.1, bf16[12,128,128]{2,1,0:T(8,128)(2,1)} %refs_2_.1), custom_call_target="tpu_custom_call" | custom-call | tf_op jit(solution)/shard_map/pallas_call | solution.py:260
  54.0 1.8 fusion
  55.8 1.7 convert_bitcast_fusion
  57.5 3.3 %copy.34 = f32[128,8,640]{0,2,1:T(8,128)} copy(f32[128,8,640]{2,0,1:T(8,128)} %convert_bitcast_fusion) | data formatting | bytes 5242880 | tf_op jit(solution)/shard_map/convert_element_type | solution.py:308
  60.7 3.5 %fusion.3 = bf16[128,5120]{0,1:T(8,128)(2,1)S(1)} fusion(f32[128,8,640]{0,2,1:T(8,128)} %copy.34, f32[5120]{0:T(1024)S(1)} %convert_element_type.66, f32[128]{0:T(128)S(1)} %add_rsqrt_fusion), kind=kLoop, calls=%fused_computation.9 | loop fusion | flops 1966080 | bytes 3953152 | tf_op jit(solution)/shard_map/convert_element_type | solution.py:310
  66.1 4.1 %convolution_add_fusion = f32[128,640]{1,0:T(8,128)S(1)} fusion(bf16[128,5120]{0,1:T(8,128)(2,1)S(1)} %fusion.3, bf16[5120,640]{1,0:T(8,128)(2,1)} %param.14, f32[640]{0:T(1024)S(1)} %convert_element_type.68), kind=kOutput, calls=%fused_computation.10 | convolution fusion | flops 838942720 | bytes 8194560 | tf_op jit(solution)/shard_map/dot_general | solution.py:311
  71.7 48.1 %shard_map.140 = bf16[8,128,896]{2,1,0:T(8,128)(2,1)} custom-call(bf16[128,896]{1,0:T(8,128)(2,1)} %pad_maximum_fusion.refs_0_), custom_call_target="tpu_custom_call" | custom-call | tf_op jit(solution)/shard_map/pallas_call | solution.py:260
  119.9 1.1 slice.45
  121.1 17.0 %shard_map.141 = (bf16[1024,768]{1,0:T(8,128)(2,1)S(1)}, bf16[48,128,128]{2,1,0:T(8,128)(2,1)S(1)}, bf16[48,128,128]{2,1,0:T(8,128)(2,1)S(1)}) custom-call(s32[48]{0:T(128)S(1)} %convert_element_type.61.used_ref, s32[48]{0:T(128)S(1)} %get-tuple-element.25.owner_ref, s32[48]{0:T(128)S(1)} %get-tuple-element.24.column_ref, s32[4]{0:T(128)S(1)} %copy-done.4, ...), custom_call_target="tpu_custom_call" | custom-call | flops 4026531840 | bytes 6029312 | tf_op jit(solution)/shard_map/pallas_call | solution.py:160
  138.1 1.1 copy-done.1
  139.3 1.1 copy-done.2
  140.4 1.1 copy-done.3
  141.5 53.3 %shard_map.142 = (bf16[8,128,768]{2,1,0:T(8,128)(2,1)}, bf16[4,12,128,128]{3,2,1,0:T(8,128)(2,1)}, bf16[4,12,128,128]{3,2,1,0:T(8,128)(2,1)}) custom-call(bf16[1024,768]{1,0:T(8,128)(2,1)} %copy-done.1, bf16[48,128,128]{2,1,0:T(8,128)(2,1)} %copy-done.2, bf16[48,128,128]{2,1,0:T(8,128)(2,1)} %copy-done.3), custom_call_target="tpu_custom_call" | custom-call | tf_op jit(solution)/shard_map/pallas_call | solution.py:260
  194.9 2.9 %gather_fusion = bf16[12,128,128]{2,1,0:T(8,128)(2,1)} fusion(bf16[4,12,128,128]{3,2,1,0:T(8,128)(2,1)} %get-tuple-element.19, s32[12]{0:T(128)S(1)} %fusion.25), kind=kCustom, calls=%fused_computation | custom fusion | bytes 786528 | tf_op jit(solution)/shard_map/gather | solution.py:356
  197.8 2.8 %gather_fusion.1 = bf16[12,128,128]{2,1,0:T(8,128)(2,1)} fusion(bf16[4,12,128,128]{3,2,1,0:T(8,128)(2,1)} %get-tuple-element.20, s32[12]{0:T(128)S(1)} %fusion.25), kind=kCustom, calls=%fused_computation.1 | custom fusion | bytes 786528 | tf_op jit(solution)/shard_map/gather | solution.py:357
  201.1 1.4 copy-done.5
  203.2 1.7 mul.174
  204.9 3.3 %copy.40 = f32[8,128,640]{2,1,0:T(8,128)} copy(f32[8,128,640]{1,2,0:T(8,128)} %bitcast.48) | data formatting | bytes 5242880 | tf_op jit(solution)/shard_map/mul | solution.py:365
  208.2 2.8 %fusion.1 = f32[128,640]{1,0:T(8,128)S(1)} fusion(f32[8,128,640]{2,1,0:T(8,128)} %copy.40, f32[8,128,768]{2,1,0:T(8,128)} %copy-done.5), kind=kLoop, calls=%fused_computation.6 | loop fusion | flops 1228800 | bytes 5570560 | tf_op jit(solution)/shard_map/reduce_sum | solution.py:365
  (47 shorter events, 9.2 us)
Async XLA Ops:
  0.6 63.6 %copy-start = (bf16[5120,128]{1,0:T(8,128)(2,1)S(1)}, bf16[5120,128]{1,0:T(8,128)(2,1)}, u32[]{:S(2)}) copy-start(bf16[5120,128]{1,0:T(8,128)(2,1)} %param.16) | copy-start | bytes 3932164
  54.0 1.8 copy-start.6
  64.2 1.3 copy-start.8
  119.9 1.2 copy-start.4
  138.1 1.2 copy-start.1
  139.3 1.1 copy-start.2
  140.4 1.1 copy-start.3
  194.8 5.7 %copy-start.7 = (bf16[8,128,768]{2,1,0:T(8,128)(2,1)S(1)}, bf16[8,128,768]{2,1,0:T(8,128)(2,1)}, u32[]{:S(2)}) copy-start(bf16[8,128,768]{2,1,0:T(8,128)(2,1)} %get-tuple-element.18) | copy-start | bytes 4718596
  200.9 1.7 copy-start.5

commit v8 on v7

--- a/solution.py
+++ b/solution.py
@@ -301,9 +301,7 @@
     cols = n_blk // ring
     position = device % ring
     kv_n = lax.axis_size("kv")
-    got_hidden, col_keys, col_values = multi_exchange(
-        [("kv", kv_n, 1, True, [hidden_in]), ("blk", cols, ring, True, [key_cache, value_cache])], 0
-    )
+    (got_hidden,) = multi_exchange([("kv", kv_n, 1, True, [hidden_in])], 0)
     whole = got_hidden.transpose(1, 0, 2).reshape(tok_dev, kv_n * hidden_in.shape[1])
     wide_in = whole.astype(jnp.float32)
     scale = lax.rsqrt(jnp.mean(wide_in * wide_in, axis=1, keepdims=True) + EPS)
@@ -328,7 +326,9 @@
     fresh_values = (value_linear + value_bias.astype(jnp.float32)[None, :]).astype(jnp.bfloat16)
     q_width = q_heads * head_dim
     packed = jnp.concatenate([fresh_queries, fresh_keys, fresh_values], axis=1)
-    (ring_packed,) = multi_exchange([("blk", ring, 1, True, [packed])], 1)
+    ring_packed, col_keys, col_values = multi_exchange(
+        [("blk", ring, 1, True, [packed]), ("blk", cols, ring, True, [key_cache, value_cache])], 1
+    )
     ring_packed = ring_packed.reshape(span, packed.shape[1])
     fresh_rows = jnp.pad(
         ring_packed[:, q_width:].astype(jnp.float32), ((block_size, block_size + 8), (0, 0))

time: 212 us -> 196 us (0.925)
  Pallas kernels: 161 us -> 145 us
    pallas_call x3, Pallas kernels: 144 us -> 130 us  [multi_exchange(): pl.pallas_call(functools.partial(multi_exchange_kernel, specs=tuple(specs...]
    pallas_call x1, Pallas kernels: 17 us -> 14.9 us  [attend(): pl.pallas_call(functools.partial(attention_kernel, q_heads=q_heads, head_...]
where the time goes in v8:
time: 196 us
  Pallas kernels  145 us (74%)
  local copies, waits for them, and re-layouts  23 us (12%)
  other arithmetic  21.7 us (11%)
  matrix products  5.24 us (3%)
    pallas_call x3, Pallas kernels, multi_exchange(): pl.pallas_call(functools.partial(multi_exchange_kernel, specs=tuple(specs...  130 us
    pallas_call x1, Pallas kernels, attend(): pl.pallas_call(functools.partial(attention_kernel, q_heads=q_heads, head_...  14.9 us
    unnamed x18, local copies, waits for them, and re-layouts  5.65 us
    mul x2, local copies, waits for them, and re-layouts, on_device(): mine_weighted = jnp.sum(got_w * scale_d[..., None], axis=0)  4.93 us
    dot_general x1, matrix products, on_device(): q_lin = jnp.dot(normed, w_query, preferred_element_type=jnp.float32)  4.11 us

profile of v8, /device:TPU:1, one launch (start us, length us, event | category | flops | bytes accessed | tf_op | source)
XLA Modules:
  0.0 195.8 jit_solution(5517746829117179235)
XLA Ops:
  0.7 1.1 select_reduce_fusion
  4.1 0.9 compare_reduce_fusion
  5.0 0.9 fusion.8
  5.9 1.5 fusion.28
  7.4 2.6 %fusion.26.start_ref = s32[48]{0:T(128)S(1)} fusion(s32[48]{0:T(128)S(1)} %get-tuple-element.25.owner_ref, s32[48]{0:T(128)S(1)} %get-tuple-element.24.column_ref, s32[]{:T(128)} %bitcast.1, s32[]{:T(128)} %bitcast.2, s32[]{:T(128)} %bitcast.4, s32[]{:T(128)} %bitcast.3), kind=kLoop, calls=%fused_computation.70 | loop fusion | flops 624 | bytes 592 | tf_op jit(solution)/shard_map/jit(clip)/min | solution.py:134
  11.6 21.8 %shard_map.139 = bf16[8,128,640]{2,1,0:T(8,128)(2,1)} custom-call(bf16[128,640]{1,0:T(8,128)(2,1)} %refs_0_.1), custom_call_target="tpu_custom_call" | custom-call | tf_op jit(solution)/shard_map/pallas_call | solution.py:260
  33.4 1.8 fusion
  35.2 1.7 convert_bitcast_fusion
  36.9 3.3 %copy.34 = f32[128,8,640]{0,2,1:T(8,128)} copy(f32[128,8,640]{2,0,1:T(8,128)} %convert_bitcast_fusion) | data formatting | bytes 5242880 | tf_op jit(solution)/shard_map/convert_element_type | solution.py:306
  40.1 3.5 %fusion.3 = bf16[128,5120]{0,1:T(8,128)(2,1)S(1)} fusion(f32[128,8,640]{0,2,1:T(8,128)} %copy.34, f32[5120]{0:T(1024)S(1)} %convert_element_type.66, f32[128]{0:T(128)S(1)} %add_rsqrt_fusion), kind=kLoop, calls=%fused_computation.9 | loop fusion | flops 1966080 | bytes 3953152 | tf_op jit(solution)/shard_map/convert_element_type | solution.py:308
  45.5 4.1 %convolution_add_fusion = f32[128,640]{1,0:T(8,128)S(1)} fusion(bf16[128,5120]{0,1:T(8,128)(2,1)S(1)} %fusion.3, bf16[5120,640]{1,0:T(8,128)(2,1)} %param.14, f32[640]{0:T(1024)S(1)} %convert_element_type.68), kind=kOutput, calls=%fused_computation.10 | convolution fusion | flops 838942720 | bytes 8194560 | tf_op jit(solution)/shard_map/dot_general | solution.py:309
  51.1 47.5 %shard_map.140 = (bf16[8,128,896]{2,1,0:T(8,128)(2,1)}, bf16[4,12,128,128]{3,2,1,0:T(8,128)(2,1)}, bf16[4,12,128,128]{3,2,1,0:T(8,128)(2,1)}) custom-call(bf16[128,896]{1,0:T(8,128)(2,1)} %pad_maximum_fusion.refs_0_, bf16[12,128,128]{2,1,0:T(8,128)(2,1)} %refs_1_.1, bf16[12,128,128]{2,1,0:T(8,128)(2,1)} %refs_2_.1), custom_call_target="tpu_custom_call" | custom-call | tf_op jit(solution)/shard_map/pallas_call | solution.py:260
  98.6 1.1 slice.45
  99.8 14.9 %shard_map.141 = (bf16[1024,768]{1,0:T(8,128)(2,1)S(1)}, bf16[48,128,128]{2,1,0:T(8,128)(2,1)S(1)}, bf16[48,128,128]{2,1,0:T(8,128)(2,1)S(1)}) custom-call(s32[48]{0:T(128)S(1)} %convert_element_type.61.used_ref, s32[48]{0:T(128)S(1)} %get-tuple-element.25.owner_ref, s32[48]{0:T(128)S(1)} %get-tuple-element.24.column_ref, s32[4]{0:T(128)S(1)} %copy-done.4, ...), custom_call_target="tpu_custom_call" | custom-call | flops 4026531840 | bytes 6029312 | tf_op jit(solution)/shard_map/pallas_call | solution.py:160
  114.7 1.1 copy-done.1
  115.9 1.1 copy-done.2
  117.0 1.1 copy-done.3
  118.1 60.8 %shard_map.142 = (bf16[8,128,768]{2,1,0:T(8,128)(2,1)}, bf16[4,12,128,128]{3,2,1,0:T(8,128)(2,1)}, bf16[4,12,128,128]{3,2,1,0:T(8,128)(2,1)}) custom-call(bf16[1024,768]{1,0:T(8,128)(2,1)} %copy-done.1, bf16[48,128,128]{2,1,0:T(8,128)(2,1)} %copy-done.2, bf16[48,128,128]{2,1,0:T(8,128)(2,1)} %copy-done.3), custom_call_target="tpu_custom_call" | custom-call | tf_op jit(solution)/shard_map/pallas_call | solution.py:260
  179.0 2.9 %gather_fusion = bf16[12,128,128]{2,1,0:T(8,128)(2,1)} fusion(bf16[4,12,128,128]{3,2,1,0:T(8,128)(2,1)} %get-tuple-element.19, s32[12]{0:T(128)S(1)} %fusion.25), kind=kCustom, calls=%fused_computation | custom fusion | bytes 786528 | tf_op jit(solution)/shard_map/gather | solution.py:356
  181.9 2.8 %gather_fusion.1 = bf16[12,128,128]{2,1,0:T(8,128)(2,1)} fusion(bf16[4,12,128,128]{3,2,1,0:T(8,128)(2,1)} %get-tuple-element.20, s32[12]{0:T(128)S(1)} %fusion.25), kind=kCustom, calls=%fused_computation.1 | custom fusion | bytes 786528 | tf_op jit(solution)/shard_map/gather | solution.py:357
  185.2 1.4 copy-done.5
  187.4 1.7 mul.174
  189.0 3.3 %copy.40 = f32[8,128,640]{2,1,0:T(8,128)} copy(f32[8,128,640]{1,2,0:T(8,128)} %bitcast.48) | data formatting | bytes 5242880 | tf_op jit(solution)/shard_map/mul | solution.py:365
  192.3 2.8 %fusion.1 = f32[128,640]{1,0:T(8,128)S(1)} fusion(f32[8,128,640]{2,1,0:T(8,128)} %copy.40, f32[8,128,768]{2,1,0:T(8,128)} %copy-done.5), kind=kLoop, calls=%fused_computation.6 | loop fusion | flops 1228800 | bytes 5570560 | tf_op jit(solution)/shard_map/reduce_sum | solution.py:365
  (47 shorter events, 9.2 us)
Async XLA Ops:
  0.6 43.0 %copy-start = (bf16[5120,128]{1,0:T(8,128)(2,1)S(1)}, bf16[5120,128]{1,0:T(8,128)(2,1)}, u32[]{:S(2)}) copy-start(bf16[5120,128]{1,0:T(8,128)(2,1)} %param.16) | copy-start | bytes 3932164
  33.4 1.8 copy-start.6
  43.6 1.3 copy-start.8
  98.6 1.2 copy-start.4
  114.7 1.2 copy-start.1
  115.9 1.1 copy-start.2
  117.0 1.1 copy-start.3
  179.0 5.7 %copy-start.7 = (bf16[8,128,768]{2,1,0:T(8,128)(2,1)S(1)}, bf16[8,128,768]{2,1,0:T(8,128)(2,1)}, u32[]{:S(2)}) copy-start(bf16[8,128,768]{2,1,0:T(8,128)(2,1)} %get-tuple-element.18) | copy-start | bytes 4718596
  185.0 1.7 copy-start.5

commit v9 on v8

--- a/solution.py
+++ b/solution.py
@@ -172,6 +172,57 @@
             bytes_accessed=span * (q_width + out_width) * 2 + n_blocks * block_size * kv_width * 4,
         ),
     )(*meta, request, queries, fresh_rows, keys, values)
+
+
+def combine_kernel(owner_ref, got_ref, bk_ref, bv_ref, out_ref, nk_ref, nv_ref, *, q_heads, head_dim):
+    ring = got_ref.shape[0]
+    q_width = q_heads * head_dim
+    stats = [got_ref[s, :, q_width:].astype(jnp.float32) for s in range(ring)]
+    for g in range(q_heads):
+        tops = [st[:, q_heads + g : q_heads + g + 1] for st in stats]
+        best = tops[0]
+        for t in tops[1:]:
+            best = jnp.maximum(best, t)
+        weighted = jnp.zeros((out_ref.shape[0], head_dim), jnp.float32)
+        total = jnp.zeros((out_ref.shape[0], 1), jnp.float32)
+        for s in range(ring):
+            factor = jnp.exp(tops[s] - best)
+            part = got_ref[s, :, g * head_dim : (g + 1) * head_dim].astype(jnp.float32)
+            weighted = weighted + part * factor
+            total = total + stats[s][:, g : g + 1] * factor
+        out_ref[:, g * head_dim : (g + 1) * head_dim] = (weighted / total).astype(out_ref.dtype)
+    for b in range(nk_ref.shape[0]):
+        nk_ref[b] = bk_ref[owner_ref[b], b]
+        nv_ref[b] = bv_ref[owner_ref[b], b]
+
+
+def combine(owner, got, back_k, back_v, q_heads, head_dim):
+    ring, rows, _ = got.shape
+    nb_dev = back_k.shape[1]
+
+    def whole(x):
+        return pl.BlockSpec(x.shape, lambda i, *_: (0,) * x.ndim)
+
+    grid_spec = pltpu.PrefetchScalarGridSpec(
+        num_scalar_prefetch=1,
+        grid=(1,),
+        in_specs=[whole(got), whole(back_k), whole(back_v)],
+        out_specs=[
+            pl.BlockSpec((rows, q_heads * head_dim), lambda i, *_: (0, 0)),
+            pl.BlockSpec(back_k.shape[1:], lambda i, *_: (0, 0, 0)),
+            pl.BlockSpec(back_v.shape[1:], lambda i, *_: (0, 0, 0)),
+        ],
+    )
+    return pl.pallas_call(
+        functools.partial(combine_kernel, q_heads=q_heads, head_dim=head_dim),
+        grid_spec=grid_spec,
+        out_shape=(
+            jax.ShapeDtypeStruct((rows, q_heads * head_dim), jnp.bfloat16),
+            jax.ShapeDtypeStruct(back_k.shape[1:], back_k.dtype),
+            jax.ShapeDtypeStruct(back_v.shape[1:], back_v.dtype),
+        ),
+        compiler_params=pltpu.CompilerParams(vmem_limit_bytes=32 * 1024 * 1024),
+    )(owner, got, back_k, back_v)
 
 
 MESH = pl.DeviceIdType.MESH
@@ -302,13 +353,22 @@
     position = device % ring
     kv_n = lax.axis_size("kv")
     (got_hidden,) = multi_exchange([("kv", kv_n, 1, True, [hidden_in])], 0)
-    whole = got_hidden.transpose(1, 0, 2).reshape(tok_dev, kv_n * hidden_in.shape[1])
-    wide_in = whole.astype(jnp.float32)
-    scale = lax.rsqrt(jnp.mean(wide_in * wide_in, axis=1, keepdims=True) + EPS)
-    normed = (wide_in * scale * gain[None, :]).astype(jnp.bfloat16)
-    q_lin = jnp.dot(normed, w_query, preferred_element_type=jnp.float32)
-    key_linear = jnp.dot(normed, key_weight, preferred_element_type=jnp.float32)
-    value_linear = jnp.dot(normed, value_weight, preferred_element_type=jnp.float32)
+    feat = hidden_in.shape[1]
+    wide_in = got_hidden.astype(jnp.float32)
+    scale = lax.rsqrt(jnp.mean(wide_in * wide_in, axis=(0, 2), keepdims=True) + EPS)
+    normed = (wide_in * scale * gain.reshape(kv_n, 1, feat)).astype(jnp.bfloat16)
+
+    def project(weight):
+        return lax.dot_general(
+            normed,
+            weight.reshape(kv_n, feat, weight.shape[1]),
+            (((0, 2), (0, 1)), ((), ())),
+            preferred_element_type=jnp.float32,
+        )
+
+    q_lin = project(w_query)
+    key_linear = project(key_weight)
+    value_linear = project(value_weight)
     my_tokens = device * tok_dev + jnp.arange(tok_dev, dtype=jnp.int32)
     my_pos = lookup(cached_len, my_tokens // span) + my_tokens % span
     fresh_queries = apply_rotary(
@@ -353,20 +413,13 @@
     )
     local_ids = device * nb_dev + jnp.arange(nb_dev, dtype=jnp.int32)
     _, owner, _ = block_owners(block_table, local_ids)
-    new_k = back_k.reshape(cols, nb_dev, block_size, kv_width)[owner, jnp.arange(nb_dev)]
-    new_v = back_v.reshape(cols, nb_dev, block_size, kv_width)[owner, jnp.arange(nb_dev)]
-    got = got.astype(jnp.float32)
-    got_w = got[..., :q_width].reshape(ring, tok_dev, q_heads, head_dim)
-    got_l = got[..., q_width : q_width + group_size]
-    got_m = got[..., q_width + group_size : q_width + 2 * group_size]
-    best = jnp.max(got_m, axis=0)
-    scale_d = jnp.exp(got_m - best[None])
-    mine_total = jnp.sum(got_l * scale_d, axis=0)
-    mine_weighted = jnp.sum(got_w * scale_d[..., None], axis=0)
-    attn_out = (
-        (mine_weighted / mine_total[..., None])
-        .astype(jnp.bfloat16)
-        .reshape(tok_dev, q_heads * head_dim)
+    attn_out, new_k, new_v = combine(
+        owner,
+        got,
+        back_k.reshape(cols, nb_dev, block_size, kv_width),
+        back_v.reshape(cols, nb_dev, block_size, kv_width),
+        q_heads,
+        head_dim,
     )
     return (attn_out, new_k, new_v)
 

time: 196 us -> 188 us (0.959)
  Pallas kernels: 145 us -> 157 us
  local copies, waits for them, and re-layouts: 23 us -> 11.5 us
  other arithmetic: 21.7 us -> 11.4 us
    pallas_call x1, Pallas kernels: 14.9 us -> 31.9 us  [attend(): pl.pallas_call(functools.partial(attention_kernel, q_heads=q_heads, head_...]
    pallas_call x3, Pallas kernels: 130 us -> 122 us  [multi_exchange(): pl.pallas_call(functools.partial(multi_exchange_kernel, specs=tuple(specs...]
    convert_element_type x5 -> x0, other arithmetic: 6.87 us -> none  [the longest x1 3.48 us: on_device(): normed = (wide_in * scale * gain[None, :]).astype(jnp.bfloat16)]
    gather x2 -> x0, local copies, waits for them, and re-layouts: 5.73 us -> none  [the longest x1 2.93 us: on_device(): back_k.reshape(cols, nb_dev, block_size, kv_width)]
    mul x2 -> x1, local copies, waits for them, and re-layouts: 4.93 us -> 0.72 us  [on_device(): wide_in * scale * gain.reshape(kv_n, 1, feat)]
    convert_element_type x1 -> x0, local copies, waits for them, and re-layouts: 3.25 us -> none  [on_device(): wide_in = whole.astype(jnp.float32)]
    reduce_sum x3 -> x1, other arithmetic: 4.78 us -> 1.65 us  [on_device(): jnp.mean(wide_in * wide_in, axis=(0, 2), keepdims=True) + EPS]
    pallas_call x0 -> x1, Pallas kernels: none -> 2.54 us  [combine(): pl.pallas_call(functools.partial(combine_kernel, q_heads=q_heads, head_di...]
where the time goes in v9:
time: 188 us; the launch traced here: 187 us
  Pallas kernels  157 us (84%)
  local copies, waits for them, and re-layouts  11.5 us (6%)
  other arithmetic  11.4 us (6%)
  matrix products  6.86 us (4%)
    pallas_call x3, Pallas kernels, multi_exchange(): pl.pallas_call(functools.partial(multi_exchange_kernel, specs=tuple(specs...  122 us
    pallas_call x1, Pallas kernels, attend(): pl.pallas_call(functools.partial(attention_kernel, q_heads=q_heads, head_...  31.9 us
    unnamed x20, local copies, waits for them, and re-layouts  7.84 us
    dot_general x3, matrix products, project(): lax.dot_general(normed, weight.reshape(kv_n, feat, weight.shape[1]), (((0...  6.86 us

profile of v9, /device:TPU:1, one launch (start us, length us, event | category | flops | bytes accessed | tf_op | source)
XLA Modules:
  0.0 187.1 jit_solution(14688943412583028402)
XLA Ops:
  0.7 1.1 select_reduce_fusion.owner_ref
  3.3 0.7 select_reduce_fusion.1
  4.2 0.9 compare_reduce_fusion
  5.1 0.9 fusion.9
  6.0 1.4 fusion.28
  7.4 2.5 %fusion.23.start_ref = s32[48]{0:T(128)S(1)} fusion(s32[48]{0:T(128)S(1)} %get-tuple-element.22.owner_ref, s32[48]{0:T(128)S(1)} %get-tuple-element.21.column_ref, s32[]{:T(128)} %bitcast.1, s32[]{:T(128)} %bitcast.2, s32[]{:T(128)} %bitcast.4, s32[]{:T(128)} %bitcast.3), kind=kLoop, calls=%fused_computation.58 | loop fusion | flops 624 | bytes 592 | tf_op jit(solution)/shard_map/jit(clip)/min | solution.py:134
  9.9 0.7 convert_element_type.45
  10.6 0.7 reshape.248
  11.5 21.8 %shard_map.139 = bf16[8,128,640]{2,1,0:T(8,128)(2,1)} custom-call(bf16[128,640]{1,0:T(8,128)(2,1)} %refs_0_.1), custom_call_target="tpu_custom_call" | custom-call | tf_op jit(solution)/shard_map/pallas_call | solution.py:311
  33.3 1.7 fusion
  35.0 2.1 %fusion.7 = bf16[128,128]{1,0:T(8,128)(2,1)S(1)} fusion(bf16[8,640,128]{2,1,0:T(8,128)(2,1)S(1)} %bitcast.48, f32[128]{0:T(128)S(1)} %convert_element_type.49, bf16[8,128,640]{2,1,0:T(8,128)(2,1)} %shard_map.139, f32[8,640]{1,0:T(8,128)S(1)} %reshape.248, f32[128]{0:T(128)S(1)} %add_rsqrt_fusion), kind=kOutput, calls=%fused_computation.12 | convolution fusion | flops 170426368 | bytes 2675712 | tf_op jit(solution)/shard_map/dot_general | solution.py:362
  37.7 4.2 %fusion.3 = f32[128,640]{1,0:T(8,128)S(1)} fusion(bf16[8,640,640]{2,1,0:T(8,128)(2,1)} %bitcast.53, f32[640]{0:T(1024)S(1)} %convert_element_type.45, bf16[8,128,640]{2,1,0:T(8,128)(2,1)S(1)} %copy-done.8, f32[8,640]{1,0:T(8,128)S(1)} %reshape.248, f32[128]{0:T(128)S(1)} %add_rsqrt_fusion), kind=kOutput, calls=%fused_computation.6 | convolution fusion | flops 841564160 | bytes 8215552 | tf_op jit(solution)/shard_map/dot_general | solution.py:362
  42.6 0.8 pad_maximum_fusion.refs_0_
  43.4 47.5 %shard_map.140 = (bf16[8,128,896]{2,1,0:T(8,128)(2,1)}, bf16[4,12,128,128]{3,2,1,0:T(8,128)(2,1)}, bf16[4,12,128,128]{3,2,1,0:T(8,128)(2,1)}) custom-call(bf16[128,896]{1,0:T(8,128)(2,1)} %pad_maximum_fusion.refs_0_, bf16[12,128,128]{2,1,0:T(8,128)(2,1)} %refs_1_.1, bf16[12,128,128]{2,1,0:T(8,128)(2,1)} %refs_2_.1), custom_call_target="tpu_custom_call" | custom-call | tf_op jit(solution)/shard_map/pallas_call | solution.py:311
  90.9 1.1 slice.29
  92.1 31.9 %shard_map.141 = (bf16[1024,768]{1,0:T(8,128)(2,1)S(1)}, bf16[48,128,128]{2,1,0:T(8,128)(2,1)S(1)}, bf16[48,128,128]{2,1,0:T(8,128)(2,1)S(1)}) custom-call(s32[48]{0:T(128)S(1)} %convert_element_type.42.used_ref, s32[48]{0:T(128)S(1)} %get-tuple-element.22.owner_ref, s32[48]{0:T(128)S(1)} %get-tuple-element.21.column_ref, s32[4]{0:T(128)S(1)} %copy-done.7, ...), custom_call_target="tpu_custom_call" | custom-call | flops 4026531840 | bytes 6029312 | tf_op jit(solution)/shard_map/pallas_call | solution.py:160
  124.0 1.1 copy-done.4
  125.2 1.2 copy-done.5
  126.3 1.2 copy-done.6
  127.5 52.8 %shard_map.142 = (bf16[8,128,768]{2,1,0:T(8,128)(2,1)}, bf16[4,12,128,128]{3,2,1,0:T(8,128)(2,1)}, bf16[4,12,128,128]{3,2,1,0:T(8,128)(2,1)}) custom-call(bf16[1024,768]{1,0:T(8,128)(2,1)} %copy-done.4, bf16[48,128,128]{2,1,0:T(8,128)(2,1)} %copy-done.5, bf16[48,128,128]{2,1,0:T(8,128)(2,1)} %copy-done.6), custom_call_target="tpu_custom_call" | custom-call | tf_op jit(solution)/shard_map/pallas_call | solution.py:311
  180.3 1.4 copy-done.1
  181.7 1.4 copy-done.2
  183.1 1.4 copy-done.3
  184.5 2.5 %shard_map.143 = (bf16[128,640]{1,0:T(8,128)(2,1)}, bf16[12,128,128]{2,1,0:T(8,128)(2,1)}, bf16[12,128,128]{2,1,0:T(8,128)(2,1)}) custom-call(s32[12]{0:T(128)S(1)} %select_reduce_fusion.owner_ref, bf16[8,128,768]{2,1,0:T(8,128)(2,1)S(1)} %copy-done.1, bf16[4,12,128,128]{3,2,1,0:T(8,128)(2,1)S(1)} %copy-done.2, bf16[4,12,128,128]{3,2,1,0:T(8,128)(2,1)S(1)} %copy-done.3), custom_call_target="tpu_custom_call" | custom-call | tf_op jit(solution)/shard_map/pallas_call | solution.py:216
  (33 shorter events, 3.3 us)
Async XLA Ops:
  0.6 1.3 copy-start
  35.0 2.1 %copy-start.8 = (bf16[8,128,640]{2,1,0:T(8,128)(2,1)S(1)}, bf16[8,128,640]{2,1,0:T(8,128)(2,1)}, u32[]{:S(2)}) copy-start(bf16[8,128,640]{2,1,0:T(8,128)(2,1)} %shard_map.139) | copy-start | bytes 3932164
  35.0 2.1 %copy-start.9 = (bf16[5120,128]{1,0:T(8,128)(2,1)S(1)}, bf16[5120,128]{1,0:T(8,128)(2,1)}, u32[]{:S(2)}) copy-start(bf16[5120,128]{1,0:T(8,128)(2,1)} %param.15) | copy-start | bytes 3932164
  90.9 1.2 copy-start.7
  124.0 1.2 copy-start.4
  125.2 1.2 copy-start.5
  126.3 1.2 copy-start.6
  180.3 1.4 copy-start.1
  181.7 1.4 copy-start.2
  183.1 1.4 copy-start.3

commit v10 on v9

--- a/solution.py
+++ b/solution.py
@@ -67,45 +67,26 @@
     used_ref, owner_ref, column_ref, clen_ref, start_ref, req_ref, q_ref, fresh_ref, kc_ref, vc_ref,
     o_ref, nk_ref, nv_ref, m_sc, l_sc, acc_sc, *, q_heads, head_dim
 ):
-    i = pl.program_id(0)
     r = req_ref[0]
     rows = q_ref.shape[0]
     block_size = kc_ref.shape[1]
-
-    @pl.when(i == 0)
-    def _init():
-        m_sc[...] = jnp.full(m_sc.shape, NEG_FILL, jnp.float32)
-        l_sc[...] = jnp.zeros(l_sc.shape, jnp.float32)
-        acc_sc[...] = jnp.zeros(acc_sc.shape, jnp.float32)
-
-    active = (used_ref[i] == 1) & (owner_ref[i] == r)
-
-    @pl.when(jnp.logical_not(active))
-    def _keep():
-        nk_ref[i] = kc_ref[i]
-        nv_ref[i] = vc_ref[i]
-
-    @pl.when(active)
-    def _work():
-        keys, values = merged_block(
-            i, used_ref, owner_ref, column_ref, clen_ref, start_ref, fresh_ref, kc_ref, vc_ref, rows
-        )
-        nk_ref[i] = keys
-        nv_ref[i] = values
-        query_pos = clen_ref[r] + lax.broadcasted_iota(jnp.int32, (rows, block_size), 0)
-        key_pos = column_ref[i] * block_size + lax.broadcasted_iota(
-            jnp.int32, (rows, block_size), 1
-        )
-        allowed = key_pos <= query_pos
+    m_sc[...] = jnp.full(m_sc.shape, NEG_FILL, jnp.float32)
+    l_sc[...] = jnp.zeros(l_sc.shape, jnp.float32)
+    acc_sc[...] = jnp.zeros(acc_sc.shape, jnp.float32)
+
+    def attend_heads(keys, values, allowed):
         for g in range(q_heads):
             queries = q_ref[:, g * head_dim : (g + 1) * head_dim]
             score = lax.dot_general(
                 queries, keys, (((1,), (1,)), ((), ())), preferred_element_type=jnp.float32
             ) / math.sqrt(head_dim)
-            score = jnp.where(allowed, score, NEG_FILL)
+            if allowed is not None:
+                score = jnp.where(allowed, score, NEG_FILL)
             top = m_sc[g]
             new_top = jnp.maximum(top, jnp.max(score, axis=1, keepdims=True))
-            weights = jnp.where(allowed, jnp.exp(score - new_top), 0.0)
+            weights = jnp.exp(score - new_top)
+            if allowed is not None:
+                weights = jnp.where(allowed, weights, 0.0)
             factor = jnp.exp(top - new_top)
             l_sc[g] = l_sc[g] * factor + jnp.sum(weights, axis=1, keepdims=True)
             acc_sc[g] = acc_sc[g] * factor + jnp.dot(
@@ -113,19 +94,50 @@
             )
             m_sc[g] = new_top
 
-    @pl.when(i == pl.num_programs(0) - 1)
-    def _finish():
-        lane = lax.broadcasted_iota(jnp.int32, (rows, head_dim), 1)
-        stats = jnp.zeros((rows, head_dim), jnp.float32)
-        for g in range(q_heads):
-            top = m_sc[g]
-            valid = top > NEG_FILL / 2
-            ref = jnp.where(valid, top.astype(jnp.bfloat16).astype(jnp.float32), NEG_FILL)
-            factor = jnp.where(valid, jnp.exp(top - ref), 0.0)
-            o_ref[:, g * head_dim : (g + 1) * head_dim] = (acc_sc[g] * factor).astype(o_ref.dtype)
-            stats = jnp.where(lane == g, l_sc[g] * factor, stats)
-            stats = jnp.where(lane == q_heads + g, ref, stats)
-        o_ref[:, q_heads * head_dim :] = stats.astype(o_ref.dtype)
+    def visit(i, carry):
+        active = (used_ref[i] == 1) & (owner_ref[i] == r)
+
+        @pl.when(jnp.logical_not(active))
+        def _keep():
+            nk_ref[i] = kc_ref[i]
+            nv_ref[i] = vc_ref[i]
+
+        @pl.when(active)
+        def _work():
+            keys, values = merged_block(
+                i, used_ref, owner_ref, column_ref, clen_ref, start_ref, fresh_ref, kc_ref, vc_ref, rows
+            )
+            nk_ref[i] = keys
+            nv_ref[i] = values
+            seen = column_ref[i] * block_size + block_size - 1 <= clen_ref[r]
+
+            @pl.when(seen)
+            def _all():
+                attend_heads(keys, values, None)
+
+            @pl.when(jnp.logical_not(seen))
+            def _masked():
+                query_pos = clen_ref[r] + lax.broadcasted_iota(jnp.int32, (rows, block_size), 0)
+                key_pos = column_ref[i] * block_size + lax.broadcasted_iota(
+                    jnp.int32, (rows, block_size), 1
+                )
+                attend_heads(keys, values, key_pos <= query_pos)
+
+        return carry
+
+    lax.fori_loop(0, kc_ref.shape[0], visit, 0)
+
+    lane = lax.broadcasted_iota(jnp.int32, (rows, head_dim), 1)
+    stats = jnp.zeros((rows, head_dim), jnp.float32)
+    for g in range(q_heads):
+        top = m_sc[g]
+        valid = top > NEG_FILL / 2
+        ref = jnp.where(valid, top.astype(jnp.bfloat16).astype(jnp.float32), NEG_FILL)
+        factor = jnp.where(valid, jnp.exp(top - ref), 0.0)
+        o_ref[:, g * head_dim : (g + 1) * head_dim] = (acc_sc[g] * factor).astype(o_ref.dtype)
+        stats = jnp.where(lane == g, l_sc[g] * factor, stats)
+        stats = jnp.where(lane == q_heads + g, ref, stats)
+    o_ref[:, q_heads * head_dim :] = stats.astype(o_ref.dtype)
 
 
 def block_meta(block_table, block_ids, cached_len, block_size, fresh_len):
@@ -142,7 +154,7 @@
     block = pl.BlockSpec(keys.shape, lambda i, *_: (0, 0, 0))
     grid_spec = pltpu.PrefetchScalarGridSpec(
         num_scalar_prefetch=6,
-        grid=(n_blocks,),
+        grid=(1,),
         in_specs=[
             pl.BlockSpec((span, q_width), lambda i, *_: (0, 0)),
             pl.BlockSpec(fresh_rows.shape, lambda i, *_: (0, 0)),

time: 188 us -> 178 us (0.947)
  Pallas kernels: 157 us -> 147 us
    pallas_call x1, Pallas kernels: 31.9 us -> 18.4 us  [attend(): pl.pallas_call(functools.partial(attention_kernel, q_heads=q_heads, head_...]
    pallas_call x3, Pallas kernels: 122 us -> 126 us  [multi_exchange(): pl.pallas_call(functools.partial(multi_exchange_kernel, specs=tuple(specs...]
where the time goes in v10:
time: 178 us; the launch traced here: 177 us
  Pallas kernels  147 us (83%)
  local copies, waits for them, and re-layouts  11.5 us (6%)
  other arithmetic  11.4 us (6%)
  matrix products  6.86 us (4%)
    pallas_call x3, Pallas kernels, multi_exchange(): pl.pallas_call(functools.partial(multi_exchange_kernel, specs=tuple(specs...  126 us
    pallas_call x1, Pallas kernels, attend(): pl.pallas_call(functools.partial(attention_kernel, q_heads=q_heads, head_...  18.4 us
    unnamed x20, local copies, waits for them, and re-layouts  7.84 us
    dot_general x3, matrix products, project(): lax.dot_general(normed, weight.reshape(kv_n, feat, weight.shape[1]), (((0...  6.86 us

profile of v10, /device:TPU:1, one launch (start us, length us, event | category | flops | bytes accessed | tf_op | source)
XLA Modules:
  0.0 177.4 jit_solution(12291839674580421806)
XLA Ops:
  0.7 1.1 select_reduce_fusion.owner_ref
  3.3 0.7 select_reduce_fusion.1
  4.2 0.9 compare_reduce_fusion
  5.1 0.9 fusion.9
  6.0 1.4 fusion.28
  7.4 2.5 %fusion.23.start_ref = s32[48]{0:T(128)S(1)} fusion(s32[48]{0:T(128)S(1)} %get-tuple-element.22.owner_ref, s32[48]{0:T(128)S(1)} %get-tuple-element.21.column_ref, s32[]{:T(128)} %bitcast.1, s32[]{:T(128)} %bitcast.2, s32[]{:T(128)} %bitcast.4, s32[]{:T(128)} %bitcast.3), kind=kLoop, calls=%fused_computation.58 | loop fusion | flops 624 | bytes 592 | tf_op jit(solution)/shard_map/jit(clip)/min | solution.py:146
  9.9 0.7 convert_element_type.45
  10.6 0.7 reshape.248
  11.5 21.8 %shard_map.139 = bf16[8,128,640]{2,1,0:T(8,128)(2,1)} custom-call(bf16[128,640]{1,0:T(8,128)(2,1)} %refs_0_.1), custom_call_target="tpu_custom_call" | custom-call | tf_op jit(solution)/shard_map/pallas_call | solution.py:323
  33.3 1.7 fusion
  35.0 2.1 %fusion.7 = bf16[128,128]{1,0:T(8,128)(2,1)S(1)} fusion(bf16[8,640,128]{2,1,0:T(8,128)(2,1)S(1)} %bitcast.48, f32[128]{0:T(128)S(1)} %convert_element_type.49, bf16[8,128,640]{2,1,0:T(8,128)(2,1)} %shard_map.139, f32[8,640]{1,0:T(8,128)S(1)} %reshape.248, f32[128]{0:T(128)S(1)} %add_rsqrt_fusion), kind=kOutput, calls=%fused_computation.12 | convolution fusion | flops 170426368 | bytes 2675712 | tf_op jit(solution)/shard_map/dot_general | solution.py:374
  37.7 4.2 %fusion.3 = f32[128,640]{1,0:T(8,128)S(1)} fusion(bf16[8,640,640]{2,1,0:T(8,128)(2,1)} %bitcast.53, f32[640]{0:T(1024)S(1)} %convert_element_type.45, bf16[8,128,640]{2,1,0:T(8,128)(2,1)S(1)} %copy-done.8, f32[8,640]{1,0:T(8,128)S(1)} %reshape.248, f32[128]{0:T(128)S(1)} %add_rsqrt_fusion), kind=kOutput, calls=%fused_computation.6 | convolution fusion | flops 841564160 | bytes 8215552 | tf_op jit(solution)/shard_map/dot_general | solution.py:374
  42.6 0.8 pad_maximum_fusion.refs_0_
  43.4 47.5 %shard_map.140 = (bf16[8,128,896]{2,1,0:T(8,128)(2,1)}, bf16[4,12,128,128]{3,2,1,0:T(8,128)(2,1)}, bf16[4,12,128,128]{3,2,1,0:T(8,128)(2,1)}) custom-call(bf16[128,896]{1,0:T(8,128)(2,1)} %pad_maximum_fusion.refs_0_, bf16[12,128,128]{2,1,0:T(8,128)(2,1)} %refs_1_.1, bf16[12,128,128]{2,1,0:T(8,128)(2,1)} %refs_2_.1), custom_call_target="tpu_custom_call" | custom-call | tf_op jit(solution)/shard_map/pallas_call | solution.py:323
  90.9 1.1 slice.29
  92.1 18.4 %shard_map.141 = (bf16[1024,768]{1,0:T(8,128)(2,1)S(1)}, bf16[48,128,128]{2,1,0:T(8,128)(2,1)S(1)}, bf16[48,128,128]{2,1,0:T(8,128)(2,1)S(1)}) custom-call(s32[48]{0:T(128)S(1)} %convert_element_type.42.used_ref, s32[48]{0:T(128)S(1)} %get-tuple-element.22.owner_ref, s32[48]{0:T(128)S(1)} %get-tuple-element.21.column_ref, s32[4]{0:T(128)S(1)} %copy-done.7, ...), custom_call_target="tpu_custom_call" | custom-call | flops 4026531840 | bytes 6029312 | tf_op jit(solution)/shard_map/pallas_call | solution.py:172
  110.5 1.1 copy-done.4
  111.7 1.2 copy-done.5
  112.8 1.2 copy-done.6
  114.0 56.6 %shard_map.142 = (bf16[8,128,768]{2,1,0:T(8,128)(2,1)}, bf16[4,12,128,128]{3,2,1,0:T(8,128)(2,1)}, bf16[4,12,128,128]{3,2,1,0:T(8,128)(2,1)}) custom-call(bf16[1024,768]{1,0:T(8,128)(2,1)} %copy-done.4, bf16[48,128,128]{2,1,0:T(8,128)(2,1)} %copy-done.5, bf16[48,128,128]{2,1,0:T(8,128)(2,1)} %copy-done.6), custom_call_target="tpu_custom_call" | custom-call | tf_op jit(solution)/shard_map/pallas_call | solution.py:323
  170.7 1.4 copy-done.1
  172.1 1.4 copy-done.2
  173.5 1.4 copy-done.3
  174.9 2.5 %shard_map.143 = (bf16[128,640]{1,0:T(8,128)(2,1)}, bf16[12,128,128]{2,1,0:T(8,128)(2,1)}, bf16[12,128,128]{2,1,0:T(8,128)(2,1)}) custom-call(s32[12]{0:T(128)S(1)} %select_reduce_fusion.owner_ref, bf16[8,128,768]{2,1,0:T(8,128)(2,1)S(1)} %copy-done.1, bf16[4,12,128,128]{3,2,1,0:T(8,128)(2,1)S(1)} %copy-done.2, bf16[4,12,128,128]{3,2,1,0:T(8,128)(2,1)S(1)} %copy-done.3), custom_call_target="tpu_custom_call" | custom-call | tf_op jit(solution)/shard_map/pallas_call | solution.py:228
  (33 shorter events, 3.3 us)
Async XLA Ops:
  0.6 1.3 copy-start
  35.0 2.1 %copy-start.8 = (bf16[8,128,640]{2,1,0:T(8,128)(2,1)S(1)}, bf16[8,128,640]{2,1,0:T(8,128)(2,1)}, u32[]{:S(2)}) copy-start(bf16[8,128,640]{2,1,0:T(8,128)(2,1)} %shard_map.139) | copy-start | bytes 3932164
  35.0 2.1 %copy-start.9 = (bf16[5120,128]{1,0:T(8,128)(2,1)S(1)}, bf16[5120,128]{1,0:T(8,128)(2,1)}, u32[]{:S(2)}) copy-start(bf16[5120,128]{1,0:T(8,128)(2,1)} %param.15) | copy-start | bytes 3932164
  90.9 1.2 copy-start.7
  110.5 1.2 copy-start.4
  111.7 1.2 copy-start.5
  112.8 1.2 copy-start.6
  170.6 1.4 copy-start.1
  172.1 1.4 copy-start.2
  173.5 1.4 copy-start.3

commit v11 on v10

--- a/solution.py
+++ b/solution.py
@@ -240,6 +240,40 @@
 MESH = pl.DeviceIdType.MESH
 
 
+def forward_gather(src, dst, send_sem, recv_sem, own_sem, right, left, pos, m):
+    streams = [(right, m // 2, 0, -1), (left, (m - 1) // 2, m // 2, 1)]
+    own = pltpu.make_async_copy(src, dst.at[pos], own_sem)
+    own.start()
+
+    def hop(target, source, origin, sem):
+        return pltpu.make_async_remote_copy(
+            src_ref=source, dst_ref=dst.at[origin], send_sem=send_sem.at[sem],
+            recv_sem=recv_sem.at[sem], device_id=target, device_id_type=MESH,
+        )
+
+    sent = []
+    for target, n, s0, side in streams:
+        if n > 0:
+            first = hop(target, src, pos, s0)
+            first.start()
+            sent.append(first)
+    own.wait()
+    for k in range(1, m // 2):
+        for target, n, s0, side in streams:
+            if k < n:
+                origin = lax.rem(pos + m + side * k, m)
+                hop(target, src, origin, s0 + k - 1).wait_recv()
+                nxt = hop(target, dst.at[origin], origin, s0 + k)
+                nxt.start()
+                sent.append(nxt)
+    for target, n, s0, side in streams:
+        if n > 0:
+            origin = lax.rem(pos + m + side * n, m)
+            hop(target, src, origin, s0 + n - 1).wait_recv()
+    for copy in sent:
+        copy.wait_send()
+
+
 def multi_exchange_kernel(*refs, specs):
     n_total = sum(s[4] for s in specs)
     srcs, dsts = refs[:n_total], refs[n_total : 2 * n_total]
@@ -249,21 +283,29 @@
     def device(axis, index):
         return (index, here["blk"]) if axis == "kv" else (here["kv"], index)
 
-    groups = []
+    groups, forwards = [], []
     arr0, sem0 = 0, 0
-    for axis, m, stride, gather, n_arr in specs:
+    n_greet = 0
+    barrier = pltpu.get_barrier_semaphore()
+    for axis, m, stride, gather, n_arr, forward in specs:
         pos = lax.rem(here[axis] // stride, m)
         base = here[axis] - pos * stride
-        groups.append((axis, m, stride, gather, n_arr, pos, base, arr0, sem0))
+        if forward:
+            right = device(axis, base + lax.rem(pos + 1, m) * stride)
+            left = device(axis, base + lax.rem(pos + m - 1, m) * stride)
+            forwards.append((right, left, pos, m, arr0, sem0))
+            for peer in [right, left][: min(2, m - 1)]:
+                pl.semaphore_signal(barrier, inc=1, device_id=peer, device_id_type=MESH)
+            n_greet += min(2, m - 1)
+        else:
+            groups.append((axis, m, stride, gather, n_arr, pos, base, arr0, sem0))
+            for k in range(1, m):
+                peer = base + lax.rem(pos + k, m) * stride
+                pl.semaphore_signal(barrier, inc=1, device_id=device(axis, peer), device_id_type=MESH)
+            n_greet += m - 1
         arr0 += n_arr
         sem0 += m * n_arr
-
-    barrier = pltpu.get_barrier_semaphore()
-    for axis, m, stride, gather, n_arr, pos, base, _, _ in groups:
-        for k in range(1, m):
-            peer = base + lax.rem(pos + k, m) * stride
-            pl.semaphore_signal(barrier, inc=1, device_id=device(axis, peer), device_id_type=MESH)
-    pl.semaphore_wait(barrier, sum(s[1] - 1 for s in specs))
+    pl.semaphore_wait(barrier, n_greet)
 
     def chunk(src, j, m, gather):
         if gather:
@@ -291,6 +333,11 @@
                 )
                 copy.start()
                 copies.append(copy)
+    for right, left, pos, m, a0, s0 in forwards:
+        forward_gather(
+            srcs[a0], dsts[a0], send_sem.at[pl.ds(s0, m)], recv_sem.at[pl.ds(s0, m)],
+            own_sem.at[a0], right, left, pos, m,
+        )
     for own in owns:
         own.wait()
     c = 0
@@ -313,8 +360,10 @@
 
 def multi_exchange(groups, collective_id):
     specs, arrays, shapes = [], [], []
-    for axis, m, stride, gather, arrs in groups:
-        specs.append((axis, m, stride, gather, len(arrs)))
+    for group in groups:
+        axis, m, stride, gather, arrs = group[:5]
+        forward = len(group) > 5 and group[5]
+        specs.append((axis, m, stride, gather, len(arrs), forward))
         for x in arrs:
             rows = x.shape[0] if gather else x.shape[0] // m
             arrays.append(x)
@@ -399,7 +448,7 @@
     q_width = q_heads * head_dim
     packed = jnp.concatenate([fresh_queries, fresh_keys, fresh_values], axis=1)
     ring_packed, col_keys, col_values = multi_exchange(
-        [("blk", ring, 1, True, [packed]), ("blk", cols, ring, True, [key_cache, value_cache])], 1
+        [("blk", ring, 1, True, [packed], True), ("blk", cols, ring, True, [key_cache, value_cache])], 1
     )
     ring_packed = ring_packed.reshape(span, packed.shape[1])
     fresh_rows = jnp.pad(

time: 178 us -> 191 us (1.073)
  Pallas kernels: 147 us -> 160 us
    pallas_call x3, Pallas kernels: 126 us -> 142 us  [multi_exchange(): pl.pallas_call(functools.partial(multi_exchange_kernel, specs=tuple(specs...]
    pallas_call x1, Pallas kernels: 18.4 us -> 15.8 us  [attend(): pl.pallas_call(functools.partial(attention_kernel, q_heads=q_heads, head_...]
where the time goes in v11:
time: 191 us
  Pallas kernels  160 us (84%)
  local copies, waits for them, and re-layouts  11.5 us (6%)
  other arithmetic  11.4 us (6%)
  matrix products  6.86 us (4%)
    pallas_call x3, Pallas kernels, multi_exchange(): pl.pallas_call(functools.partial(multi_exchange_kernel, specs=tuple(specs...  142 us
    pallas_call x1, Pallas kernels, attend(): pl.pallas_call(functools.partial(attention_kernel, q_heads=q_heads, head_...  15.8 us
    unnamed x20, local copies, waits for them, and re-layouts  7.84 us
    dot_general x3, matrix products, project(): lax.dot_general(normed, weight.reshape(kv_n, feat, weight.shape[1]), (((0...  6.86 us

profile of v11, /device:TPU:1, one launch (start us, length us, event | category | flops | bytes accessed | tf_op | source)
XLA Modules:
  0.0 190.6 jit_solution(17053054644194344479)
XLA Ops:
  0.7 1.1 select_reduce_fusion.owner_ref
  3.3 0.7 select_reduce_fusion.1
  4.2 0.9 compare_reduce_fusion
  5.1 0.9 fusion.9
  6.0 1.4 fusion.28
  7.4 2.5 %fusion.23.start_ref = s32[48]{0:T(128)S(1)} fusion(s32[48]{0:T(128)S(1)} %get-tuple-element.22.owner_ref, s32[48]{0:T(128)S(1)} %get-tuple-element.21.column_ref, s32[]{:T(128)} %bitcast.1, s32[]{:T(128)} %bitcast.2, s32[]{:T(128)} %bitcast.4, s32[]{:T(128)} %bitcast.3), kind=kLoop, calls=%fused_computation.58 | loop fusion | flops 624 | bytes 592 | tf_op jit(solution)/shard_map/jit(clip)/min | solution.py:146
  9.9 0.7 convert_element_type.45
  10.6 0.7 reshape.248
  11.5 21.8 %shard_map.139 = bf16[8,128,640]{2,1,0:T(8,128)(2,1)} custom-call(bf16[128,640]{1,0:T(8,128)(2,1)} %refs_0_.1), custom_call_target="tpu_custom_call" | custom-call | tf_op jit(solution)/shard_map/pallas_call | solution.py:372
  33.3 1.7 fusion
  35.0 2.1 %fusion.7 = bf16[128,128]{1,0:T(8,128)(2,1)S(1)} fusion(bf16[8,640,128]{2,1,0:T(8,128)(2,1)S(1)} %bitcast.48, f32[128]{0:T(128)S(1)} %convert_element_type.49, bf16[8,128,640]{2,1,0:T(8,128)(2,1)} %shard_map.139, f32[8,640]{1,0:T(8,128)S(1)} %reshape.248, f32[128]{0:T(128)S(1)} %add_rsqrt_fusion), kind=kOutput, calls=%fused_computation.12 | convolution fusion | flops 170426368 | bytes 2675712 | tf_op jit(solution)/shard_map/dot_general | solution.py:423
  37.7 4.2 %fusion.3 = f32[128,640]{1,0:T(8,128)S(1)} fusion(bf16[8,640,640]{2,1,0:T(8,128)(2,1)} %bitcast.53, f32[640]{0:T(1024)S(1)} %convert_element_type.45, bf16[8,128,640]{2,1,0:T(8,128)(2,1)S(1)} %copy-done.8, f32[8,640]{1,0:T(8,128)S(1)} %reshape.248, f32[128]{0:T(128)S(1)} %add_rsqrt_fusion), kind=kOutput, calls=%fused_computation.6 | convolution fusion | flops 841564160 | bytes 8215552 | tf_op jit(solution)/shard_map/dot_general | solution.py:423
  42.6 0.8 pad_maximum_fusion.refs_0_
  43.4 58.5 %shard_map.140 = (bf16[8,128,896]{2,1,0:T(8,128)(2,1)}, bf16[4,12,128,128]{3,2,1,0:T(8,128)(2,1)}, bf16[4,12,128,128]{3,2,1,0:T(8,128)(2,1)}) custom-call(bf16[128,896]{1,0:T(8,128)(2,1)} %pad_maximum_fusion.refs_0_, bf16[12,128,128]{2,1,0:T(8,128)(2,1)} %refs_1_.1, bf16[12,128,128]{2,1,0:T(8,128)(2,1)} %refs_2_.1), custom_call_target="tpu_custom_call" | custom-call | tf_op jit(solution)/shard_map/pallas_call | solution.py:372
  101.9 1.1 slice.29
  103.1 15.8 %shard_map.141 = (bf16[1024,768]{1,0:T(8,128)(2,1)S(1)}, bf16[48,128,128]{2,1,0:T(8,128)(2,1)S(1)}, bf16[48,128,128]{2,1,0:T(8,128)(2,1)S(1)}) custom-call(s32[48]{0:T(128)S(1)} %convert_element_type.42.used_ref, s32[48]{0:T(128)S(1)} %get-tuple-element.22.owner_ref, s32[48]{0:T(128)S(1)} %get-tuple-element.21.column_ref, s32[4]{0:T(128)S(1)} %copy-done.7, ...), custom_call_target="tpu_custom_call" | custom-call | flops 4026531840 | bytes 6029312 | tf_op jit(solution)/shard_map/pallas_call | solution.py:172
  118.9 1.1 copy-done.4
  120.1 1.2 copy-done.5
  121.2 1.2 copy-done.6
  122.4 61.5 %shard_map.142 = (bf16[8,128,768]{2,1,0:T(8,128)(2,1)}, bf16[4,12,128,128]{3,2,1,0:T(8,128)(2,1)}, bf16[4,12,128,128]{3,2,1,0:T(8,128)(2,1)}) custom-call(bf16[1024,768]{1,0:T(8,128)(2,1)} %copy-done.4, bf16[48,128,128]{2,1,0:T(8,128)(2,1)} %copy-done.5, bf16[48,128,128]{2,1,0:T(8,128)(2,1)} %copy-done.6), custom_call_target="tpu_custom_call" | custom-call | tf_op jit(solution)/shard_map/pallas_call | solution.py:372
  183.9 1.4 copy-done.1
  185.3 1.4 copy-done.2
  186.7 1.4 copy-done.3
  188.1 2.5 %shard_map.143 = (bf16[128,640]{1,0:T(8,128)(2,1)}, bf16[12,128,128]{2,1,0:T(8,128)(2,1)}, bf16[12,128,128]{2,1,0:T(8,128)(2,1)}) custom-call(s32[12]{0:T(128)S(1)} %select_reduce_fusion.owner_ref, bf16[8,128,768]{2,1,0:T(8,128)(2,1)S(1)} %copy-done.1, bf16[4,12,128,128]{3,2,1,0:T(8,128)(2,1)S(1)} %copy-done.2, bf16[4,12,128,128]{3,2,1,0:T(8,128)(2,1)S(1)} %copy-done.3), custom_call_target="tpu_custom_call" | custom-call | tf_op jit(solution)/shard_map/pallas_call | solution.py:228
  (33 shorter events, 3.3 us)
Async XLA Ops:
  0.6 1.3 copy-start
  35.0 2.1 %copy-start.8 = (bf16[8,128,640]{2,1,0:T(8,128)(2,1)S(1)}, bf16[8,128,640]{2,1,0:T(8,128)(2,1)}, u32[]{:S(2)}) copy-start(bf16[8,128,640]{2,1,0:T(8,128)(2,1)} %shard_map.139) | copy-start | bytes 3932164
  35.0 2.1 %copy-start.9 = (bf16[5120,128]{1,0:T(8,128)(2,1)S(1)}, bf16[5120,128]{1,0:T(8,128)(2,1)}, u32[]{:S(2)}) copy-start(bf16[5120,128]{1,0:T(8,128)(2,1)} %param.15) | copy-start | bytes 3932164
  101.9 1.2 copy-start.7
  118.9 1.2 copy-start.4
  120.1 1.2 copy-start.5
  121.2 1.2 copy-start.6
  183.8 1.4 copy-start.1
  185.3 1.4 copy-start.2
  186.7 1.4 copy-start.3

commit v12 on v10

--- a/solution.py
+++ b/solution.py
@@ -97,18 +97,26 @@
     def visit(i, carry):
         active = (used_ref[i] == 1) & (owner_ref[i] == r)
 
-        @pl.when(jnp.logical_not(active))
-        def _keep():
-            nk_ref[i] = kc_ref[i]
-            nv_ref[i] = vc_ref[i]
-
         @pl.when(active)
         def _work():
-            keys, values = merged_block(
-                i, used_ref, owner_ref, column_ref, clen_ref, start_ref, fresh_ref, kc_ref, vc_ref, rows
-            )
-            nk_ref[i] = keys
-            nv_ref[i] = values
+            has_new = column_ref[i] * block_size + block_size - 1 >= clen_ref[r]
+
+            @pl.when(has_new)
+            def _merge():
+                keys, values = merged_block(
+                    i, used_ref, owner_ref, column_ref, clen_ref, start_ref, fresh_ref, kc_ref,
+                    vc_ref, rows,
+                )
+                nk_ref[i] = keys
+                nv_ref[i] = values
+
+            @pl.when(jnp.logical_not(has_new))
+            def _cached():
+                nk_ref[i] = kc_ref[i]
+                nv_ref[i] = vc_ref[i]
+
+            keys = nk_ref[i]
+            values = nv_ref[i]
             seen = column_ref[i] * block_size + block_size - 1 <= clen_ref[r]
 
             @pl.when(seen)
@@ -186,7 +194,7 @@
     )(*meta, request, queries, fresh_rows, keys, values)
 
 
-def combine_kernel(owner_ref, got_ref, bk_ref, bv_ref, out_ref, nk_ref, nv_ref, *, q_heads, head_dim):
+def combine_kernel(used_ref, owner_ref, got_ref, bk_ref, bv_ref, kc_ref, vc_ref, out_ref, nk_ref, nv_ref, *, q_heads, head_dim):
     ring = got_ref.shape[0]
     q_width = q_heads * head_dim
     stats = [got_ref[s, :, q_width:].astype(jnp.float32) for s in range(ring)]
@@ -204,11 +212,11 @@
             total = total + stats[s][:, g : g + 1] * factor
         out_ref[:, g * head_dim : (g + 1) * head_dim] = (weighted / total).astype(out_ref.dtype)
     for b in range(nk_ref.shape[0]):
-        nk_ref[b] = bk_ref[owner_ref[b], b]
-        nv_ref[b] = bv_ref[owner_ref[b], b]
-
-
-def combine(owner, got, back_k, back_v, q_heads, head_dim):
+        nk_ref[b] = jnp.where(used_ref[b] == 1, bk_ref[owner_ref[b], b], kc_ref[b])
+        nv_ref[b] = jnp.where(used_ref[b] == 1, bv_ref[owner_ref[b], b], vc_ref[b])
+
+
+def combine(used, owner, got, back_k, back_v, key_cache, value_cache, q_heads, head_dim):
     ring, rows, _ = got.shape
     nb_dev = back_k.shape[1]
 
@@ -216,9 +224,9 @@
         return pl.BlockSpec(x.shape, lambda i, *_: (0,) * x.ndim)
 
     grid_spec = pltpu.PrefetchScalarGridSpec(
-        num_scalar_prefetch=1,
+        num_scalar_prefetch=2,
         grid=(1,),
-        in_specs=[whole(got), whole(back_k), whole(back_v)],
+        in_specs=[whole(got), whole(back_k), whole(back_v), whole(key_cache), whole(value_cache)],
         out_specs=[
             pl.BlockSpec((rows, q_heads * head_dim), lambda i, *_: (0, 0)),
             pl.BlockSpec(back_k.shape[1:], lambda i, *_: (0, 0, 0)),
@@ -234,7 +242,7 @@
             jax.ShapeDtypeStruct(back_v.shape[1:], back_v.dtype),
         ),
         compiler_params=pltpu.CompilerParams(vmem_limit_bytes=32 * 1024 * 1024),
-    )(owner, got, back_k, back_v)
+    )(used, owner, got, back_k, back_v, key_cache, value_cache)
 
 
 MESH = pl.DeviceIdType.MESH
@@ -423,13 +431,17 @@
     got, back_k, back_v = multi_exchange(
         [("blk", ring, 1, False, [parts]), ("blk", cols, ring, False, [merged_k, merged_v])], 2
     )
-    local_ids = device * nb_dev + jnp.arange(nb_dev, dtype=jnp.int32)
-    _, owner, _ = block_owners(block_table, local_ids)
+    mine = (device // ring) * nb_dev
+    used = lax.dynamic_slice_in_dim(meta[0], mine, nb_dev)
+    owner = lax.dynamic_slice_in_dim(meta[1], mine, nb_dev)
     attn_out, new_k, new_v = combine(
+        used,
         owner,
         got,
         back_k.reshape(cols, nb_dev, block_size, kv_width),
         back_v.reshape(cols, nb_dev, block_size, kv_width),
+        key_cache,
+        value_cache,
         q_heads,
         head_dim,
     )

time: 178 us -> 169 us (0.949)
  other arithmetic: 11.4 us -> 7.01 us
  Pallas kernels: 147 us -> 144 us
    pallas_call x3, Pallas kernels: 126 us -> 124 us  [multi_exchange(): pl.pallas_call(functools.partial(multi_exchange_kernel, specs=tuple(specs...]
    unnamed x20 -> x34, local copies, waits for them, and re-layouts: 7.84 us -> 8.98 us
where the time goes in v12:
time: 169 us
  Pallas kernels  144 us (85%)
  local copies, waits for them, and re-layouts  11.3 us (7%)
  other arithmetic  7.01 us (4%)
  matrix products  5.77 us (3%)
    pallas_call x3, Pallas kernels, multi_exchange(): pl.pallas_call(functools.partial(multi_exchange_kernel, specs=tuple(specs...  124 us
    pallas_call x1, Pallas kernels, attend(): pl.pallas_call(functools.partial(attention_kernel, q_heads=q_heads, head_...  17.7 us
    unnamed x34, local copies, waits for them, and re-layouts  8.98 us
    dot_general x3, matrix products, project(): lax.dot_general(normed, weight.reshape(kv_n, feat, weight.shape[1]), (((0...  5.77 us

profile of v12, /device:TPU:1, one launch (start us, length us, event | category | flops | bytes accessed | tf_op | source)
XLA Modules:
  0.0 169.0 jit_solution(5693560596172402100)
XLA Ops:
  0.7 0.8 select_reduce_fusion
  1.8 21.8 %shard_map.139 = bf16[8,128,640]{2,1,0:T(8,128)(2,1)} custom-call(bf16[128,640]{1,0:T(8,128)(2,1)} %refs_0_.1), custom_call_target="tpu_custom_call" | custom-call | tf_op jit(solution)/shard_map/pallas_call | solution.py:331
  23.5 1.7 fusion
  25.3 4.5 %fusion.3 = f32[128,640]{1,0:T(8,128)S(1)} fusion(bf16[8,640,640]{2,1,0:T(8,128)(2,1)} %bitcast.53, f32[640]{0:T(1024)S(1)} %convert_element_type.45, bf16[8,128,640]{2,1,0:T(8,128)(2,1)} %shard_map.139, f32[8,640]{1,0:T(8,128)S(1)} %reshape.244, f32[128]{0:T(128)S(1)} %add_rsqrt_fusion), kind=kOutput, calls=%fused_computation.6 | convolution fusion | flops 841564160 | bytes 8215552 | tf_op jit(solution)/shard_map/dot_general | solution.py:382
  30.2 0.2 copy-done.15
  30.5 0.7 copy-done.10
  31.1 0.6 fusion.5
  31.8 0.3 fusion.19
  32.1 0.4 copy-done.14
  32.5 0.6 fusion.7
  33.1 0.8 pad_maximum_fusion.refs_0_
  33.9 47.5 %shard_map.140 = (bf16[8,128,896]{2,1,0:T(8,128)(2,1)}, bf16[4,12,128,128]{3,2,1,0:T(8,128)(2,1)}, bf16[4,12,128,128]{3,2,1,0:T(8,128)(2,1)}) custom-call(bf16[128,896]{1,0:T(8,128)(2,1)} %pad_maximum_fusion.refs_0_, bf16[12,128,128]{2,1,0:T(8,128)(2,1)} %kc_ref.1, bf16[12,128,128]{2,1,0:T(8,128)(2,1)} %vc_ref.1), custom_call_target="tpu_custom_call" | custom-call | tf_op jit(solution)/shard_map/pallas_call | solution.py:331
  81.4 1.1 slice.29
  83.0 0.6 fusion.28
  83.6 2.6 %fusion.23.start_ref = s32[48]{0:T(128)S(1)} fusion(s32[48]{0:T(128)S(1)} %get-tuple-element.22.owner_ref, s32[48]{0:T(128)S(1)} %get-tuple-element.21.column_ref, s32[]{:T(128)} %bitcast.1, s32[]{:T(128)} %bitcast.2, s32[]{:T(128)} %bitcast.4, s32[]{:T(128)} %bitcast.3), kind=kLoop, calls=%fused_computation.56 | loop fusion | flops 624 | bytes 592 | tf_op jit(solution)/shard_map/jit(clip)/min | solution.py:154
  86.4 17.7 %shard_map.141 = (bf16[1024,768]{1,0:T(8,128)(2,1)S(1)}, bf16[48,128,128]{2,1,0:T(8,128)(2,1)S(1)}, bf16[48,128,128]{2,1,0:T(8,128)(2,1)S(1)}) custom-call(s32[48]{0:T(128)S(1)} %convert_element_type.42.used_ref, s32[48]{0:T(128)S(1)} %get-tuple-element.22.owner_ref, s32[48]{0:T(128)S(1)} %get-tuple-element.21.column_ref, s32[4]{0:T(128)S(1)} %copy-done.9, ...), custom_call_target="tpu_custom_call" | custom-call | flops 4026531840 | bytes 6029312 | tf_op jit(solution)/shard_map/pallas_call | solution.py:180
  104.1 1.1 copy-done.6
  105.3 1.2 copy-done.7
  106.4 1.2 copy-done.8
  107.6 54.3 %shard_map.142 = (bf16[8,128,768]{2,1,0:T(8,128)(2,1)}, bf16[4,12,128,128]{3,2,1,0:T(8,128)(2,1)}, bf16[4,12,128,128]{3,2,1,0:T(8,128)(2,1)}) custom-call(bf16[1024,768]{1,0:T(8,128)(2,1)} %copy-done.6, bf16[48,128,128]{2,1,0:T(8,128)(2,1)} %copy-done.7, bf16[48,128,128]{2,1,0:T(8,128)(2,1)} %copy-done.8), custom_call_target="tpu_custom_call" | custom-call | tf_op jit(solution)/shard_map/pallas_call | solution.py:331
  162.1 1.4 copy-done.3
  163.5 1.4 copy-done.4
  164.9 1.4 copy-done.5
  166.3 2.7 %shard_map.143 = (bf16[128,640]{1,0:T(8,128)(2,1)}, bf16[12,128,128]{2,1,0:T(8,128)(2,1)}, bf16[12,128,128]{2,1,0:T(8,128)(2,1)}) custom-call(s32[12]{0:T(128)S(1)} %dynamic_slice.6.used_ref, s32[12]{0:T(128)S(1)} %dynamic_slice.7.owner_ref, bf16[8,128,768]{2,1,0:T(8,128)(2,1)S(1)} %copy-done.3, bf16[4,12,128,128]{3,2,1,0:T(8,128)(2,1)S(1)} %copy-done.4, ...), custom_call_target="tpu_custom_call" | custom-call | tf_op jit(solution)/shard_map/pallas_call | solution.py:236
  (47 shorter events, 1.5 us)
Async XLA Ops:
  0.6 29.8 %copy-start = (bf16[5120,128]{1,0:T(8,128)(2,1)S(1)}, bf16[5120,128]{1,0:T(8,128)(2,1)}, u32[]{:S(2)}) copy-start(bf16[5120,128]{1,0:T(8,128)(2,1)} %param.15) | copy-start | bytes 3932164
  0.6 24.6 %copy-start.11 = (bf16[5120]{0:T(1024)(128)(2,1)S(1)}, bf16[5120]{0:T(1024)(128)(2,1)}, u32[]{:S(2)}) copy-start(bf16[5120]{0:T(1024)(128)(2,1)} %param.13) | copy-start | bytes 30724
  0.7 24.6 %copy-start.13 = (bf16[640]{0:T(1024)(128)(2,1)S(1)}, bf16[640]{0:T(1024)(128)(2,1)}, u32[]{:S(2)}) copy-start(bf16[640]{0:T(1024)(128)(2,1)} %param.17) | copy-start | bytes 3844
  29.8 0.7 copy-start.15
  29.8 1.3 copy-start.10
  31.1 1.0 copy-start.16
  31.1 1.3 copy-start.14
  81.4 1.4 copy-start.12
  81.4 1.6 copy-start.9
  104.1 1.2 copy-start.6
  105.2 1.2 copy-start.7
  106.4 1.2 copy-start.8
  107.6 54.5 %copy-start.1 = (bf16[12,128,128]{2,1,0:T(8,128)(2,1)S(1)}, bf16[12,128,128]{2,1,0:T(8,128)(2,1)}, u32[]{:S(2)}) copy-start(bf16[12,128,128]{2,1,0:T(8,128)(2,1)} %kc_ref.1) | copy-start | bytes 1179652
  107.6 54.5 %copy-start.2 = (bf16[12,128,128]{2,1,0:T(8,128)(2,1)S(1)}, bf16[12,128,128]{2,1,0:T(8,128)(2,1)}, u32[]{:S(2)}) copy-start(bf16[12,128,128]{2,1,0:T(8,128)(2,1)} %vc_ref.1) | copy-start | bytes 1179652
  162.1 1.4 copy-start.3
  163.5 1.4 copy-start.4
  164.9 1.4 copy-start.5

commit v13 on v12

--- a/solution.py
+++ b/solution.py
@@ -65,7 +65,7 @@
 
 def attention_kernel(
     used_ref, owner_ref, column_ref, clen_ref, start_ref, req_ref, q_ref, fresh_ref, kc_ref, vc_ref,
-    o_ref, nk_ref, nv_ref, m_sc, l_sc, acc_sc, *, q_heads, head_dim
+    o_hbm, nk_hbm, nv_hbm, o_ref, nk_ref, nv_ref, m_sc, l_sc, acc_sc, out_sem, *, q_heads, head_dim
 ):
     r = req_ref[0]
     rows = q_ref.shape[0]
@@ -146,6 +146,15 @@
         stats = jnp.where(lane == g, l_sc[g] * factor, stats)
         stats = jnp.where(lane == q_heads + g, ref, stats)
     o_ref[:, q_heads * head_dim :] = stats.astype(o_ref.dtype)
+    outs = [
+        pltpu.make_async_copy(o_ref, o_hbm, out_sem.at[0]),
+        pltpu.make_async_copy(nk_ref, nk_hbm, out_sem.at[1]),
+        pltpu.make_async_copy(nv_ref, nv_hbm, out_sem.at[2]),
+    ]
+    for copy in outs:
+        copy.start()
+    for copy in outs:
+        copy.wait()
 
 
 def block_meta(block_table, block_ids, cached_len, block_size, fresh_len):
@@ -169,11 +178,15 @@
             block,
             block,
         ],
-        out_specs=[pl.BlockSpec((span, out_width), lambda i, *_: (0, 0)), block, block],
+        out_specs=[pl.BlockSpec(memory_space=pl.ANY)] * 3,
         scratch_shapes=[
+            pltpu.VMEM((span, out_width), jnp.bfloat16),
+            pltpu.VMEM(keys.shape, keys.dtype),
+            pltpu.VMEM(values.shape, values.dtype),
             pltpu.VMEM((q_heads, span, head_dim), jnp.float32),
             pltpu.VMEM((q_heads, span, head_dim), jnp.float32),
             pltpu.VMEM((q_heads, span, head_dim), jnp.float32),
+            pltpu.SemaphoreType.DMA((3,)),
         ],
     )
     flops = n_blocks * span * q_heads * block_size * head_dim
@@ -194,7 +207,16 @@
     )(*meta, request, queries, fresh_rows, keys, values)
 
 
-def combine_kernel(used_ref, owner_ref, got_ref, bk_ref, bv_ref, kc_ref, vc_ref, out_ref, nk_ref, nv_ref, *, q_heads, head_dim):
+def combine_kernel(
+    used_ref, owner_ref, got_ref, bk_hbm, bv_hbm, kc_ref, vc_ref, out_ref, nk_ref, nv_ref, bk_ref, bv_ref,
+    sem, *, q_heads, head_dim
+):
+    fetches = []
+    for b in range(nk_ref.shape[0]):
+        for a, (src, dst) in enumerate(((bk_hbm, bk_ref), (bv_hbm, bv_ref))):
+            fetch = pltpu.make_async_copy(src.at[owner_ref[b], b], dst.at[b], sem.at[a, b])
+            fetch.start()
+            fetches.append(fetch)
     ring = got_ref.shape[0]
     q_width = q_heads * head_dim
     stats = [got_ref[s, :, q_width:].astype(jnp.float32) for s in range(ring)]
@@ -211,9 +233,11 @@
             weighted = weighted + part * factor
             total = total + stats[s][:, g : g + 1] * factor
         out_ref[:, g * head_dim : (g + 1) * head_dim] = (weighted / total).astype(out_ref.dtype)
+    for fetch in fetches:
+        fetch.wait()
     for b in range(nk_ref.shape[0]):
-        nk_ref[b] = jnp.where(used_ref[b] == 1, bk_ref[owner_ref[b], b], kc_ref[b])
-        nv_ref[b] = jnp.where(used_ref[b] == 1, bv_ref[owner_ref[b], b], vc_ref[b])
+        nk_ref[b] = jnp.where(used_ref[b] == 1, bk_ref[b], kc_ref[b])
+        nv_ref[b] = jnp.where(used_ref[b] == 1, bv_ref[b], vc_ref[b])
 
 
 def combine(used, owner, got, back_k, back_v, key_cache, value_cache, q_heads, head_dim):
@@ -226,11 +250,22 @@
     grid_spec = pltpu.PrefetchScalarGridSpec(
         num_scalar_prefetch=2,
         grid=(1,),
-        in_specs=[whole(got), whole(back_k), whole(back_v), whole(key_cache), whole(value_cache)],
+        in_specs=[
+            whole(got),
+            pl.BlockSpec(memory_space=pl.ANY),
+            pl.BlockSpec(memory_space=pl.ANY),
+            whole(key_cache),
+            whole(value_cache),
+        ],
         out_specs=[
             pl.BlockSpec((rows, q_heads * head_dim), lambda i, *_: (0, 0)),
             pl.BlockSpec(back_k.shape[1:], lambda i, *_: (0, 0, 0)),
             pl.BlockSpec(back_v.shape[1:], lambda i, *_: (0, 0, 0)),
+        ],
+        scratch_shapes=[
+            pltpu.VMEM(back_k.shape[1:], back_k.dtype),
+            pltpu.VMEM(back_v.shape[1:], back_v.dtype),
+            pltpu.SemaphoreType.DMA((2, nb_dev)),
         ],
     )
     return pl.pallas_call(

time: 169 us -> 170 us (level); the launches traced: 169 us -> 173 us
  Pallas kernels: 144 us -> 148 us
    pallas_call x1, Pallas kernels: 17.7 us -> 19.6 us  [attend(): pl.pallas_call(functools.partial(attention_kernel, q_heads=q_heads, head_...]
where the time goes in v13:
time: 170 us; the launch traced here: 173 us
  Pallas kernels  148 us (87%)
  local copies, waits for them, and re-layouts  11.3 us (7%)
  other arithmetic  7.01 us (4%)
  matrix products  5.77 us (3%)
    pallas_call x3, Pallas kernels, multi_exchange(): pl.pallas_call(functools.partial(multi_exchange_kernel, specs=tuple(specs...  124 us
    pallas_call x1, Pallas kernels, attend(): pl.pallas_call(functools.partial(attention_kernel, q_heads=q_heads, head_...  19.6 us
    unnamed x34, local copies, waits for them, and re-layouts  8.98 us
    dot_general x3, matrix products, project(): lax.dot_general(normed, weight.reshape(kv_n, feat, weight.shape[1]), (((0...  5.77 us
    pallas_call x1, Pallas kernels, combine(): pl.pallas_call(functools.partial(combine_kernel, q_heads=q_heads, head_di...  4.18 us

profile of v13, /device:TPU:1, one launch (start us, length us, event | category | flops | bytes accessed | tf_op | source)
XLA Modules:
  0.0 172.9 jit_solution(7183946549301767481)
XLA Ops:
  0.7 0.8 select_reduce_fusion
  1.8 21.8 %shard_map.139 = bf16[8,128,640]{2,1,0:T(8,128)(2,1)} custom-call(bf16[128,640]{1,0:T(8,128)(2,1)} %refs_0_.1), custom_call_target="tpu_custom_call" | custom-call | tf_op jit(solution)/shard_map/pallas_call | solution.py:366
  23.5 1.7 fusion
  25.3 4.5 %fusion.3 = f32[128,640]{1,0:T(8,128)S(1)} fusion(bf16[8,640,640]{2,1,0:T(8,128)(2,1)} %bitcast.53, f32[640]{0:T(1024)S(1)} %convert_element_type.45, bf16[8,128,640]{2,1,0:T(8,128)(2,1)} %shard_map.139, f32[8,640]{1,0:T(8,128)S(1)} %reshape.244, f32[128]{0:T(128)S(1)} %add_rsqrt_fusion), kind=kOutput, calls=%fused_computation.6 | convolution fusion | flops 841564160 | bytes 8215552 | tf_op jit(solution)/shard_map/dot_general | solution.py:417
  30.2 0.2 copy-done.15
  30.5 0.7 copy-done.10
  31.1 0.6 fusion.5
  31.8 0.3 fusion.19
  32.1 0.4 copy-done.14
  32.5 0.6 fusion.7
  33.1 0.8 pad_maximum_fusion.refs_0_
  33.9 47.5 %shard_map.140 = (bf16[8,128,896]{2,1,0:T(8,128)(2,1)}, bf16[4,12,128,128]{3,2,1,0:T(8,128)(2,1)}, bf16[4,12,128,128]{3,2,1,0:T(8,128)(2,1)}) custom-call(bf16[128,896]{1,0:T(8,128)(2,1)} %pad_maximum_fusion.refs_0_, bf16[12,128,128]{2,1,0:T(8,128)(2,1)} %kc_ref.1, bf16[12,128,128]{2,1,0:T(8,128)(2,1)} %vc_ref.1), custom_call_target="tpu_custom_call" | custom-call | tf_op jit(solution)/shard_map/pallas_call | solution.py:366
  81.4 1.1 slice.29
  83.0 0.6 fusion.28
  83.6 2.6 %fusion.23.start_ref = s32[48]{0:T(128)S(1)} fusion(s32[48]{0:T(128)S(1)} %get-tuple-element.22.owner_ref, s32[48]{0:T(128)S(1)} %get-tuple-element.21.column_ref, s32[]{:T(128)} %bitcast.1, s32[]{:T(128)} %bitcast.2, s32[]{:T(128)} %bitcast.4, s32[]{:T(128)} %bitcast.3), kind=kLoop, calls=%fused_computation.56 | loop fusion | flops 624 | bytes 592 | tf_op jit(solution)/shard_map/jit(clip)/min | solution.py:163
  86.4 19.6 %shard_map.141 = (bf16[1024,768]{1,0:T(8,128)(2,1)S(1)}, bf16[48,128,128]{2,1,0:T(8,128)(2,1)S(1)}, bf16[48,128,128]{2,1,0:T(8,128)(2,1)S(1)}) custom-call(s32[48]{0:T(128)S(1)} %convert_element_type.42.used_ref, s32[48]{0:T(128)S(1)} %get-tuple-element.22.owner_ref, s32[48]{0:T(128)S(1)} %get-tuple-element.21.column_ref, s32[4]{0:T(128)S(1)} %copy-done.9, ...), custom_call_target="tpu_custom_call" | custom-call | flops 4026531840 | bytes 6029312 | tf_op jit(solution)/shard_map/pallas_call | solution.py:193
  106.0 1.1 copy-done.6
  107.2 1.2 copy-done.7
  108.3 1.2 copy-done.8
  109.5 54.6 %shard_map.142 = (bf16[8,128,768]{2,1,0:T(8,128)(2,1)}, bf16[4,12,128,128]{3,2,1,0:T(8,128)(2,1)}, bf16[4,12,128,128]{3,2,1,0:T(8,128)(2,1)}) custom-call(bf16[1024,768]{1,0:T(8,128)(2,1)} %copy-done.6, bf16[48,128,128]{2,1,0:T(8,128)(2,1)} %copy-done.7, bf16[48,128,128]{2,1,0:T(8,128)(2,1)} %copy-done.8), custom_call_target="tpu_custom_call" | custom-call | tf_op jit(solution)/shard_map/pallas_call | solution.py:366
  164.3 1.4 copy-done.3
  165.7 1.4 copy-done.4
  167.1 1.4 copy-done.5
  168.5 4.2 %shard_map.143 = (bf16[128,640]{1,0:T(8,128)(2,1)}, bf16[12,128,128]{2,1,0:T(8,128)(2,1)}, bf16[12,128,128]{2,1,0:T(8,128)(2,1)}) custom-call(s32[12]{0:T(128)S(1)} %dynamic_slice.6.used_ref, s32[12]{0:T(128)S(1)} %dynamic_slice.7.owner_ref, bf16[8,128,768]{2,1,0:T(8,128)(2,1)S(1)} %copy-done.3, bf16[4,12,128,128]{3,2,1,0:T(8,128)(2,1)S(1)} %copy-done.4, ...), custom_call_target="tpu_custom_call" | custom-call | tf_op jit(solution)/shard_map/pallas_call | solution.py:271
  (47 shorter events, 1.5 us)
Async XLA Ops:
  0.6 29.8 %copy-start = (bf16[5120,128]{1,0:T(8,128)(2,1)S(1)}, bf16[5120,128]{1,0:T(8,128)(2,1)}, u32[]{:S(2)}) copy-start(bf16[5120,128]{1,0:T(8,128)(2,1)} %param.15) | copy-start | bytes 3932164
  0.6 24.6 %copy-start.11 = (bf16[5120]{0:T(1024)(128)(2,1)S(1)}, bf16[5120]{0:T(1024)(128)(2,1)}, u32[]{:S(2)}) copy-start(bf16[5120]{0:T(1024)(128)(2,1)} %param.13) | copy-start | bytes 30724
  0.7 24.6 %copy-start.13 = (bf16[640]{0:T(1024)(128)(2,1)S(1)}, bf16[640]{0:T(1024)(128)(2,1)}, u32[]{:S(2)}) copy-start(bf16[640]{0:T(1024)(128)(2,1)} %param.17) | copy-start | bytes 3844
  29.8 0.7 copy-start.15
  29.8 1.3 copy-start.10
  31.1 1.0 copy-start.16
  31.1 1.3 copy-start.14
  81.4 1.4 copy-start.12
  81.4 1.6 copy-start.9
  106.0 1.2 copy-start.6
  107.2 1.2 copy-start.7
  108.3 1.2 copy-start.8
  109.5 54.8 %copy-start.1 = (bf16[12,128,128]{2,1,0:T(8,128)(2,1)S(1)}, bf16[12,128,128]{2,1,0:T(8,128)(2,1)}, u32[]{:S(2)}) copy-start(bf16[12,128,128]{2,1,0:T(8,128)(2,1)} %kc_ref.1) | copy-start | bytes 1179652
  109.5 54.8 %copy-start.2 = (bf16[12,128,128]{2,1,0:T(8,128)(2,1)S(1)}, bf16[12,128,128]{2,1,0:T(8,128)(2,1)}, u32[]{:S(2)}) copy-start(bf16[12,128,128]{2,1,0:T(8,128)(2,1)} %vc_ref.1) | copy-start | bytes 1179652
  164.3 1.4 copy-start.3
  165.7 1.4 copy-start.4
  167.1 1.4 copy-start.5

commit v14 on v13

--- a/solution.py
+++ b/solution.py
@@ -441,8 +441,8 @@
     fresh_values = (value_linear + value_bias.astype(jnp.float32)[None, :]).astype(jnp.bfloat16)
     q_width = q_heads * head_dim
     packed = jnp.concatenate([fresh_queries, fresh_keys, fresh_values], axis=1)
-    ring_packed, col_keys, col_values = multi_exchange(
-        [("blk", ring, 1, True, [packed]), ("blk", cols, ring, True, [key_cache, value_cache])], 1
+    col_keys, col_values, ring_packed = multi_exchange(
+        [("blk", cols, ring, True, [key_cache, value_cache]), ("blk", ring, 1, True, [packed])], 1
     )
     ring_packed = ring_packed.reshape(span, packed.shape[1])
     fresh_rows = jnp.pad(
@@ -463,8 +463,8 @@
         q_heads,
         head_dim,
     )
-    got, back_k, back_v = multi_exchange(
-        [("blk", ring, 1, False, [parts]), ("blk", cols, ring, False, [merged_k, merged_v])], 2
+    back_k, back_v, got = multi_exchange(
+        [("blk", cols, ring, False, [merged_k, merged_v]), ("blk", ring, 1, False, [parts])], 2
     )
     mine = (device // ring) * nb_dev
     used = lax.dynamic_slice_in_dim(meta[0], mine, nb_dev)

time: 170 us -> 168 us (0.988); the launches traced: 173 us -> 167 us
  Pallas kernels: 148 us -> 142 us
    pallas_call x1, Pallas kernels: 19.6 us -> 11.8 us  [attend(): pl.pallas_call(functools.partial(attention_kernel, q_heads=q_heads, head_...]
    pallas_call x3, Pallas kernels: 124 us -> 126 us  [multi_exchange(): pl.pallas_call(functools.partial(multi_exchange_kernel, specs=tuple(specs...]
where the time goes in v14:
time: 168 us; the launch traced here: 167 us
  Pallas kernels  142 us (85%)
  local copies, waits for them, and re-layouts  11.3 us (7%)
  other arithmetic  7.01 us (4%)
  matrix products  5.77 us (3%)
    pallas_call x3, Pallas kernels, multi_exchange(): pl.pallas_call(functools.partial(multi_exchange_kernel, specs=tuple(specs...  126 us
    pallas_call x1, Pallas kernels, attend(): pl.pallas_call(functools.partial(attention_kernel, q_heads=q_heads, head_...  11.8 us
    unnamed x34, local copies, waits for them, and re-layouts  8.98 us
    dot_general x3, matrix products, project(): lax.dot_general(normed, weight.reshape(kv_n, feat, weight.shape[1]), (((0...  5.77 us
    pallas_call x1, Pallas kernels, combine(): pl.pallas_call(functools.partial(combine_kernel, q_heads=q_heads, head_di...  4.18 us

profile of v14, /device:TPU:1, one launch (start us, length us, event | category | flops | bytes accessed | tf_op | source)
XLA Modules:
  0.0 167.4 jit_solution(18200207361987408336)
XLA Ops:
  0.7 0.8 select_reduce_fusion
  1.8 21.8 %shard_map.139 = bf16[8,128,640]{2,1,0:T(8,128)(2,1)} custom-call(bf16[128,640]{1,0:T(8,128)(2,1)} %refs_0_.2), custom_call_target="tpu_custom_call" | custom-call | tf_op jit(solution)/shard_map/pallas_call | solution.py:366
  23.5 1.7 fusion
  25.3 4.5 %fusion.3 = f32[128,640]{1,0:T(8,128)S(1)} fusion(bf16[8,640,640]{2,1,0:T(8,128)(2,1)} %bitcast.53, f32[640]{0:T(1024)S(1)} %convert_element_type.45, bf16[8,128,640]{2,1,0:T(8,128)(2,1)} %shard_map.139, f32[8,640]{1,0:T(8,128)S(1)} %reshape.244, f32[128]{0:T(128)S(1)} %add_rsqrt_fusion), kind=kOutput, calls=%fused_computation.6 | convolution fusion | flops 841564160 | bytes 8215552 | tf_op jit(solution)/shard_map/dot_general | solution.py:417
  30.2 0.2 copy-done.15
  30.5 0.7 copy-done.10
  31.1 0.6 fusion.5
  31.8 0.3 fusion.19
  32.1 0.4 copy-done.14
  32.5 0.6 fusion.7
  33.1 0.8 pad_maximum_fusion.refs_2_
  33.9 47.5 %shard_map.140 = (bf16[4,12,128,128]{3,2,1,0:T(8,128)(2,1)}, bf16[4,12,128,128]{3,2,1,0:T(8,128)(2,1)}, bf16[8,128,896]{2,1,0:T(8,128)(2,1)}) custom-call(bf16[12,128,128]{2,1,0:T(8,128)(2,1)} %kc_ref.1, bf16[12,128,128]{2,1,0:T(8,128)(2,1)} %vc_ref.1, bf16[128,896]{1,0:T(8,128)(2,1)} %pad_maximum_fusion.refs_2_), custom_call_target="tpu_custom_call" | custom-call | tf_op jit(solution)/shard_map/pallas_call | solution.py:366
  81.4 1.1 slice.29
  82.9 0.6 fusion.28
  83.6 2.6 %fusion.23.start_ref = s32[48]{0:T(128)S(1)} fusion(s32[48]{0:T(128)S(1)} %get-tuple-element.22.owner_ref, s32[48]{0:T(128)S(1)} %get-tuple-element.21.column_ref, s32[]{:T(128)} %bitcast.1, s32[]{:T(128)} %bitcast.2, s32[]{:T(128)} %bitcast.4, s32[]{:T(128)} %bitcast.3), kind=kLoop, calls=%fused_computation.56 | loop fusion | flops 624 | bytes 592 | tf_op jit(solution)/shard_map/jit(clip)/min | solution.py:163
  86.3 11.8 %shard_map.141 = (bf16[1024,768]{1,0:T(8,128)(2,1)S(1)}, bf16[48,128,128]{2,1,0:T(8,128)(2,1)S(1)}, bf16[48,128,128]{2,1,0:T(8,128)(2,1)S(1)}) custom-call(s32[48]{0:T(128)S(1)} %convert_element_type.42.used_ref, s32[48]{0:T(128)S(1)} %get-tuple-element.22.owner_ref, s32[48]{0:T(128)S(1)} %get-tuple-element.21.column_ref, s32[4]{0:T(128)S(1)} %copy-done.9, ...), custom_call_target="tpu_custom_call" | custom-call | flops 4026531840 | bytes 6029312 | tf_op jit(solution)/shard_map/pallas_call | solution.py:193
  98.1 1.1 copy-done.6
  99.3 1.1 copy-done.7
  100.4 1.2 copy-done.8
  101.6 57.0 %shard_map.142 = (bf16[4,12,128,128]{3,2,1,0:T(8,128)(2,1)}, bf16[4,12,128,128]{3,2,1,0:T(8,128)(2,1)}, bf16[8,128,768]{2,1,0:T(8,128)(2,1)}) custom-call(bf16[48,128,128]{2,1,0:T(8,128)(2,1)} %copy-done.7, bf16[48,128,128]{2,1,0:T(8,128)(2,1)} %copy-done.8, bf16[1024,768]{1,0:T(8,128)(2,1)} %copy-done.6), custom_call_target="tpu_custom_call" | custom-call | tf_op jit(solution)/shard_map/pallas_call | solution.py:366
  158.8 1.4 copy-done.3
  160.2 1.4 copy-done.4
  161.6 1.4 copy-done.5
  163.0 4.2 %shard_map.143 = (bf16[128,640]{1,0:T(8,128)(2,1)}, bf16[12,128,128]{2,1,0:T(8,128)(2,1)}, bf16[12,128,128]{2,1,0:T(8,128)(2,1)}) custom-call(s32[12]{0:T(128)S(1)} %dynamic_slice.6.used_ref, s32[12]{0:T(128)S(1)} %dynamic_slice.7.owner_ref, bf16[8,128,768]{2,1,0:T(8,128)(2,1)S(1)} %copy-done.5, bf16[4,12,128,128]{3,2,1,0:T(8,128)(2,1)S(1)} %copy-done.3, ...), custom_call_target="tpu_custom_call" | custom-call | tf_op jit(solution)/shard_map/pallas_call | solution.py:271
  (47 shorter events, 1.5 us)
Async XLA Ops:
  0.6 29.8 %copy-start = (bf16[5120,128]{1,0:T(8,128)(2,1)S(1)}, bf16[5120,128]{1,0:T(8,128)(2,1)}, u32[]{:S(2)}) copy-start(bf16[5120,128]{1,0:T(8,128)(2,1)} %param.15) | copy-start | bytes 3932164
  0.6 24.6 %copy-start.11 = (bf16[5120]{0:T(1024)(128)(2,1)S(1)}, bf16[5120]{0:T(1024)(128)(2,1)}, u32[]{:S(2)}) copy-start(bf16[5120]{0:T(1024)(128)(2,1)} %param.13) | copy-start | bytes 30724
  0.7 24.6 %copy-start.13 = (bf16[640]{0:T(1024)(128)(2,1)S(1)}, bf16[640]{0:T(1024)(128)(2,1)}, u32[]{:S(2)}) copy-start(bf16[640]{0:T(1024)(128)(2,1)} %param.17) | copy-start | bytes 3844
  29.8 0.7 copy-start.15
  29.8 1.3 copy-start.10
  31.1 1.0 copy-start.16
  31.1 1.3 copy-start.14
  81.4 1.4 copy-start.12
  81.4 1.6 copy-start.9
  98.1 1.2 copy-start.6
  99.3 1.2 copy-start.7
  100.4 1.2 copy-start.8
  101.6 57.2 %copy-start.1 = (bf16[12,128,128]{2,1,0:T(8,128)(2,1)S(1)}, bf16[12,128,128]{2,1,0:T(8,128)(2,1)}, u32[]{:S(2)}) copy-start(bf16[12,128,128]{2,1,0:T(8,128)(2,1)} %kc_ref.1) | copy-start | bytes 1179652
  101.6 57.2 %copy-start.2 = (bf16[12,128,128]{2,1,0:T(8,128)(2,1)S(1)}, bf16[12,128,128]{2,1,0:T(8,128)(2,1)}, u32[]{:S(2)}) copy-start(bf16[12,128,128]{2,1,0:T(8,128)(2,1)} %vc_ref.1) | copy-start | bytes 1179652
  158.8 1.4 copy-start.3
  160.2 1.4 copy-start.4
  161.6 1.4 copy-start.5

commit v15 on v13

--- a/solution.py
+++ b/solution.py
@@ -320,8 +320,11 @@
             own = pltpu.make_async_copy(chunk(srcs[a], pos, m, gather), dsts[a].at[pos], own_sem.at[a])
             own.start()
             owns.append(own)
-    for axis, m, stride, gather, n_arr, pos, base, a0, s0 in groups:
-        for k in range(1, m):
+    started = {}
+    for k in range(1, max(g[1] for g in groups)):
+        for gi, (axis, m, stride, gather, n_arr, pos, base, a0, s0) in enumerate(groups):
+            if k >= m:
+                continue
             peer_pos = lax.rem(pos + k, m)
             for a in range(n_arr):
                 copy = pltpu.make_async_remote_copy(
@@ -333,7 +336,11 @@
                     device_id_type=MESH,
                 )
                 copy.start()
-                copies.append(copy)
+                started[(gi, k, a)] = copy
+    for gi, (axis, m, stride, gather, n_arr, pos, base, a0, s0) in enumerate(groups):
+        for k in range(1, m):
+            for a in range(n_arr):
+                copies.append(started[(gi, k, a)])
     for own in owns:
         own.wait()
     c = 0

time: 170 us -> 169 us (level)
  Pallas kernels: 148 us -> 146 us
    pallas_call x3, Pallas kernels: 124 us -> 115 us  [multi_exchange(): pl.pallas_call(functools.partial(multi_exchange_kernel, specs=tuple(specs...]
    pallas_call x1, Pallas kernels: 19.6 us -> 27.2 us  [attend(): pl.pallas_call(functools.partial(attention_kernel, q_heads=q_heads, head_...]
where the time goes in v15:
time: 169 us; the launch traced here: 171 us
  Pallas kernels  146 us (86%)
  local copies, waits for them, and re-layouts  11.3 us (7%)
  other arithmetic  7.01 us (4%)
  matrix products  5.77 us (3%)
    pallas_call x3, Pallas kernels, multi_exchange(): pl.pallas_call(functools.partial(multi_exchange_kernel, specs=tuple(specs...  115 us
    pallas_call x1, Pallas kernels, attend(): pl.pallas_call(functools.partial(attention_kernel, q_heads=q_heads, head_...  27.2 us
    unnamed x34, local copies, waits for them, and re-layouts  8.98 us
    dot_general x3, matrix products, project(): lax.dot_general(normed, weight.reshape(kv_n, feat, weight.shape[1]), (((0...  5.77 us
    pallas_call x1, Pallas kernels, combine(): pl.pallas_call(functools.partial(combine_kernel, q_heads=q_heads, head_di...  4.18 us

profile of v15, /device:TPU:1, one launch (start us, length us, event | category | flops | bytes accessed | tf_op | source)
XLA Modules:
  0.0 171.4 jit_solution(9338242624019659655)
XLA Ops:
  0.7 0.8 select_reduce_fusion
  1.8 21.8 %shard_map.139 = bf16[8,128,640]{2,1,0:T(8,128)(2,1)} custom-call(bf16[128,640]{1,0:T(8,128)(2,1)} %refs_0_.1), custom_call_target="tpu_custom_call" | custom-call | tf_op jit(solution)/shard_map/pallas_call | solution.py:373
  23.5 1.7 fusion
  25.3 4.5 %fusion.3 = f32[128,640]{1,0:T(8,128)S(1)} fusion(bf16[8,640,640]{2,1,0:T(8,128)(2,1)} %bitcast.53, f32[640]{0:T(1024)S(1)} %convert_element_type.45, bf16[8,128,640]{2,1,0:T(8,128)(2,1)} %shard_map.139, f32[8,640]{1,0:T(8,128)S(1)} %reshape.244, f32[128]{0:T(128)S(1)} %add_rsqrt_fusion), kind=kOutput, calls=%fused_computation.6 | convolution fusion | flops 841564160 | bytes 8215552 | tf_op jit(solution)/shard_map/dot_general | solution.py:424
  30.2 0.2 copy-done.15
  30.5 0.7 copy-done.10
  31.1 0.6 fusion.5
  31.8 0.3 fusion.19
  32.1 0.4 copy-done.14
  32.5 0.6 fusion.7
  33.1 0.8 pad_maximum_fusion.refs_0_
  33.9 47.5 %shard_map.140 = (bf16[8,128,896]{2,1,0:T(8,128)(2,1)}, bf16[4,12,128,128]{3,2,1,0:T(8,128)(2,1)}, bf16[4,12,128,128]{3,2,1,0:T(8,128)(2,1)}) custom-call(bf16[128,896]{1,0:T(8,128)(2,1)} %pad_maximum_fusion.refs_0_, bf16[12,128,128]{2,1,0:T(8,128)(2,1)} %kc_ref.1, bf16[12,128,128]{2,1,0:T(8,128)(2,1)} %vc_ref.1), custom_call_target="tpu_custom_call" | custom-call | tf_op jit(solution)/shard_map/pallas_call | solution.py:373
  81.4 1.1 slice.29
  83.0 0.6 fusion.28
  83.6 2.6 %fusion.23.start_ref = s32[48]{0:T(128)S(1)} fusion(s32[48]{0:T(128)S(1)} %get-tuple-element.22.owner_ref, s32[48]{0:T(128)S(1)} %get-tuple-element.21.column_ref, s32[]{:T(128)} %bitcast.1, s32[]{:T(128)} %bitcast.2, s32[]{:T(128)} %bitcast.4, s32[]{:T(128)} %bitcast.3), kind=kLoop, calls=%fused_computation.56 | loop fusion | flops 624 | bytes 592 | tf_op jit(solution)/shard_map/jit(clip)/min | solution.py:163
  86.4 27.2 %shard_map.141 = (bf16[1024,768]{1,0:T(8,128)(2,1)S(1)}, bf16[48,128,128]{2,1,0:T(8,128)(2,1)S(1)}, bf16[48,128,128]{2,1,0:T(8,128)(2,1)S(1)}) custom-call(s32[48]{0:T(128)S(1)} %convert_element_type.42.used_ref, s32[48]{0:T(128)S(1)} %get-tuple-element.22.owner_ref, s32[48]{0:T(128)S(1)} %get-tuple-element.21.column_ref, s32[4]{0:T(128)S(1)} %copy-done.9, ...), custom_call_target="tpu_custom_call" | custom-call | flops 4026531840 | bytes 6029312 | tf_op jit(solution)/shard_map/pallas_call | solution.py:193
  113.5 1.1 copy-done.6
  114.7 1.2 copy-done.7
  115.8 1.2 copy-done.8
  117.0 45.6 %shard_map.142 = (bf16[8,128,768]{2,1,0:T(8,128)(2,1)}, bf16[4,12,128,128]{3,2,1,0:T(8,128)(2,1)}, bf16[4,12,128,128]{3,2,1,0:T(8,128)(2,1)}) custom-call(bf16[1024,768]{1,0:T(8,128)(2,1)} %copy-done.6, bf16[48,128,128]{2,1,0:T(8,128)(2,1)} %copy-done.7, bf16[48,128,128]{2,1,0:T(8,128)(2,1)} %copy-done.8), custom_call_target="tpu_custom_call" | custom-call | tf_op jit(solution)/shard_map/pallas_call | solution.py:373
  162.8 1.4 copy-done.3
  164.2 1.4 copy-done.4
  165.6 1.4 copy-done.5
  167.0 4.2 %shard_map.143 = (bf16[128,640]{1,0:T(8,128)(2,1)}, bf16[12,128,128]{2,1,0:T(8,128)(2,1)}, bf16[12,128,128]{2,1,0:T(8,128)(2,1)}) custom-call(s32[12]{0:T(128)S(1)} %dynamic_slice.6.used_ref, s32[12]{0:T(128)S(1)} %dynamic_slice.7.owner_ref, bf16[8,128,768]{2,1,0:T(8,128)(2,1)S(1)} %copy-done.3, bf16[4,12,128,128]{3,2,1,0:T(8,128)(2,1)S(1)} %copy-done.4, ...), custom_call_target="tpu_custom_call" | custom-call | tf_op jit(solution)/shard_map/pallas_call | solution.py:271
  (47 shorter events, 1.5 us)
Async XLA Ops:
  0.6 29.8 %copy-start = (bf16[5120,128]{1,0:T(8,128)(2,1)S(1)}, bf16[5120,128]{1,0:T(8,128)(2,1)}, u32[]{:S(2)}) copy-start(bf16[5120,128]{1,0:T(8,128)(2,1)} %param.15) | copy-start | bytes 3932164
  0.6 24.6 %copy-start.11 = (bf16[5120]{0:T(1024)(128)(2,1)S(1)}, bf16[5120]{0:T(1024)(128)(2,1)}, u32[]{:S(2)}) copy-start(bf16[5120]{0:T(1024)(128)(2,1)} %param.13) | copy-start | bytes 30724
  0.7 24.6 %copy-start.13 = (bf16[640]{0:T(1024)(128)(2,1)S(1)}, bf16[640]{0:T(1024)(128)(2,1)}, u32[]{:S(2)}) copy-start(bf16[640]{0:T(1024)(128)(2,1)} %param.17) | copy-start | bytes 3844
  29.8 0.7 copy-start.15
  29.8 1.3 copy-start.10
  31.1 1.0 copy-start.16
  31.1 1.3 copy-start.14
  81.4 1.4 copy-start.12
  81.4 1.6 copy-start.9
  113.5 1.2 copy-start.6
  114.7 1.2 copy-start.7
  115.8 1.2 copy-start.8
  117.0 45.8 %copy-start.1 = (bf16[12,128,128]{2,1,0:T(8,128)(2,1)S(1)}, bf16[12,128,128]{2,1,0:T(8,128)(2,1)}, u32[]{:S(2)}) copy-start(bf16[12,128,128]{2,1,0:T(8,128)(2,1)} %kc_ref.1) | copy-start | bytes 1179652
  117.0 45.8 %copy-start.2 = (bf16[12,128,128]{2,1,0:T(8,128)(2,1)S(1)}, bf16[12,128,128]{2,1,0:T(8,128)(2,1)}, u32[]{:S(2)}) copy-start(bf16[12,128,128]{2,1,0:T(8,128)(2,1)} %vc_ref.1) | copy-start | bytes 1179652
  162.8 1.4 copy-start.3
  164.2 1.4 copy-start.4
  165.6 1.4 copy-start.5
